TPU v7x, 512 devices: a whole 4x4x16 slice. The times are simulated.
512 devices in a mesh: seq: 128 (over x_hi, y, z), dp: 4 (over x_lo, core).
Axes of the slice: x: 4 (x_hi: 2, x_lo: 2; x = x_hi * 2 + x_lo), y: 4, z: 16, core: 2. Of those that a mesh axis runs over, the one named last changes fastest.
Arguments:
- asking_vectors: bfloat16 [4, 16384, 2048], P('dp', 'seq'), may hold values from -100 to 100
- lookup_vectors: bfloat16 [4, 16384, 2048], P('dp', 'seq'), may hold values from -13 to 13
- payload_vectors: bfloat16 [4, 16384, 2048], P('dp', 'seq'), may hold values from -6 to 6
- incoming_sensitivity: bfloat16 [4, 16384, 2048], P('dp', 'seq'), may hold values from -6 to 6
- learned_sharpness: float32 [16], replicated, may hold values from 0.5 to 2
- reply_list_sizes: int32 [4, 8], P('dp'), may hold values from 1 to 8192, 16384 in all within a row
Outputs:
- attention_result: bfloat16 [4, 16384, 2048], P('dp', 'seq')
- query_gradient: bfloat16 [4, 16384, 2048], P('dp', 'seq')
- key_gradient: bfloat16 [4, 16384, 2048], P('dp', 'seq')
- value_gradient: bfloat16 [4, 16384, 2048], P('dp', 'seq')
- scale_gradient: float32 [16], replicated
All inputs are finite; a program needn't handle non-finite values.
Results may differ from a plain program's by a relative error of at most 0.02.
The roundings to bfloat16 on the way count: a program that leaves them out, or rounds other values in their place, can miss the bound.
Values may be sent and summed in bfloat16 or wider, within the bound.
No kernel may reach another device: no remote copies, remote signals or barrier semaphores. Data moves between devices by JAX's collectives and lax.ppermute only.
A program may use at most 64 MiB of HBM per device.

v0:
```python
import math

import jax
import jax.numpy as jnp
from jax import lax
from jax.sharding import PartitionSpec as P

MIXER_CHANNELS = 16


def partner(array, axis, apart):
    return lax.ppermute(array, axis, [(i, i ^ 1 << apart) for i in range(lax.axis_size(axis))])


def level_plan(level_idx, head_idx, seq_devices):
    group_span = min(2**level_idx, seq_devices)
    dilation = max(1, group_span // 4)
    offset = (5 + head_idx * (dilation // 2)) % dilation
    return (group_span, dilation, offset)


def body(
    asking_vectors,
    lookup_vectors,
    payload_vectors,
    incoming_sensitivity,
    learned_sharpness,
    reply_list_sizes,
):
    seq_devices = lax.axis_size("seq")
    device_idx = lax.axis_index("seq")
    tokens = asking_vectors.shape[1]
    channel_extent = asking_vectors.shape[2] // MIXER_CHANNELS
    level_count = MIXER_CHANNELS // 2
    queries = asking_vectors[0]
    keyed = lookup_vectors[0]
    valued = payload_vectors[0]
    upstream = incoming_sensitivity[0]
    doc_ends = jnp.cumsum(reply_list_sizes[0])[:-1]

    def doc_of(positions):
        return jnp.sum((positions[..., None] >= doc_ends).astype(jnp.int32), axis=-1)

    def select_rows(source, channel_count, dilation, offset):
        column = channel_count * channel_extent
        column_block = source[:, column : column + channel_extent]
        return column_block.reshape(tokens // dilation, dilation, channel_extent)[:, offset]

    def spread_rows(values_sel, dilation, offset):
        per_dev = tokens // dilation
        holder = jnp.zeros((per_dev, dilation, channel_extent), values_sel.dtype)
        return holder.at[:, offset].set(values_sel).reshape(tokens, channel_extent)

    top_span = min(2 ** (level_count - 1), seq_devices)
    bit_order = list(range(top_span.bit_length() - 1))
    gathered, level_bits, level_masks = ([], [], [])
    for level_idx in range(level_count):
        group_span, dilation, offset_zero = level_plan(level_idx, 0, seq_devices)
        nbits = group_span.bit_length() - 1
        own_bits = [bit_num for bit_num in bit_order if bit_num < nbits]
        masks_now = [0]
        for bit_num in own_bits:
            masks_now = masks_now + [entry ^ 1 << bit_num for entry in masks_now]
        level_bits.append(own_bits)
        level_masks.append(masks_now)
        key_heads, val_heads = ([], [])
        for head_idx in range(2):
            offset = level_plan(level_idx, head_idx, seq_devices)[2]
            key_heads.append(select_rows(keyed, 2 * level_idx + head_idx, dilation, offset))
            val_heads.append(select_rows(valued, 2 * level_idx + head_idx, dilation, offset))
        gathered.append(
            jnp.concatenate([jnp.concatenate(key_heads, 1), jnp.concatenate(val_heads, 1)], 0)
        )
    for level_id in range(level_count):
        for bit_num in level_bits[level_id]:
            current = gathered[level_id]
            gathered[level_id] = jnp.concatenate([current, partner(current, "seq", bit_num)], 0)
    out_cols, dq_cols, scale_terms, level_grads = ([], [], [], [])
    for level_id in range(level_count):
        group_span, dilation, offset_zero = level_plan(level_id, 0, seq_devices)
        per_dev = tokens // dilation
        arranged = gathered[level_id].reshape(group_span, 2, per_dev, 2 * channel_extent)
        all_keys = arranged[:, 0].reshape(group_span * per_dev, 2 * channel_extent)
        all_vals = arranged[:, 1].reshape(group_span * per_dev, 2 * channel_extent)
        sources = jnp.bitwise_xor(device_idx, jnp.array(level_masks[level_id], jnp.int32))
        key_grad_heads, val_grad_heads = ([], [])
        for head_idx in range(2):
            offset = level_plan(level_id, head_idx, seq_devices)[2]
            channel_count = 2 * level_id + head_idx
            local_idx = jnp.arange(per_dev, dtype=jnp.int32) * dilation + offset
            query_docs = doc_of(device_idx * tokens + local_idx)
            key_docs = doc_of((sources[:, None] * tokens + local_idx[None, :]).reshape(-1))
            allowed = query_docs[:, None] == key_docs[None, :]
            query_sel = select_rows(queries, channel_count, dilation, offset)
            up_sel = select_rows(upstream, channel_count, dilation, offset)
            key_sel = all_keys[:, head_idx * channel_extent : (head_idx + 1) * channel_extent]
            val_sel = all_vals[:, head_idx * channel_extent : (head_idx + 1) * channel_extent]
            raw = lax.dot_general(
                query_sel, key_sel, (((1,), (1,)), ((), ())), preferred_element_type=jnp.float32
            )
            logit_multiplier = learned_sharpness[channel_count] / math.sqrt(channel_extent)
            scores = jnp.where(allowed, raw * logit_multiplier, -jnp.inf)
            highest = jnp.max(scores, axis=1, keepdims=True)
            expo = jnp.where(allowed, jnp.exp(scores - highest), 0.0)
            probs = expo / jnp.sum(expo, axis=1, keepdims=True)
            probs_narrow = probs.astype(jnp.bfloat16)
            attended_output = jnp.dot(probs_narrow, val_sel, preferred_element_type=jnp.float32)
            delta = jnp.sum(up_sel.astype(jnp.float32) * attended_output, axis=1, keepdims=True)
            gradient_probs = lax.dot_general(
                up_sel, val_sel, (((1,), (1,)), ((), ())), preferred_element_type=jnp.float32
            )
            dscores = probs * (gradient_probs - delta)
            scale_terms.append(jnp.sum(dscores * raw) / math.sqrt(channel_extent))
            dscore_low = dscores.astype(jnp.bfloat16)
            grad_q = (
                jnp.dot(dscore_low, key_sel, preferred_element_type=jnp.float32) * logit_multiplier
            )
            grad_k = (
                lax.dot_general(
                    dscore_low,
                    query_sel,
                    (((0,), (0,)), ((), ())),
                    preferred_element_type=jnp.float32,
                )
                * logit_multiplier
            )
            grad_v = lax.dot_general(
                probs_narrow, up_sel, (((0,), (0,)), ((), ())), preferred_element_type=jnp.float32
            )
            out_cols.append(spread_rows(attended_output.astype(jnp.bfloat16), dilation, offset))
            dq_cols.append(spread_rows(grad_q.astype(jnp.bfloat16), dilation, offset))
            key_grad_heads.append(grad_k)
            val_grad_heads.append(grad_v)
        key_pack = jnp.concatenate(key_grad_heads, 1).reshape(
            group_span, per_dev, 2 * channel_extent
        )
        val_pack = jnp.concatenate(val_grad_heads, 1).reshape(
            group_span, per_dev, 2 * channel_extent
        )
        level_grads.append(
            jnp.stack([key_pack, val_pack], 1).reshape(group_span * 2 * per_dev, 2 * channel_extent)
        )
    for level_id in range(level_count):
        for bit_num in level_bits[level_id][::-1]:
            current = level_grads[level_id]
            half_rows = current.shape[0] // 2
            level_grads[level_id] = current[:half_rows] + partner(
                current[half_rows:], "seq", bit_num
            )
    dk_cols, dv_cols = ([], [])
    for level_id in range(level_count):
        group_span, dilation, offset_zero = level_plan(level_id, 0, seq_devices)
        per_dev = tokens // dilation
        own_grad = level_grads[level_id]
        for head_idx in range(2):
            offset = level_plan(level_id, head_idx, seq_devices)[2]
            cols_lo = head_idx * channel_extent
            key_part = own_grad[:per_dev, cols_lo : cols_lo + channel_extent]
            val_part = own_grad[per_dev:, cols_lo : cols_lo + channel_extent]
            dk_cols.append(spread_rows(key_part.astype(jnp.bfloat16), dilation, offset))
            dv_cols.append(spread_rows(val_part.astype(jnp.bfloat16), dilation, offset))
    scale_gradient = lax.psum(jnp.stack(scale_terms), ("seq", "dp"))
    attention_result = jnp.concatenate(out_cols, 1)[None]
    query_gradient = jnp.concatenate(dq_cols, 1)[None]
    key_gradient = jnp.concatenate(dk_cols, 1)[None]
    value_gradient = jnp.concatenate(dv_cols, 1)[None]
    return (attention_result, query_gradient, key_gradient, value_gradient, scale_gradient)


def solution(mesh):
    in_specs = (
        P("dp", "seq", None),
        P("dp", "seq", None),
        P("dp", "seq", None),
        P("dp", "seq", None),
        P(),
        P("dp", None),
    )
    out_specs = (
        P("dp", "seq", None),
        P("dp", "seq", None),
        P("dp", "seq", None),
        P("dp", "seq", None),
        P(),
    )
    return jax.shard_map(body, mesh=mesh, in_specs=in_specs, out_specs=out_specs, check_vma=False)
```

profile of v0, /device:TPU:1, one launch (start us, length us, event | category | flops | bytes accessed | tf_op | source)
XLA Modules:
  0.0 626.4 jit_solution(6130555929108911474)
XLA Ops:
  2.0 4.4 collective-permute-start.21
  6.5 1.9 collective-permute-start.15
  8.5 3.4 collective-permute-start.10
  14.1 3.4 collective-permute-start.3
  60.9 4.9 collective-permute-start.22
  66.8 3.4 collective-permute-start
  70.2 4.3 collective-permute-start.16
  75.6 8.9 %collective-permute-start.23 = (bf16[32,256]{1,0:T(8,128)(2,1)S(1)}, bf16[32,256]{1,0:T(8,128)(2,1)S(1)}, u32[]{:S(2)}, u32[]{:S(2)}) collective-permute-start(bf16[32,256]{1,0:T(8,128)(2,1)S(1)} %pad_maximum_fusion.36), channel_id=1, source_target_pairs={{0,16},{4,20},{8,24},{12,28},{16,0},{20,4},{24,8},{28,12},{32,48},... | collective-permute-start | bytes 49160 | tf_op jit(solution)/shard_map/ppermute | solution.py:12
  85.6 4.3 collective-permute-start.11
  90.0 7.3 %collective-permute-start.17 = (bf16[64,256]{1,0:T(8,128)(2,1)S(1)}, bf16[64,256]{1,0:T(8,128)(2,1)S(1)}, u32[]{:S(2)}, u32[]{:S(2)}) collective-permute-start(bf16[64,256]{1,0:T(8,128)(2,1)S(1)} %pad_maximum_fusion.32), channel_id=1, source_target_pairs={{0,16},{4,20},{8,24},{12,28},{16,0},{20,4},{24,8},{28,12},{32,48},... | collective-permute-start | bytes 98312 | tf_op jit(solution)/shard_map/ppermute | solution.py:12
  97.9 7.9 %collective-permute-start.24 = (bf16[64,256]{1,0:T(8,128)(2,1)S(1)}, bf16[64,256]{1,0:T(8,128)(2,1)S(1)}, u32[]{:S(2)}, u32[]{:S(2)}) collective-permute-start(bf16[64,256]{1,0:T(8,128)(2,1)S(1)} %concatenate.419), channel_id=1, source_target_pairs={{0,32},{4,36},{8,40},{12,44},{16,48},{20,52},{24,56},{28,60},{32,0... | collective-permute-start | bytes 98312 | tf_op jit(solution)/shard_map/ppermute | solution.py:12
  106.4 3.1 collective-permute-start.7
  111.6 3.7 collective-permute-start.12
  115.3 9.0 %collective-permute-start.18 = (bf16[128,256]{1,0:T(8,128)(2,1)}, bf16[128,256]{1,0:T(8,128)(2,1)S(1)}, u32[]{:S(2)}, u32[]{:S(2)}) collective-permute-start(bf16[128,256]{1,0:T(8,128)(2,1)} %get-tuple-element.952), channel_id=1, source_target_pairs={{0,32},{4,36},{8,40},{12,44},{16,48},{20,52},{24,56},{28,60},{32,0... | collective-permute-start | bytes 196616 | tf_op jit(solution)/shard_map/ppermute | solution.py:12
  125.0 3.2 collective-permute-start.25
  129.5 3.2 collective-permute-start.4
  133.4 4.0 collective-permute-start.8
  138.1 6.5 %collective-permute-start.13 = (bf16[256,256]{1,0:T(8,128)(2,1)}, bf16[256,256]{1,0:T(8,128)(2,1)}, u32[]{:S(2)}, u32[]{:S(2)}) collective-permute-start(bf16[256,256]{1,0:T(8,128)(2,1)} %get-tuple-element.938), channel_id=1, source_target_pairs={{0,32},{4,36},{8,40},{12,44},{16,48},{20,52},{24,56},{28,60},{32,0... | collective-permute-start | bytes 393224 | tf_op jit(solution)/shard_map/ppermute | solution.py:12
  144.6 3.6 concatenate.421
  148.2 3.2 collective-permute-start.19
  156.1 4.5 collective-permute-start.26
  160.7 2.2 collective-permute-start.2
  163.7 7.3 %collective-permute-start.5 = (bf16[512,256]{1,0:T(8,128)(2,1)}, bf16[512,256]{1,0:T(8,128)(2,1)}, u32[]{:S(2)}, u32[]{:S(2)}) collective-permute-start(bf16[512,256]{1,0:T(8,128)(2,1)} %pad_maximum_fusion.21), channel_id=1, source_target_pairs={{0,16},{4,20},{8,24},{12,28},{16,0},{20,4},{24,8},{28,12},{32,48},... | collective-permute-start | bytes 786440 | tf_op jit(solution)/shard_map/ppermute | solution.py:12
  172.6 5.3 collective-permute-start.9
  179.6 2.3 collective-permute-start.14
  183.5 3.5 collective-permute-start.20
  187.0 4.3 concatenate.422
  191.9 4.8 collective-permute-start.27
  228.8 3.1 collective-permute-start.29
  246.0 2.8 collective-permute-start.28
  269.5 4.0 collective-permute-start.31
  295.0 8.5 %collective-permute-start.34 = (f32[512,256]{1,0:T(8,128)}, f32[512,256]{1,0:T(8,128)}, u32[]{:S(2)}, u32[]{:S(2)}) collective-permute-start(f32[512,256]{1,0:T(8,128)} %bitcast.198), channel_id=1, source_target_pairs={{0,32},{4,36},{8,40},{12,44},{16,48},{20,52},{24,56},{28,60},{32,0... | collective-permute-start | bytes 1572872 | tf_op jit(solution)/shard_map/ppermute | solution.py:12
  319.3 1.9 fusion.64
  327.3 2.2 collective-permute-start.38
  329.6 1.9 concatenate.423
  347.6 2.0 copy.616
  349.6 2.0 stack_reshape.62
  358.4 111.3 %psum.7 = f32[16]{0:T(128)} all-reduce(f32[16]{0:T(128)S(1)} %stack.99), channel_id=1, replica_groups=mesh['seq'=128,'dp'=4] {'seq','dp'}, use_global_device_ids=true, to_apply=%region_89.90 | all-reduce | flops 16 | bytes 128 | tf_op jit(solution)/shard_map/psum | solution.py:162
  474.9 2.0 copy.653
  476.9 2.0 copy.652
  479.0 3.2 collective-permute-start.43
  483.9 2.5 collective-permute-start.49
  487.5 3.7 collective-permute-start.30
  492.3 1.9 collective-permute-start.32
  495.4 6.0 collective-permute-start.35
  502.5 6.2 collective-permute-start.39
  508.8 3.1 collective-permute-start.44
  512.0 4.4 collective-permute-start.50
  517.1 9.8 %collective-permute-done.32 = f32[256,256]{1,0:T(8,128)S(1)} collective-permute-done((f32[256,256]{1,0:T(8,128)S(1)}, f32[256,256]{1,0:T(8,128)S(1)}, u32[]{:S(2)}, u32[]{:S(2)}) %collective-permute-start.32) | collective-permute-done | bytes 262176 | tf_op jit(solution)/shard_map/ppermute | solution.py:12
  528.9 19.6 %collective-permute-done.35 = f32[256,256]{1,0:T(8,128)S(1)} collective-permute-done((f32[256,256]{1,0:T(8,128)S(1)}, f32[256,256]{1,0:T(8,128)S(1)}, u32[]{:S(2)}, u32[]{:S(2)}) %collective-permute-start.35) | collective-permute-done | bytes 262176 | tf_op jit(solution)/shard_map/ppermute | solution.py:12
  552.6 7.9 %collective-permute-start.45 = (f32[128,256]{1,0:T(8,128)S(1)}, f32[128,256]{1,0:T(8,128)S(1)}, u32[]{:S(2)}, u32[]{:S(2)}) collective-permute-start(f32[128,256]{1,0:T(8,128)S(1)} %slice.2495), channel_id=1, source_target_pairs={{0,32},{4,36},{8,40},{12,44},{16,48},{20,52},{24,56},{28,60},{32,0... | collective-permute-start | bytes 393224 | tf_op jit(solution)/shard_map/ppermute | solution.py:12
  560.6 2.1 collective-permute-start.51
  563.7 5.0 collective-permute-start.37
  568.6 8.7 %collective-permute-done.40 = f32[128,256]{1,0:T(8,128)S(1)} collective-permute-done((f32[128,256]{1,0:T(8,128)S(1)}, f32[128,256]{1,0:T(8,128)S(1)}, u32[]{:S(2)}, u32[]{:S(2)}) %collective-permute-start.40) | collective-permute-done | bytes 131104 | tf_op jit(solution)/shard_map/ppermute | solution.py:12
  577.4 1.9 collective-permute-start.41
  579.4 8.5 %collective-permute-start.46 = (f32[64,256]{1,0:T(8,128)S(1)}, f32[64,256]{1,0:T(8,128)S(1)}, u32[]{:S(2)}, u32[]{:S(2)}) collective-permute-start(f32[64,256]{1,0:T(8,128)S(1)} %slice.2497), channel_id=1, source_target_pairs={{0,16},{4,20},{8,24},{12,28},{16,0},{20,4},{24,8},{28,12},{32,48},... | collective-permute-start | bytes 196616 | tf_op jit(solution)/shard_map/ppermute | solution.py:12
  587.9 7.7 %collective-permute-start.52 = (f32[64,256]{1,0:T(8,128)S(1)}, f32[64,256]{1,0:T(8,128)S(1)}, u32[]{:S(2)}, u32[]{:S(2)}) collective-permute-start(f32[64,256]{1,0:T(8,128)S(1)} %slice.2511), channel_id=1, source_target_pairs={{0,32},{4,36},{8,40},{12,44},{16,48},{20,52},{24,56},{28,60},{32,0... | collective-permute-start | bytes 196616 | tf_op jit(solution)/shard_map/ppermute | solution.py:12
  596.4 1.9 collective-permute-start.42
  600.3 4.9 collective-permute-done.52
  605.3 1.9 collective-permute-start.53
  608.0 1.9 collective-permute-start.48
  609.9 3.9 collective-permute-done.53
  616.5 2.8 collective-permute-done.54
  621.2 2.5 collective-permute-done.55
  (847 shorter events, 208.2 us)
Async XLA Ops:
  2.0 56.9 %collective-permute-start.21 = (bf16[8,256]{1,0:T(8,128)(2,1)S(1)}, bf16[8,256]{1,0:T(8,128)(2,1)S(1)}, u32[]{:S(2)}, u32[]{:S(2)}) collective-permute-start(bf16[8,256]{1,0:T(8,128)(2,1)S(1)} %maximum_maximum_fusion.4), channel_id=1, source_target_pairs={{0,4},{4,0},{8,12},{12,8},{16,20},{20,16},{24,28},{28,24},{32,36},... | collective-permute-start | bytes 12296 | tf_op jit(solution)/shard_map/ppermute | solution.py:12
  6.5 54.4 %collective-permute-start.15 = (bf16[16,256]{1,0:T(8,128)(2,1)S(1)}, bf16[16,256]{1,0:T(8,128)(2,1)S(1)}, u32[]{:S(2)}, u32[]{:S(2)}) collective-permute-start(bf16[16,256]{1,0:T(8,128)(2,1)S(1)} %maximum_maximum_fusion.3), channel_id=1, source_target_pairs={{0,4},{4,0},{8,12},{12,8},{16,20},{20,16},{24,28},{28,24},{32,36},... | collective-permute-start | bytes 24584 | tf_op jit(solution)/shard_map/ppermute | solution.py:12
  8.5 61.7 %collective-permute-start.10 = (bf16[32,256]{1,0:T(8,128)(2,1)S(1)}, bf16[32,256]{1,0:T(8,128)(2,1)S(1)}, u32[]{:S(2)}, u32[]{:S(2)}) collective-permute-start(bf16[32,256]{1,0:T(8,128)(2,1)S(1)} %maximum_maximum_fusion.2), channel_id=1, source_target_pairs={{0,4},{4,0},{8,12},{12,8},{16,20},{20,16},{24,28},{28,24},{32,36},... | collective-permute-start | bytes 49160 | tf_op jit(solution)/shard_map/ppermute | solution.py:12
  12.0 77.9 %collective-permute-start.6 = (bf16[64,256]{1,0:T(8,128)(2,1)S(1)}, bf16[64,256]{1,0:T(8,128)(2,1)S(1)}, u32[]{:S(2)}, u32[]{:S(2)}) collective-permute-start(bf16[64,256]{1,0:T(8,128)(2,1)S(1)} %maximum_maximum_fusion.1), channel_id=1, source_target_pairs={{0,4},{4,0},{8,12},{12,8},{16,20},{20,16},{24,28},{28,24},{32,36},... | collective-permute-start | bytes 98312 | tf_op jit(solution)/shard_map/ppermute | solution.py:12
  14.1 101.2 %collective-permute-start.3 = (bf16[128,256]{1,0:T(8,128)(2,1)S(1)}, bf16[128,256]{1,0:T(8,128)(2,1)S(1)}, u32[]{:S(2)}, u32[]{:S(2)}) collective-permute-start(bf16[128,256]{1,0:T(8,128)(2,1)S(1)} %maximum_maximum_fusion), channel_id=1, source_target_pairs={{0,4},{4,0},{8,12},{12,8},{16,20},{20,16},{24,28},{28,24},{32,36},... | collective-permute-start | bytes 196616 | tf_op jit(solution)/shard_map/ppermute | solution.py:12
  26.2 4.2 copy-start.52
  58.9 96.6 %collective-permute-start.1 = (bf16[256,256]{1,0:T(8,128)(2,1)S(1)}, bf16[256,256]{1,0:T(8,128)(2,1)S(1)}, u32[]{:S(2)}, u32[]{:S(2)}) collective-permute-start(bf16[256,256]{1,0:T(8,128)(2,1)S(1)} %pad_maximum_fusion.26), channel_id=1, source_target_pairs={{0,4},{4,0},{8,12},{12,8},{16,20},{20,16},{24,28},{28,24},{32,36},... | collective-permute-start | bytes 393224 | tf_op jit(solution)/shard_map/ppermute | solution.py:12
  60.9 5.9 collective-permute-start.22
  66.8 81.4 %collective-permute-start = (bf16[256,256]{1,0:T(8,128)(2,1)S(1)}, bf16[256,256]{1,0:T(8,128)(2,1)S(1)}, u32[]{:S(2)}, u32[]{:S(2)}) collective-permute-start(bf16[256,256]{1,0:T(8,128)(2,1)S(1)} %pad_maximum_fusion.25), channel_id=1, source_target_pairs={{0,4},{4,0},{8,12},{12,8},{16,20},{20,16},{24,28},{28,24},{32,36},... | collective-permute-start | bytes 393224 | tf_op jit(solution)/shard_map/ppermute | solution.py:12
  70.2 5.4 collective-permute-start.16
  75.6 10.0 %collective-permute-start.23 = (bf16[32,256]{1,0:T(8,128)(2,1)S(1)}, bf16[32,256]{1,0:T(8,128)(2,1)S(1)}, u32[]{:S(2)}, u32[]{:S(2)}) collective-permute-start(bf16[32,256]{1,0:T(8,128)(2,1)S(1)} %pad_maximum_fusion.36), channel_id=1, source_target_pairs={{0,16},{4,20},{8,24},{12,28},{16,0},{20,4},{24,8},{28,12},{32,48},... | collective-permute-start | bytes 49160 | tf_op jit(solution)/shard_map/ppermute | solution.py:12
  85.6 12.3 %collective-permute-start.11 = (bf16[64,256]{1,0:T(8,128)(2,1)S(1)}, bf16[64,256]{1,0:T(8,128)(2,1)S(1)}, u32[]{:S(2)}, u32[]{:S(2)}) collective-permute-start(bf16[64,256]{1,0:T(8,128)(2,1)S(1)} %pad_maximum_fusion.31), channel_id=1, source_target_pairs={{0,8},{4,12},{8,0},{12,4},{16,24},{20,28},{24,16},{28,20},{32,40},... | collective-permute-start | bytes 98312 | tf_op jit(solution)/shard_map/ppermute | solution.py:12
  90.0 16.4 %collective-permute-start.17 = (bf16[64,256]{1,0:T(8,128)(2,1)S(1)}, bf16[64,256]{1,0:T(8,128)(2,1)S(1)}, u32[]{:S(2)}, u32[]{:S(2)}) collective-permute-start(bf16[64,256]{1,0:T(8,128)(2,1)S(1)} %pad_maximum_fusion.32), channel_id=1, source_target_pairs={{0,16},{4,20},{8,24},{12,28},{16,0},{20,4},{24,8},{28,12},{32,48},... | collective-permute-start | bytes 98312 | tf_op jit(solution)/shard_map/ppermute | solution.py:12
  97.9 13.7 %collective-permute-start.24 = (bf16[64,256]{1,0:T(8,128)(2,1)S(1)}, bf16[64,256]{1,0:T(8,128)(2,1)S(1)}, u32[]{:S(2)}, u32[]{:S(2)}) collective-permute-start(bf16[64,256]{1,0:T(8,128)(2,1)S(1)} %concatenate.419), channel_id=1, source_target_pairs={{0,32},{4,36},{8,40},{12,44},{16,48},{20,52},{24,56},{28,60},{32,0... | collective-permute-start | bytes 98312 | tf_op jit(solution)/shard_map/ppermute | solution.py:12
  106.4 18.6 %collective-permute-start.7 = (bf16[128,256]{1,0:T(8,128)(2,1)S(1)}, bf16[128,256]{1,0:T(8,128)(2,1)S(1)}, u32[]{:S(2)}, u32[]{:S(2)}) collective-permute-start(bf16[128,256]{1,0:T(8,128)(2,1)S(1)} %pad_maximum_fusion.29), channel_id=1, source_target_pairs={{0,8},{4,12},{8,0},{12,4},{16,24},{20,28},{24,16},{28,20},{32,40},... | collective-permute-start | bytes 196616 | tf_op jit(solution)/shard_map/ppermute | solution.py:12
  111.6 18.0 %collective-permute-start.12 = (bf16[128,256]{1,0:T(8,128)(2,1)S(1)}, bf16[128,256]{1,0:T(8,128)(2,1)S(1)}, u32[]{:S(2)}, u32[]{:S(2)}) collective-permute-start(bf16[128,256]{1,0:T(8,128)(2,1)S(1)} %pad_maximum_fusion.30), channel_id=1, source_target_pairs={{0,16},{4,20},{8,24},{12,28},{16,0},{20,4},{24,8},{28,12},{32,48},... | collective-permute-start | bytes 196616 | tf_op jit(solution)/shard_map/ppermute | solution.py:12
  115.3 18.0 %collective-permute-start.18 = (bf16[128,256]{1,0:T(8,128)(2,1)}, bf16[128,256]{1,0:T(8,128)(2,1)S(1)}, u32[]{:S(2)}, u32[]{:S(2)}) collective-permute-start(bf16[128,256]{1,0:T(8,128)(2,1)} %get-tuple-element.952), channel_id=1, source_target_pairs={{0,32},{4,36},{8,40},{12,44},{16,48},{20,52},{24,56},{28,60},{32,0... | collective-permute-start | bytes 196616 | tf_op jit(solution)/shard_map/ppermute | solution.py:12
  125.0 13.1 %collective-permute-start.25 = (bf16[128,256]{1,0:T(8,128)(2,1)S(1)}, bf16[128,256]{1,0:T(8,128)(2,1)S(1)}, u32[]{:S(2)}, u32[]{:S(2)}) collective-permute-start(bf16[128,256]{1,0:T(8,128)(2,1)S(1)} %concatenate.420), channel_id=1, source_target_pairs={{0,64},{4,68},{8,72},{12,76},{16,80},{20,84},{24,88},{28,92},{32,9... | collective-permute-start | bytes 196616 | tf_op jit(solution)/shard_map/ppermute | solution.py:12
  129.5 31.1 %collective-permute-start.4 = (bf16[256,256]{1,0:T(8,128)(2,1)}, bf16[256,256]{1,0:T(8,128)(2,1)S(1)}, u32[]{:S(2)}, u32[]{:S(2)}) collective-permute-start(bf16[256,256]{1,0:T(8,128)(2,1)} %pad_maximum_fusion.27), channel_id=1, source_target_pairs={{0,8},{4,12},{8,0},{12,4},{16,24},{20,28},{24,16},{28,20},{32,40},... | collective-permute-start | bytes 393224 | tf_op jit(solution)/shard_map/ppermute | solution.py:12
  133.4 30.3 %collective-permute-start.8 = (bf16[256,256]{1,0:T(8,128)(2,1)}, bf16[256,256]{1,0:T(8,128)(2,1)}, u32[]{:S(2)}, u32[]{:S(2)}) collective-permute-start(bf16[256,256]{1,0:T(8,128)(2,1)} %pad_maximum_fusion.28), channel_id=1, source_target_pairs={{0,16},{4,20},{8,24},{12,28},{16,0},{20,4},{24,8},{28,12},{32,48},... | collective-permute-start | bytes 393224 | tf_op jit(solution)/shard_map/ppermute | solution.py:12
  138.1 34.5 %collective-permute-start.13 = (bf16[256,256]{1,0:T(8,128)(2,1)}, bf16[256,256]{1,0:T(8,128)(2,1)}, u32[]{:S(2)}, u32[]{:S(2)}) collective-permute-start(bf16[256,256]{1,0:T(8,128)(2,1)} %get-tuple-element.938), channel_id=1, source_target_pairs={{0,32},{4,36},{8,40},{12,44},{16,48},{20,52},{24,56},{28,60},{32,0... | collective-permute-start | bytes 393224 | tf_op jit(solution)/shard_map/ppermute | solution.py:12
  148.2 31.3 %collective-permute-start.19 = (bf16[256,256]{1,0:T(8,128)(2,1)}, bf16[256,256]{1,0:T(8,128)(2,1)}, u32[]{:S(2)}, u32[]{:S(2)}) collective-permute-start(bf16[256,256]{1,0:T(8,128)(2,1)} %get-tuple-element.935), channel_id=1, source_target_pairs={{0,64},{4,68},{8,72},{12,76},{16,80},{20,84},{24,88},{28,92},{32,9... | collective-permute-start | bytes 393224 | tf_op jit(solution)/shard_map/ppermute | solution.py:12
  156.1 27.4 %collective-permute-start.26 = (bf16[256,256]{1,0:T(8,128)(2,1)S(1)}, bf16[256,256]{1,0:T(8,128)(2,1)S(1)}, u32[]{:S(2)}, u32[]{:S(2)}) collective-permute-start(bf16[256,256]{1,0:T(8,128)(2,1)S(1)} %copy-done.25), channel_id=1, source_target_pairs={{0,128},{4,132},{8,136},{12,140},{16,144},{20,148},{24,152},{28,15... | collective-permute-start | bytes 393224 | tf_op jit(solution)/shard_map/ppermute | solution.py:12
  160.7 30.6 %collective-permute-start.2 = (bf16[512,256]{1,0:T(8,128)(2,1)S(1)}, bf16[512,256]{1,0:T(8,128)(2,1)S(1)}, u32[]{:S(2)}, u32[]{:S(2)}) collective-permute-start(bf16[512,256]{1,0:T(8,128)(2,1)S(1)} %pad_maximum_fusion.20), channel_id=1, source_target_pairs={{0,8},{4,12},{8,0},{12,4},{16,24},{20,28},{24,16},{28,20},{32,40},... | collective-permute-start | bytes 786440 | tf_op jit(solution)/shard_map/ppermute | solution.py:12
  163.7 65.1 %collective-permute-start.5 = (bf16[512,256]{1,0:T(8,128)(2,1)}, bf16[512,256]{1,0:T(8,128)(2,1)}, u32[]{:S(2)}, u32[]{:S(2)}) collective-permute-start(bf16[512,256]{1,0:T(8,128)(2,1)} %pad_maximum_fusion.21), channel_id=1, source_target_pairs={{0,16},{4,20},{8,24},{12,28},{16,0},{20,4},{24,8},{28,12},{32,48},... | collective-permute-start | bytes 786440 | tf_op jit(solution)/shard_map/ppermute | solution.py:12
  172.6 73.5 %collective-permute-start.9 = (bf16[512,256]{1,0:T(8,128)(2,1)}, bf16[512,256]{1,0:T(8,128)(2,1)}, u32[]{:S(2)}, u32[]{:S(2)}) collective-permute-start(bf16[512,256]{1,0:T(8,128)(2,1)} %get-tuple-element.925), channel_id=1, source_target_pairs={{0,32},{4,36},{8,40},{12,44},{16,48},{20,52},{24,56},{28,60},{32,0... | collective-permute-start | bytes 786440 | tf_op jit(solution)/shard_map/ppermute | solution.py:12
  179.6 89.9 %collective-permute-start.14 = (bf16[512,256]{1,0:T(8,128)(2,1)}, bf16[512,256]{1,0:T(8,128)(2,1)}, u32[]{:S(2)}, u32[]{:S(2)}) collective-permute-start(bf16[512,256]{1,0:T(8,128)(2,1)} %get-tuple-element.923), channel_id=1, source_target_pairs={{0,64},{4,68},{8,72},{12,76},{16,80},{20,84},{24,88},{28,92},{32,9... | collective-permute-start | bytes 786440 | tf_op jit(solution)/shard_map/ppermute | solution.py:12
  183.5 7.8 %copy-start.9 = (bf16[256,256]{1,0:T(8,128)(2,1)}, bf16[256,256]{1,0:T(8,128)(2,1)S(1)}, u32[]{:S(2)}) copy-start(bf16[256,256]{1,0:T(8,128)(2,1)S(1)} %collective-permute-done.26) | copy-start | bytes 393220
  183.5 111.5 %collective-permute-start.20 = (bf16[512,256]{1,0:T(8,128)(2,1)}, bf16[512,256]{1,0:T(8,128)(2,1)}, u32[]{:S(2)}, u32[]{:S(2)}) collective-permute-start(bf16[512,256]{1,0:T(8,128)(2,1)} %get-tuple-element.921), channel_id=1, source_target_pairs={{0,128},{4,132},{8,136},{12,140},{16,144},{20,148},{24,152},{28,15... | collective-permute-start | bytes 786440 | tf_op jit(solution)/shard_map/ppermute | solution.py:12
  191.9 135.4 %collective-permute-start.27 = (bf16[512,256]{1,0:T(8,128)(2,1)}, bf16[512,256]{1,0:T(8,128)(2,1)}, u32[]{:S(2)}, u32[]{:S(2)}) collective-permute-start(bf16[512,256]{1,0:T(8,128)(2,1)} %concatenate.422), channel_id=1, source_target_pairs={{0,256},{4,260},{8,264},{12,268},{16,272},{20,276},{24,280},{28,28... | collective-permute-start | bytes 786440 | tf_op jit(solution)/shard_map/ppermute | solution.py:12
  197.8 21.2 %copy-start.5 = (bf16[4,1,128,256]{3,2,1,0:T(8,128)(2,1)}, bf16[4,1,128,256]{3,2,1,0:T(8,128)(2,1)S(1)}, u32[]{:S(2)}) copy-start(bf16[4,1,128,256]{3,2,1,0:T(8,128)(2,1)S(1)} %get-tuple-element.905) | copy-start | bytes 786436
  205.8 5.9 copy-start.36
  206.7 5.3 copy-start.38
  208.2 4.4 copy-start.46
  228.8 255.1 %collective-permute-start.29 = (f32[512,256]{0,1:T(8,128)}, f32[512,256]{0,1:T(8,128)}, u32[]{:S(2)}, u32[]{:S(2)}) collective-permute-start(f32[512,256]{0,1:T(8,128)} %slice.2212), channel_id=1, source_target_pairs={{0,8},{4,12},{8,0},{12,4},{16,24},{20,28},{24,16},{28,20},{32,40},... | collective-permute-start | bytes 1572872 | tf_op jit(solution)/shard_map/ppermute | solution.py:12
  246.0 232.9 %collective-permute-start.28 = (f32[256,256]{0,1:T(8,128)}, f32[256,256]{0,1:T(8,128)}, u32[]{:S(2)}, u32[]{:S(2)}) collective-permute-start(f32[256,256]{0,1:T(8,128)} %bitcast.622), channel_id=1, source_target_pairs={{0,4},{4,0},{8,12},{12,8},{16,20},{20,16},{24,28},{28,24},{32,36},... | collective-permute-start | bytes 786440 | tf_op jit(solution)/shard_map/ppermute | solution.py:12
  269.5 218.1 %collective-permute-start.31 = (f32[512,256]{1,0:T(8,128)}, f32[512,256]{1,0:T(8,128)}, u32[]{:S(2)}, u32[]{:S(2)}) collective-permute-start(f32[512,256]{1,0:T(8,128)} %bitcast.190), channel_id=1, source_target_pairs={{0,16},{4,20},{8,24},{12,28},{16,0},{20,4},{24,8},{28,12},{32,48},... | collective-permute-start | bytes 1572872 | tf_op jit(solution)/shard_map/ppermute | solution.py:12
  295.0 197.3 %collective-permute-start.34 = (f32[512,256]{1,0:T(8,128)}, f32[512,256]{1,0:T(8,128)}, u32[]{:S(2)}, u32[]{:S(2)}) collective-permute-start(f32[512,256]{1,0:T(8,128)} %bitcast.198), channel_id=1, source_target_pairs={{0,32},{4,36},{8,40},{12,44},{16,48},{20,52},{24,56},{28,60},{32,0... | collective-permute-start | bytes 1572872 | tf_op jit(solution)/shard_map/ppermute | solution.py:12
  305.2 3.8 copy-start.69
  327.3 168.1 %collective-permute-start.38 = (f32[512,256]{1,0:T(8,128)}, f32[512,256]{1,0:T(8,128)}, u32[]{:S(2)}, u32[]{:S(2)}) collective-permute-start(f32[512,256]{1,0:T(8,128)} %bitcast.206), channel_id=1, source_target_pairs={{0,64},{4,68},{8,72},{12,76},{16,80},{20,84},{24,88},{28,92},{32,9... | collective-permute-start | bytes 1572872 | tf_op jit(solution)/shard_map/ppermute | solution.py:12
  479.0 4.9 copy-start.8
  479.0 23.6 %collective-permute-start.43 = (f32[512,256]{1,0:T(8,128)}, f32[512,256]{1,0:T(8,128)S(1)}, u32[]{:S(2)}, u32[]{:S(2)}) collective-permute-start(f32[512,256]{1,0:T(8,128)} %bitcast.691), channel_id=1, source_target_pairs={{0,128},{4,132},{8,136},{12,140},{16,144},{20,148},{24,152},{28,15... | collective-permute-start | bytes 1572872 | tf_op jit(solution)/shard_map/ppermute | solution.py:12
  483.9 24.9 %collective-permute-start.49 = (f32[512,256]{1,0:T(8,128)S(1)}, f32[512,256]{1,0:T(8,128)S(1)}, u32[]{:S(2)}, u32[]{:S(2)}) collective-permute-start(f32[512,256]{1,0:T(8,128)S(1)} %copy-done.8), channel_id=1, source_target_pairs={{0,256},{4,260},{8,264},{12,268},{16,272},{20,276},{24,280},{28,28... | collective-permute-start | bytes 1572872 | tf_op jit(solution)/shard_map/ppermute | solution.py:12
  487.5 24.5 %collective-permute-start.30 = (f32[256,256]{0,1:T(8,128)S(1)}, f32[256,256]{0,1:T(8,128)S(1)}, u32[]{:S(2)}, u32[]{:S(2)}) collective-permute-start(f32[256,256]{0,1:T(8,128)S(1)} %slice.2458), channel_id=1, source_target_pairs={{0,4},{4,0},{8,12},{12,8},{16,20},{20,16},{24,28},{28,24},{32,36},... | collective-permute-start | bytes 786440 | tf_op jit(solution)/shard_map/ppermute | solution.py:12
  492.3 34.6 %collective-permute-start.32 = (f32[256,256]{1,0:T(8,128)S(1)}, f32[256,256]{1,0:T(8,128)S(1)}, u32[]{:S(2)}, u32[]{:S(2)}) collective-permute-start(f32[256,256]{1,0:T(8,128)S(1)} %slice.2463), channel_id=1, source_target_pairs={{0,8},{4,12},{8,0},{12,4},{16,24},{20,28},{24,16},{28,20},{32,40},... | collective-permute-start | bytes 786440 | tf_op jit(solution)/shard_map/ppermute | solution.py:12
  495.4 53.2 %collective-permute-start.35 = (f32[256,256]{1,0:T(8,128)S(1)}, f32[256,256]{1,0:T(8,128)S(1)}, u32[]{:S(2)}, u32[]{:S(2)}) collective-permute-start(f32[256,256]{1,0:T(8,128)S(1)} %slice.2471), channel_id=1, source_target_pairs={{0,16},{4,20},{8,24},{12,28},{16,0},{20,4},{24,8},{28,12},{32,48},... | collective-permute-start | bytes 786440 | tf_op jit(solution)/shard_map/ppermute | solution.py:12
  502.5 48.0 %collective-permute-start.39 = (f32[256,256]{1,0:T(8,128)S(1)}, f32[256,256]{1,0:T(8,128)S(1)}, u32[]{:S(2)}, u32[]{:S(2)}) collective-permute-start(f32[256,256]{1,0:T(8,128)S(1)} %slice.2481), channel_id=1, source_target_pairs={{0,32},{4,36},{8,40},{12,44},{16,48},{20,52},{24,56},{28,60},{32,0... | collective-permute-start | bytes 786440 | tf_op jit(solution)/shard_map/ppermute | solution.py:12
  508.8 43.7 %collective-permute-start.44 = (f32[256,256]{1,0:T(8,128)S(1)}, f32[256,256]{1,0:T(8,128)S(1)}, u32[]{:S(2)}, u32[]{:S(2)}) collective-permute-start(f32[256,256]{1,0:T(8,128)S(1)} %slice.2493), channel_id=1, source_target_pairs={{0,64},{4,68},{8,72},{12,76},{16,80},{20,84},{24,88},{28,92},{32,9... | collective-permute-start | bytes 786440 | tf_op jit(solution)/shard_map/ppermute | solution.py:12
  512.0 48.5 %collective-permute-start.50 = (f32[256,256]{1,0:T(8,128)S(1)}, f32[256,256]{1,0:T(8,128)S(1)}, u32[]{:S(2)}, u32[]{:S(2)}) collective-permute-start(f32[256,256]{1,0:T(8,128)S(1)} %slice.2507), channel_id=1, source_target_pairs={{0,128},{4,132},{8,136},{12,140},{16,144},{20,148},{24,152},{28,15... | collective-permute-start | bytes 786440 | tf_op jit(solution)/shard_map/ppermute | solution.py:12
  527.0 35.7 %collective-permute-start.33 = (f32[128,256]{1,0:T(8,128)S(1)}, f32[128,256]{1,0:T(8,128)S(1)}, u32[]{:S(2)}, u32[]{:S(2)}) collective-permute-start(f32[128,256]{1,0:T(8,128)S(1)} %slice.2465), channel_id=1, source_target_pairs={{0,4},{4,0},{8,12},{12,8},{16,20},{20,16},{24,28},{28,24},{32,36},... | collective-permute-start | bytes 393224 | tf_op jit(solution)/shard_map/ppermute | solution.py:12
  548.6 15.0 %collective-permute-start.36 = (f32[128,256]{1,0:T(8,128)S(1)}, f32[128,256]{1,0:T(8,128)S(1)}, u32[]{:S(2)}, u32[]{:S(2)}) collective-permute-start(f32[128,256]{1,0:T(8,128)S(1)} %slice.2473), channel_id=1, source_target_pairs={{0,8},{4,12},{8,0},{12,4},{16,24},{20,28},{24,16},{28,20},{32,40},... | collective-permute-start | bytes 393224 | tf_op jit(solution)/shard_map/ppermute | solution.py:12
  550.6 26.7 %collective-permute-start.40 = (f32[128,256]{1,0:T(8,128)S(1)}, f32[128,256]{1,0:T(8,128)S(1)}, u32[]{:S(2)}, u32[]{:S(2)}) collective-permute-start(f32[128,256]{1,0:T(8,128)S(1)} %slice.2483), channel_id=1, source_target_pairs={{0,16},{4,20},{8,24},{12,28},{16,0},{20,4},{24,8},{28,12},{32,48},... | collective-permute-start | bytes 393224 | tf_op jit(solution)/shard_map/ppermute | solution.py:12
  552.6 26.7 %collective-permute-start.45 = (f32[128,256]{1,0:T(8,128)S(1)}, f32[128,256]{1,0:T(8,128)S(1)}, u32[]{:S(2)}, u32[]{:S(2)}) collective-permute-start(f32[128,256]{1,0:T(8,128)S(1)} %slice.2495), channel_id=1, source_target_pairs={{0,32},{4,36},{8,40},{12,44},{16,48},{20,52},{24,56},{28,60},{32,0... | collective-permute-start | bytes 393224 | tf_op jit(solution)/shard_map/ppermute | solution.py:12
  560.6 27.3 %collective-permute-start.51 = (f32[128,256]{1,0:T(8,128)S(1)}, f32[128,256]{1,0:T(8,128)S(1)}, u32[]{:S(2)}, u32[]{:S(2)}) collective-permute-start(f32[128,256]{1,0:T(8,128)S(1)} %slice.2509), channel_id=1, source_target_pairs={{0,64},{4,68},{8,72},{12,76},{16,80},{20,84},{24,88},{28,92},{32,9... | collective-permute-start | bytes 393224 | tf_op jit(solution)/shard_map/ppermute | solution.py:12
  563.7 31.9 %collective-permute-start.37 = (f32[64,256]{1,0:T(8,128)S(1)}, f32[64,256]{1,0:T(8,128)S(1)}, u32[]{:S(2)}, u32[]{:S(2)}) collective-permute-start(f32[64,256]{1,0:T(8,128)S(1)} %slice.2475), channel_id=1, source_target_pairs={{0,4},{4,0},{8,12},{12,8},{16,20},{20,16},{24,28},{28,24},{32,36},... | collective-permute-start | bytes 196616 | tf_op jit(solution)/shard_map/ppermute | solution.py:12
  577.4 19.0 %collective-permute-start.41 = (f32[64,256]{1,0:T(8,128)S(1)}, f32[64,256]{1,0:T(8,128)S(1)}, u32[]{:S(2)}, u32[]{:S(2)}) collective-permute-start(f32[64,256]{1,0:T(8,128)S(1)} %slice.2485), channel_id=1, source_target_pairs={{0,8},{4,12},{8,0},{12,4},{16,24},{20,28},{24,16},{28,20},{32,40},... | collective-permute-start | bytes 196616 | tf_op jit(solution)/shard_map/ppermute | solution.py:12
  579.4 19.0 %collective-permute-start.46 = (f32[64,256]{1,0:T(8,128)S(1)}, f32[64,256]{1,0:T(8,128)S(1)}, u32[]{:S(2)}, u32[]{:S(2)}) collective-permute-start(f32[64,256]{1,0:T(8,128)S(1)} %slice.2497), channel_id=1, source_target_pairs={{0,16},{4,20},{8,24},{12,28},{16,0},{20,4},{24,8},{28,12},{32,48},... | collective-permute-start | bytes 196616 | tf_op jit(solution)/shard_map/ppermute | solution.py:12
  587.9 17.4 %collective-permute-start.52 = (f32[64,256]{1,0:T(8,128)S(1)}, f32[64,256]{1,0:T(8,128)S(1)}, u32[]{:S(2)}, u32[]{:S(2)}) collective-permute-start(f32[64,256]{1,0:T(8,128)S(1)} %slice.2511), channel_id=1, source_target_pairs={{0,32},{4,36},{8,40},{12,44},{16,48},{20,52},{24,56},{28,60},{32,0... | collective-permute-start | bytes 196616 | tf_op jit(solution)/shard_map/ppermute | solution.py:12
  596.4 10.8 %collective-permute-start.42 = (f32[32,256]{1,0:T(8,128)S(1)}, f32[32,256]{1,0:T(8,128)S(1)}, u32[]{:S(2)}, u32[]{:S(2)}) collective-permute-start(f32[32,256]{1,0:T(8,128)S(1)} %slice.2487), channel_id=1, source_target_pairs={{0,4},{4,0},{8,12},{12,8},{16,20},{20,16},{24,28},{28,24},{32,36},... | collective-permute-start | bytes 98312 | tf_op jit(solution)/shard_map/ppermute | solution.py:12
  598.4 9.5 %collective-permute-start.47 = (f32[32,256]{1,0:T(8,128)S(1)}, f32[32,256]{1,0:T(8,128)S(1)}, u32[]{:S(2)}, u32[]{:S(2)}) collective-permute-start(f32[32,256]{1,0:T(8,128)S(1)} %slice.2499), channel_id=1, source_target_pairs={{0,8},{4,12},{8,0},{12,4},{16,24},{20,28},{24,16},{28,20},{32,40},... | collective-permute-start | bytes 98312 | tf_op jit(solution)/shard_map/ppermute | solution.py:12
  605.3 8.6 %collective-permute-start.53 = (f32[32,256]{1,0:T(8,128)S(1)}, f32[32,256]{1,0:T(8,128)S(1)}, u32[]{:S(2)}, u32[]{:S(2)}) collective-permute-start(f32[32,256]{1,0:T(8,128)S(1)} %slice.2513), channel_id=1, source_target_pairs={{0,16},{4,20},{8,24},{12,28},{16,0},{20,4},{24,8},{28,12},{32,48},... | collective-permute-start | bytes 98312 | tf_op jit(solution)/shard_map/ppermute | solution.py:12
  608.0 7.8 %collective-permute-start.48 = (f32[16,256]{1,0:T(8,128)S(1)}, f32[16,256]{1,0:T(8,128)S(1)}, u32[]{:S(2)}, u32[]{:S(2)}) collective-permute-start(f32[16,256]{1,0:T(8,128)S(1)} %slice.2501), channel_id=1, source_target_pairs={{0,4},{4,0},{8,12},{12,8},{16,20},{20,16},{24,28},{28,24},{32,36},... | collective-permute-start | bytes 49160 | tf_op jit(solution)/shard_map/ppermute | solution.py:12
  613.9 5.4 collective-permute-start.54
  619.3 4.4 collective-permute-start.55
  (109 other events, 119.6 us)
where the time goes:
time: 634 us; the launch traced here: 626 us
  starting transfers between devices  225 us (35%)
  local copies, waits for them, and re-layouts  133 us (21%)
  blocking collectives  111 us (18%)
  waiting for transfers between devices  55.3 us (9%)
  matrix products  47.1 us (7%)
  other arithmetic  29.4 us (5%)
  between operations  24.8 us (4%)
    ppermute x56, starting transfers between devices, partner(): lax.ppermute(array, axis, [(i, i ^ 1 << apart) for i in range(lax.axis_si...  225 us
    psum x1, blocking collectives, body(): scale_gradient = lax.psum(jnp.stack(scale_terms), ('seq', 'dp'))  111 us
    ppermute x56, waiting for transfers between devices, partner(): lax.ppermute(array, axis, [(i, i ^ 1 << apart) for i in range(lax.axis_si...  55.3 us
    unnamed x331, local copies, waits for them, and re-layouts  54 us
    concatenate x12, local copies, waits for them, and re-layouts, body(): jnp.concatenate([current, partner(current, 'seq', bit_num)], 0)  20.7 us
    dot_general x16, matrix products, body(): lax.dot_general(up_sel, val_sel, (((1,), (1,)), ((), ())), preferred_elem...  13.5 us
  transfers between devices with their start and end apart: 56, of which 11 were waited for; matrix products, arithmetic and copies ran while one was open for 29% of the time, Pallas kernels for 0%

commit v1 on v0

v1 whole, which is shorter than its diff:
```python
import math

import jax
import jax.numpy as jnp
from jax import lax
from jax.experimental import pallas as pl
from jax.experimental.pallas import tpu as pltpu
from jax.sharding import Mesh, PartitionSpec as P

D = 128
BF = jnp.bfloat16
F32 = jnp.float32
DIL = (1, 1, 1, 2, 4, 8, 16, 32)
SEQ = ("x", "y", "q", "r")


def off(level, j):
    dil = DIL[level]
    return (5 + j * (dil // 2)) % dil


def iota(shape, dim):
    return lax.broadcasted_iota(jnp.int32, shape, dim)


def onehot(cond):
    return cond.astype(F32).astype(BF)


def mm(a, b):
    return jnp.dot(a, b, preferred_element_type=F32)


def mm_nt(a, b):
    return lax.dot_general(a, b, (((1,), (1,)), ((), ())), preferred_element_type=F32)


def mm_tn(a, b):
    return lax.dot_general(a, b, (((0,), (0,)), ((), ())), preferred_element_type=F32)


def pick(level, j, rows=128):
    n = 128 // DIL[level]
    return onehot(iota((n, 128), 1) == iota((n, 128), 0) * DIL[level] + off(level, j))


def cols(ref, head, first=0):
    return ref[:, pl.ds(pl.multiple_of((head - first) * D, D), D)]


def xyqr(dev):
    return dev >> 6, (dev >> 4) & 3, (dev >> 2) & 3, dev & 3


def xy_col(x, y, row):
    t, m = row >> 5, row & 31
    six = (x * 4 + (m >> 3)) * 32 + t * 8 + (m & 7)
    seven = (m >> 2) * 32 + t * 4 + (m & 3)
    return jnp.where(y < 2, six, jnp.where(y == 2, seven, -1))


def pack_kernel(ids, q_ref, k_ref, v_ref, u_ref, g1_ref, g3_ref, g5_ref, xy_ref):
    x, y, q, r = xyqr(ids[0])
    srcs = (q_ref, k_ref, v_ref, u_ref)
    h1 = 3 - (r & 1)
    j3 = 1 - (q & 1)
    j5 = 1 - (y & 1)
    s3, s5 = pick(3, j3), pick(5, j5)
    xy_ref[...] = jnp.zeros(xy_ref.shape, BF)
    for t, ref in enumerate(srcs):
        g1_ref[t * 128 : (t + 1) * 128] = cols(ref, h1)
        g3_ref[t * 64 : (t + 1) * 64] = mm(s3, cols(ref, 6 + j3)).astype(BF)
        g5_ref[t * 16 : (t + 1) * 16] = mm(s5, cols(ref, 10 + j5)).astype(BF)
    for j in range(2):
        acc6 = jnp.zeros((32, D), F32)
        acc7 = jnp.zeros((32, D), F32)
        ri, ci = iota((32, 128), 0), iota((32, 128), 1)
        for t, ref in enumerate(srcs):
            w6 = onehot((ci == (ri - t * 8) * 16 + off(6, j)))
            w7 = onehot((ci == (ri - t * 4) * 32 + off(7, j)))
            acc6 += mm(w6, ref[:, (12 + j) * D : (13 + j) * D])
            acc7 += mm(w7, ref[:, (14 + j) * D : (15 + j) * D])
        xy_ref[x * 4 + j] = acc6.astype(BF)
        xy_ref[j * 4 + 2] = acc7.astype(BF)


def to_q_kernel(ids, q_ref, k_ref, v_ref, u_ref, g5_ref, xy_ref, out_ref):
    x, y, q, r = xyqr(ids[0])
    j5 = y & 1
    s40, s41, s5 = pick(4, 0), pick(4, 1), pick(5, j5)
    for t, ref in enumerate((q_ref, k_ref, v_ref, u_ref)):
        out_ref[0, t * 32 : (t + 1) * 32] = mm(s40, ref[:, :D]).astype(BF)
        out_ref[1, t * 32 : (t + 1) * 32] = mm(s41, ref[:, D : 2 * D]).astype(BF)
        out_ref[2, t * 32 : t * 32 + 16] = mm(s5, cols(ref, 2 + j5)).astype(BF)
        out_ref[2, t * 32 + 16 : t * 32 + 32] = g5_ref[t * 16 : (t + 1) * 16]
    want = xy_col(x, y, iota((128, 256), 0))
    perm = onehot(want == iota((128, 256), 1))
    out_ref[3] = mm(perm, xy_ref[...].reshape(256, D)).astype(BF)


def to_r_kernel(ids, q_ref, k_ref, v_ref, u_ref, g3_ref, qr_ref, out_ref):
    x, y, q, r = xyqr(ids[0])
    j3 = q & 1
    s3 = pick(3, j3)
    for t, ref in enumerate((q_ref, k_ref, v_ref, u_ref)):
        lo = t * 128
        out_ref[0, lo : lo + 128] = ref[:, :D]
        out_ref[1, lo : lo + 128] = ref[:, D : 2 * D]
        out_ref[2, lo : lo + 64] = mm(s3, cols(ref, 2 + j3)).astype(BF)
        out_ref[2, lo + 64 : lo + 128] = g3_ref[t * 64 : (t + 1) * 64]
        for u in range(4):
            out_ref[3, lo + u * 32 : lo + u * 32 + 32] = qr_ref[u, t * 32 : (t + 1) * 32]


def attention(qs, ks, vs, us, docs, mult):
    nb = len(qs)
    keys, vals = jnp.concatenate(ks, 0), jnp.concatenate(vs, 0)
    doc_all = jnp.concatenate(docs, 0)
    outs, dqs, dk, dv, term = [], [], None, None, jnp.zeros((1, 1), F32)
    for b in range(nb):
        raw = mm_nt(qs[b], keys)
        allowed = mm_nt(docs[b], doc_all) > 0.5
        scores = jnp.where(allowed, raw * mult, -1e30)
        expo = jnp.exp(scores - jnp.max(scores, axis=1, keepdims=True))
        probs = expo * (1.0 / jnp.sum(expo, axis=1, keepdims=True))
        low = probs.astype(BF)
        att = mm(low, vals)
        delta = jnp.sum(us[b].astype(F32) * att, axis=1, keepdims=True)
        ds = probs * (mm_nt(us[b], vals) - delta)
        term += jnp.sum(jnp.sum(ds * raw, axis=1, keepdims=True), axis=0, keepdims=True)
        ds_low = ds.astype(BF)
        outs.append(att.astype(BF))
        dqs.append((mm(ds_low, keys) * mult).astype(BF))
        dk_b, dv_b = mm_tn(ds_low, qs[b]), mm_tn(low, us[b])
        dk, dv = (dk_b, dv_b) if dk is None else (dk + dk_b, dv + dv_b)
    dk = (dk * mult).astype(BF)
    dv = dv.astype(BF)
    part = lambda z: [z[b * 128 : (b + 1) * 128] for b in range(nb)]
    return outs, dqs, part(dk), part(dv), term * (1.0 / math.sqrt(D))


def doc_onehot(pos, bounds_ref):
    return onehot((pos >= bounds_ref[0:1]) & (pos < bounds_ref[1:2]))


def at_lane(term, head):
    return jnp.where(iota((1, 128), 1) == head, term, 0.0)


def near_kernel(ids, sharp, q_ref, k_ref, v_ref, u_ref, bounds_ref, g1_ref, z0_ref, own_ref, back_ref, terms_ref):
    dev = ids[0]
    x, y, q, r = xyqr(dev)
    row = iota((128, 128), 0)
    here = doc_onehot(dev * 128 + row, bounds_ref)
    there = doc_onehot((dev ^ 1) * 128 + row, bounds_ref)
    inv = 1.0 / math.sqrt(D)
    refs = (q_ref, k_ref, v_ref, u_ref)
    total = jnp.zeros((1, 128), F32)
    for h in range(2):
        blocks = [[ref[:, h * D : (h + 1) * D]] for ref in refs]
        *res, term = attention(*blocks, [here], sharp[h] * inv)
        for t in range(4):
            z0_ref[t * 128 : (t + 1) * 128, h * D : (h + 1) * D] = res[t][0]
        total += at_lane(term, h)
    h = 2 + (r & 1)
    blocks = [[cols(ref, h), g1_ref[t * 128 : (t + 1) * 128]] for t, ref in enumerate(refs)]
    *res, term = attention(*blocks, [here, there], sharp[h] * inv)
    for t in range(4):
        own_ref[t * 128 : (t + 1) * 128] = res[t][0]
        back_ref[t * 128 : (t + 1) * 128] = res[t][1]
    terms_ref[...] = jnp.broadcast_to(total + at_lane(term, h), (8, 128))


def pieces(v):
    hi = v.astype(BF).astype(F32)
    mid = (v - hi).astype(BF).astype(F32)
    lo = v - hi - mid
    row = iota((16, 128), 0)
    return jnp.where(row == 0, hi, jnp.where(row == 1, mid, jnp.where(row == 2, lo, 0.0))).astype(BF)


def total_of(blocks):
    acc = blocks[0].astype(F32)
    for b in blocks[1:]:
        acc += b.astype(F32)
    return jnp.sum(acc, axis=0, keepdims=True)


def task_kernel(ids, sharp, in_ref, bounds_ref, terms_ref, out_ref):
    x, y, q, r = xyqr(ids[0])
    m = iota((128, 128), 0)
    j4, j5 = q, y & 1
    near, r3 = r < 2, r == 2
    far = r == 3
    q3 = q == 3
    u_m = jnp.where(near, q, jnp.where(r3, q ^ (m >> 6), m >> 5))
    y_m = jnp.where(far & (q == 2), y ^ ((m >> 4) & 1), jnp.where(far & q3, jnp.where(y < 2, (m >> 3) & 3, (m >> 2) & 3), y))
    x_m = jnp.where(far & q3 & (y >= 2), (m >> 4) & 1, x)
    level = jnp.where(near, 2, jnp.where(r3, 3, jnp.where(q < 2, 4, jnp.where(q == 2, 5, jnp.where(y < 2, 6, 7)))))
    j = jnp.where(near, r, jnp.where(r3, q & 1, jnp.where(q < 2, q, jnp.where(q == 2, y & 1, jnp.where(y < 2, y, x)))))
    sh = level - 2
    dil = jnp.left_shift(1, sh)
    offset = (5 + j * (dil >> 1)) & (dil - 1)
    i_m = m & (jnp.right_shift(128, sh) - 1)
    low = (x_m * 64 + y_m * 16 + u_m * 4) * 128 + i_m * dil + offset
    docs = [doc_onehot(low + s * 128, bounds_ref) for s in range(4)]
    head = level * 2 + j
    blocks = [[in_ref[s, t * 128 : (t + 1) * 128] for s in range(4)] for t in range(4)]
    *res, term = attention(*blocks, docs, sharp[head] * (1.0 / math.sqrt(D)))
    for s in range(4):
        for t in range(4):
            out_ref[s, t * 128 : (t + 1) * 128] = res[t][s]
    extra = pieces(terms_ref[0:1] + at_lane(term, head))
    for s in range(4):
        out_ref[s, 512:528] = extra


def from_r_kernel(in_ref, g3_ref, out_ref):
    for t in range(4):
        g3_ref[t * 64 : (t + 1) * 64] = in_ref[2, t * 128 + 64 : t * 128 + 128]
        for u in range(4):
            out_ref[u, t * 32 : (t + 1) * 32] = in_ref[3, t * 128 + u * 32 : t * 128 + u * 32 + 32]
    extra = pieces(total_of([in_ref[s, 512:528] for s in range(4)]))
    for u in range(4):
        out_ref[u, 128:144] = extra


def from_q_kernel(ids, in_ref, g5_ref, out_ref):
    x, y, q, r = xyqr(ids[0])
    for t in range(4):
        g5_ref[t * 16 : (t + 1) * 16] = in_ref[2, t * 32 + 16 : t * 32 + 32]
    want = xy_col(x, y, iota((256, 128), 1))
    perm = onehot(want == iota((256, 128), 0))
    rows = mm(perm, in_ref[3, 0:128]).astype(BF)
    extra = pieces(total_of([in_ref[s, 128:144] for s in range(4)]))
    for d in range(8):
        out_ref[d, 0:32] = rows[d * 32 : (d + 1) * 32]
        out_ref[d, 32:48] = extra


def sum_kernel(in_ref, out_ref):
    out_ref[...] = jnp.broadcast_to(total_of([in_ref[s, 32:48] for s in range(8)]), (8, 128))


def unpack_kernel(ids, z0_ref, own_ref, g1_ref, rr_ref, g3_ref, qr_ref, g5_ref, xy_ref, o_ref, dq_ref, dk_ref, dv_ref):
    x, y, q, r = xyqr(ids[0])

    def spread(level, j):
        n = 128 // DIL[level]
        return onehot(iota((128, n), 0) == iota((128, n), 1) * DIL[level] + off(level, j))

    def put(ref, head, value):
        ref[:, pl.ds(pl.multiple_of(head * D, D), D)] = value.astype(BF)

    j1, j3, j5 = r & 1, q & 1, y & 1
    w3, w3b = spread(3, j3), spread(3, 1 - j3)
    w40, w41 = spread(4, 0), spread(4, 1)
    w5, w5b = spread(5, j5), spread(5, 1 - j5)
    pi, ci = iota((128, 32), 0), iota((128, 32), 1)
    for t, ref in enumerate((o_ref, dq_ref, dk_ref, dv_ref)):
        lo = t * 128
        ref[:, : 2 * D] = z0_ref[lo : lo + 128]
        put(ref, 2 + j1, own_ref[lo : lo + 128])
        put(ref, 3 - j1, g1_ref[lo : lo + 128])
        ref[:, 4 * D : 5 * D] = rr_ref[0, lo : lo + 128]
        ref[:, 5 * D : 6 * D] = rr_ref[1, lo : lo + 128]
        put(ref, 6 + j3, mm(w3, rr_ref[2, lo : lo + 64]))
        put(ref, 7 - j3, mm(w3b, g3_ref[t * 64 : (t + 1) * 64]))
        put(ref, 8, mm(w40, qr_ref[0, t * 32 : (t + 1) * 32]))
        put(ref, 9, mm(w41, qr_ref[1, t * 32 : (t + 1) * 32]))
        put(ref, 10 + j5, mm(w5, qr_ref[2, t * 32 : t * 32 + 16]))
        put(ref, 11 - j5, mm(w5b, g5_ref[t * 16 : (t + 1) * 16]))
        for j in range(2):
            w6 = onehot(pi == (ci - t * 8) * 16 + off(6, j))
            w7 = onehot(pi == (ci - t * 4) * 32 + off(7, j))
            put(ref, 12 + j, mm(w6, xy_ref[x * 4 + j, 0:32]))
            put(ref, 14 + j, mm(w7, xy_ref[j * 4 + 2, 0:32]))


SMEM = pl.BlockSpec(memory_space=pltpu.SMEM)
VMEM = pl.BlockSpec(memory_space=pltpu.VMEM)


def heads(first, count):
    return pl.BlockSpec((128, count * D), lambda i: (0, first // count))


def whole(array):
    return pl.BlockSpec(array.shape, lambda i: (0,) * len(array.shape))


def call(kernel, outs, scalars, sliced, rest, name):
    shapes = [jax.ShapeDtypeStruct(s, d) for s, d in outs]
    single = len(shapes) == 1
    specs = [pl.BlockSpec(s.shape, lambda i, n=len(s.shape): (0,) * n) for s in shapes]
    return pl.pallas_call(
        kernel,
        grid=(1,),
        in_specs=[SMEM] * len(scalars) + [heads(f, c) for _, f, c in sliced] + [whole(a) for a in rest],
        out_specs=specs[0] if single else specs,
        out_shape=shapes[0] if single else shapes,
        name=name,
    )(*scalars, *[a for a, _, _ in sliced], *rest)


def xor_pairs(n, v):
    return [(i, i ^ v) for i in range(n)]


def body(asking_vectors, lookup_vectors, payload_vectors, incoming_sensitivity, learned_sharpness, reply_list_sizes):
    four = [a[0] for a in (asking_vectors, lookup_vectors, payload_vectors, incoming_sensitivity)]
    ids = lax.axis_index(SEQ).astype(jnp.int32).reshape(1)
    ends = jnp.cumsum(reply_list_sizes[0])
    n_docs = ends.shape[0]
    starts = jnp.concatenate([jnp.zeros((1,), jnp.int32), ends[:-1]])
    ends = jnp.concatenate([ends[:-1], jnp.full((1,), 1 << 30, jnp.int32)])
    bounds = jnp.pad(jnp.stack([starts, ends]), ((0, 6), (0, 128 - n_docs)))

    g1, g3, g5, xy = call(
        pack_kernel,
        [((512, D), BF), ((256, D), BF), ((64, D), BF), ((8, 32, D), BF)],
        [ids], [(a, 0, 16) for a in four], [], "pack",
    )
    g3 = lax.ppermute(g3, "q", xor_pairs(4, 1))
    g5 = lax.ppermute(g5, "y", xor_pairs(4, 1))
    g1 = lax.ppermute(g1, "r", xor_pairs(4, 1))
    xy = lax.all_to_all(xy, ("x", "y"), 0, 0)
    qs = call(to_q_kernel, [((4, 128, D), BF)], [ids], [(a, 8, 4) for a in four], [g5, xy], "to_q")
    qs = lax.all_to_all(qs, "q", 0, 0)
    rs = call(to_r_kernel, [((4, 512, D), BF)], [ids], [(a, 4, 4) for a in four], [g3, qs], "to_r")
    z0, own1, back1, terms = call(
        near_kernel,
        [((512, 2 * D), BF), ((512, D), BF), ((512, D), BF), ((8, 128), F32)],
        [ids, learned_sharpness], [(a, 0, 4) for a in four], [bounds, g1], "near",
    )
    back1 = lax.ppermute(back1, "r", xor_pairs(4, 1))
    rs = lax.all_to_all(rs, "r", 0, 0)
    rs = call(task_kernel, [((4, 528, D), BF)], [ids, learned_sharpness], [], [rs, bounds, terms], "task")
    rs = lax.all_to_all(rs, "r", 0, 0)
    back3, qs = call(from_r_kernel, [((256, D), BF), ((4, 144, D), BF)], [], [], [rs], "from_r")
    back3 = lax.ppermute(back3, "q", xor_pairs(4, 1))
    qs = lax.all_to_all(qs, "q", 0, 0)
    back5, xy = call(from_q_kernel, [((64, D), BF), ((8, 48, D), BF)], [ids], [], [qs], "from_q")
    back5 = lax.ppermute(back5, "y", xor_pairs(4, 1))
    xy = lax.all_to_all(xy, ("x", "y"), 0, 0)
    terms = call(sum_kernel, [((8, 128), F32)], [], [], [xy], "scale_sum")
    parts = [lax.ppermute(terms, "dp", xor_pairs(4, v)) for v in (1, 2, 3)]
    outs = call(
        unpack_kernel, [((128, 16 * D), BF)] * 4, [ids], [],
        [z0, own1, back1, rs, back3, qs, back5, xy], "unpack",
    )
    scale_gradient = ((terms + parts[0]) + (parts[1] + parts[2]))[0, :16]
    return (*[o[None] for o in outs], scale_gradient)


def solution(mesh):
    fine = Mesh(mesh.devices.reshape(2, 4, 4, 4, 4), SEQ + ("dp",))
    rows = P("dp", SEQ, None)
    in_specs = (rows, rows, rows, rows, P(), P("dp", None))
    out_specs = (rows, rows, rows, rows, P())
    return jax.shard_map(body, mesh=fine, in_specs=in_specs, out_specs=out_specs, check_vma=False)
```

time: 634 us -> 157 us (0.25); the launches traced: 626 us -> 156 us
  starting transfers between devices: 225 us -> 75.6 us
  local copies, waits for them, and re-layouts: 133 us -> 6.38 us
  blocking collectives: 111 us -> 19 us
  matrix products: 47.1 us -> 0 us
  other arithmetic: 29.4 us -> 0.28 us
  waiting for transfers between devices: 55.3 us -> 30 us
  Pallas kernels: 0 us -> 24 us
  between operations: 24.8 us -> 0.89 us
    ppermute x56 -> x9, starting transfers between devices: 225 us -> 37.2 us  [the longest x3 12.7 us: body(): parts = [lax.ppermute(terms, 'dp', xor_pairs(4, v)) for v in (1, 2, 3)]]
    psum x1 -> x0, blocking collectives: 111 us -> none  [body(): scale_gradient = lax.psum(jnp.stack(scale_terms), ('seq', 'dp'))]
    unnamed x331 -> x38, local copies, waits for them, and re-layouts: 54 us -> 5.26 us
    dot_general x96 -> x0, matrix products: 47.1 us -> none  [the longest x16 13.5 us: body(): lax.dot_general(up_sel, val_sel, (((1,), (1,)), ((), ())), preferred_elem...]
    all_to_all x0 -> x5, starting transfers between devices: none -> 38.4 us  [the longest x2 22 us: body(): qs = lax.all_to_all(qs, 'q', 0, 0)]
    ppermute x56 -> x9, waiting for transfers between devices: 55.3 us -> 17.6 us  [the longest x1 10.3 us: body(): g3 = lax.ppermute(g3, 'q', xor_pairs(4, 1))]
    slice x93 -> x1, local copies, waits for them, and re-layouts: 31.4 us -> 0.01 us  [body(): starts = jnp.concatenate([jnp.zeros((1,), jnp.int32), ends[:-1]])]
    concatenate x27 -> x0, local copies, waits for them, and re-layouts: 28.4 us -> none  [the longest x12 20.7 us: body(): jnp.concatenate([current, partner(current, 'seq', bit_num)], 0)]
  transfers between devices with their start and end apart: 56 -> 14, of which waited for: 11 -> 5; matrix products, arithmetic and copies ran while one was open for 29% -> 1% of each run, Pallas kernels for 0% -> 7%
where the time goes in v1:
time: 157 us; the launch traced here: 156 us
  starting transfers between devices  75.6 us (48%)
  waiting for transfers between devices  30 us (19%)
  Pallas kernels  24 us (15%)
  blocking collectives  19 us (12%)
  local copies, waits for them, and re-layouts  6.38 us (4%)
    pallas_call x9, Pallas kernels, call(): pl.pallas_call(kernel, grid=(1,), in_specs=[SMEM] * len(scalars) + [heads...  24 us
    all_to_all x2, starting transfers between devices, body(): qs = lax.all_to_all(qs, 'q', 0, 0)  22 us
    all_to_all x1, blocking collectives, body(): rs = lax.all_to_all(rs, 'r', 0, 0)  19 us
    all_to_all x2, starting transfers between devices, body(): xy = lax.all_to_all(xy, ('x', 'y'), 0, 0)  12.8 us
    ppermute x3, starting transfers between devices, body(): parts = [lax.ppermute(terms, 'dp', xor_pairs(4, v)) for v in (1, 2, 3)]  12.7 us
    ppermute x1, waiting for transfers between devices, body(): g3 = lax.ppermute(g3, 'q', xor_pairs(4, 1))  10.3 us
    all_to_all x2, waiting for transfers between devices, body(): qs = lax.all_to_all(qs, 'q', 0, 0)  10.1 us
    ppermute x1, starting transfers between devices, body(): g3 = lax.ppermute(g3, 'q', xor_pairs(4, 1))  7.27 us
  transfers between devices with their start and end apart: 14, of which 5 were waited for; matrix products, arithmetic and copies ran while one was open for 1% of the time, Pallas kernels for 7%

profile of v1, /device:TPU:1, one launch (start us, length us, event | category | flops | bytes accessed | tf_op | source)
XLA Modules:
  0.0 156.1 jit_solution(7447894727871318042)
XLA Ops:
  0.6 2.5 %pack.1 = (bf16[512,128]{1,0:T(8,128)(2,1)}, bf16[256,128]{1,0:T(8,128)(2,1)}, bf16[64,128]{1,0:T(8,128)(2,1)}, bf16[8,32,128]{2,1,0:T(8,128)(2,1)}) custom-call(s32[1]{0:T(128)} %bitcast.ids, bf16[128,2048]{1,0:T(8,128)(2,1)} %bitcast.18, bf16[128,2048]{1,0:T(8,128)(2,1)} %bitcast.22, bf16[128,2048]{1,0:T(8,128)(2,1)} %bitcast.26, bf16[128,2048]{1,0:T(8,128)(2,1)} %bitcast.30), custom_call_target="tpu_custom_call" | custom-call | tf_op jit(solution)/shard_map/pack/pallas_call | solution.py:296
  3.1 7.6 %all-to-all-start = ((bf16[8,32,128]{2,1,0:T(8,128)(2,1)}), bf16[8,32,128]{2,1,0:T(8,128)(2,1)S(1)}, u32[]{:S(2)}, u32[]{:S(2)}) async-start(bf16[8,32,128]{2,1,0:T(8,128)(2,1)} %get-tuple-element.27), calls=%async_computation | async-start | bytes 131072 | tf_op jit(solution)/shard_map/all_to_all | solution.py:327
  10.7 0.0 copy-done.17
  10.7 3.4 %collective-permute-start.3 = (bf16[64,128]{1,0:T(8,128)(2,1)S(1)}, bf16[64,128]{1,0:T(8,128)(2,1)S(1)}, u32[]{:S(2)}, u32[]{:S(2)}) collective-permute-start(bf16[64,128]{1,0:T(8,128)(2,1)S(1)} %copy-done.17), channel_id=1, source_target_pairs={{0,64},{64,0},{128,192},{192,128},{1,65},{65,1},{129,193},{193,129... | collective-permute-start | bytes 49160 | tf_op jit(solution)/shard_map/ppermute | solution.py:325
  14.1 1.1 collective-permute-done.3.g5_ref
  15.2 2.2 %all-to-all-done.xy_ref = bf16[8,32,128]{2,1,0:T(8,128)(2,1)S(1)} async-done(((bf16[8,32,128]{2,1,0:T(8,128)(2,1)}), bf16[8,32,128]{2,1,0:T(8,128)(2,1)S(1)}, u32[]{:S(2)}, u32[]{:S(2)}) %all-to-all-start) | async-done | bytes 65568 | tf_op jit(solution)/shard_map/all_to_all | solution.py:327
  17.4 0.0 copy-done.10
  17.4 0.6 copy-done.4
  18.1 2.0 %to_q.1 = bf16[4,128,128]{2,1,0:T(8,128)(2,1)} custom-call(s32[1]{0:T(128)} %bitcast.ids, bf16[128,2048]{1,0:T(8,128)(2,1)} %bitcast.19, bf16[128,2048]{1,0:T(8,128)(2,1)} %bitcast.23, bf16[128,2048]{1,0:T(8,128)(2,1)} %bitcast.27, bf16[128,2048]{1,0:T(8,128)(2,1)} %bitcast.31, bf16[64,128]{1,0:T(8,128)(2,1)} %copy-done.10, bf16[8,32,128]{2,1,0:T(8,128)(2,1)} %copy-done.4), custom_call_target="tpu_custom_call" | custom-call | tf_op jit(solution)/shard_map/to_q/pallas_call | solution.py:296
  20.1 14.9 %all-to-all-start.1 = ((bf16[4,128,128]{2,1,0:T(8,128)(2,1)}), bf16[4,128,128]{2,1,0:T(8,128)(2,1)S(1)}, u32[]{:S(2)}, u32[]{:S(2)}) async-start(bf16[4,128,128]{2,1,0:T(8,128)(2,1)} %to_q.1), calls=%async_computation.1 | async-start | bytes 262144 | tf_op jit(solution)/shard_map/all_to_all | solution.py:329
  35.0 0.0 copy-done.15
  35.0 7.3 %collective-permute-start.2 = (bf16[256,128]{1,0:T(8,128)(2,1)S(1)}, bf16[256,128]{1,0:T(8,128)(2,1)S(1)}, u32[]{:S(2)}, u32[]{:S(2)}) collective-permute-start(bf16[256,128]{1,0:T(8,128)(2,1)S(1)} %copy-done.15), channel_id=1, source_target_pairs={{0,16},{16,0},{32,48},{48,32},{1,17},{17,1},{33,49},{49,33},{2,18}... | collective-permute-start | bytes 196616 | tf_op jit(solution)/shard_map/ppermute | solution.py:324
  42.3 10.3 %collective-permute-done.2.g3_ref = bf16[256,128]{1,0:T(8,128)(2,1)S(1)} collective-permute-done((bf16[256,128]{1,0:T(8,128)(2,1)S(1)}, bf16[256,128]{1,0:T(8,128)(2,1)S(1)}, u32[]{:S(2)}, u32[]{:S(2)}) %collective-permute-start.2) | collective-permute-done | bytes 65568 | tf_op jit(solution)/shard_map/ppermute | solution.py:324
  52.6 0.0 all-to-all-done.1.qr_ref
  52.6 0.6 copy-done.8
  53.2 0.7 copy-done.3
  53.9 2.2 %to_r.1 = bf16[4,512,128]{2,1,0:T(8,128)(2,1)} custom-call(s32[1]{0:T(128)} %bitcast.ids, bf16[128,2048]{1,0:T(8,128)(2,1)} %bitcast.20, bf16[128,2048]{1,0:T(8,128)(2,1)} %bitcast.24, bf16[128,2048]{1,0:T(8,128)(2,1)} %bitcast.28, bf16[128,2048]{1,0:T(8,128)(2,1)} %bitcast.32, bf16[256,128]{1,0:T(8,128)(2,1)} %copy-done.8, bf16[4,128,128]{2,1,0:T(8,128)(2,1)} %copy-done.3), custom_call_target="tpu_custom_call" | custom-call | tf_op jit(solution)/shard_map/to_r/pallas_call | solution.py:296
  56.0 3.6 %all-to-all-start.2 = ((bf16[4,512,128]{2,1,0:T(8,128)(2,1)}), bf16[4,512,128]{2,1,0:T(8,128)(2,1)S(1)}, u32[]{:S(2)}, u32[]{:S(2)}) async-start(bf16[4,512,128]{2,1,0:T(8,128)(2,1)} %to_r.1), calls=%async_computation.2 | async-start | bytes 1048576 | tf_op jit(solution)/shard_map/all_to_all | solution.py:337
  59.6 0.0 copy-done.12
  59.6 0.0 copy-start.18
  59.6 3.4 %collective-permute-start = (bf16[512,128]{1,0:T(8,128)(2,1)S(1)}, bf16[512,128]{1,0:T(8,128)(2,1)S(1)}, u32[]{:S(2)}, u32[]{:S(2)}) collective-permute-start(bf16[512,128]{1,0:T(8,128)(2,1)S(1)} %copy-done.12), channel_id=1, source_target_pairs={{0,4},{4,0},{8,12},{12,8},{1,5},{5,1},{9,13},{13,9},{2,6},{6,2},{1... | collective-permute-start | bytes 393224 | tf_op jit(solution)/shard_map/ppermute | solution.py:326
  63.1 0.0 copy-done.18
  63.1 0.2 reduce-window.4
  63.3 0.1 add_bitcast_fusion
  63.4 0.6 pad.4.bounds_ref
  64.0 6.2 %collective-permute-done.g1_ref = bf16[512,128]{1,0:T(8,128)(2,1)S(1)} collective-permute-done((bf16[512,128]{1,0:T(8,128)(2,1)S(1)}, bf16[512,128]{1,0:T(8,128)(2,1)S(1)}, u32[]{:S(2)}, u32[]{:S(2)}) %collective-permute-start) | collective-permute-done | bytes 131104 | tf_op jit(solution)/shard_map/ppermute | solution.py:326
  70.2 0.7 copy-done.6
  70.9 4.4 %near.1 = (bf16[512,256]{1,0:T(8,128)(2,1)}, bf16[512,128]{1,0:T(8,128)(2,1)}, bf16[512,128]{1,0:T(8,128)(2,1)}, f32[8,128]{1,0:T(8,128)}) custom-call(s32[1]{0:T(128)} %bitcast.ids, f32[16]{0:T(128)} %sharp.3, bf16[128,2048]{1,0:T(8,128)(2,1)} %bitcast.21, bf16[128,2048]{1,0:T(8,128)(2,1)} %bitcast.25, bf16[128,2048]{1,0:T(8,128)(2,1)} %bitcast.29, ...), custom_call_target="tpu_custom_call" | custom-call | tf_op jit(solution)/shard_map/near/pallas_call | solution.py:296
  75.2 0.0 all-to-all-done.2.in_ref
  75.3 0.8 copy-done
  76.0 4.9 %task.1 = bf16[4,528,128]{2,1,0:T(8,128)(2,1)} custom-call(s32[1]{0:T(128)} %bitcast.ids, f32[16]{0:T(128)} %sharp.3, bf16[4,512,128]{2,1,0:T(8,128)(2,1)} %copy-done, s32[8,128]{1,0:T(8,128)} %pad.4.bounds_ref, f32[8,128]{1,0:T(8,128)} %get-tuple-element.28.terms_ref), custom_call_target="tpu_custom_call" | custom-call | tf_op jit(solution)/shard_map/task/pallas_call | solution.py:296
  80.9 19.0 %all_to_all.30.in_ref.rr_ref = bf16[4,528,128]{2,1,0:T(8,128)(2,1)} all-to-all(bf16[4,528,128]{2,1,0:T(8,128)(2,1)} %task.1), channel_id=1, replica_groups=mesh['x'=2,'y'=4,'q'=4,'r'=4,'dp'=4] {'r'}, dimensions={0} | all-to-all | bytes 1081344 | tf_op jit(solution)/shard_map/all_to_all | solution.py:339
  99.9 1.7 %from_r.1 = (bf16[256,128]{1,0:T(8,128)(2,1)}, bf16[4,144,128]{2,1,0:T(8,128)(2,1)}) custom-call(bf16[4,528,128]{2,1,0:T(8,128)(2,1)} %all_to_all.30.in_ref.rr_ref), custom_call_target="tpu_custom_call" | custom-call | tf_op jit(solution)/shard_map/from_r/pallas_call | solution.py:296
  101.7 7.1 %all-to-all-start.4 = ((bf16[4,144,128]{2,1,0:T(8,128)(2,1)}), bf16[4,144,128]{2,1,0:T(8,128)(2,1)S(1)}, u32[]{:S(2)}, u32[]{:S(2)}) async-start(bf16[4,144,128]{2,1,0:T(8,128)(2,1)} %get-tuple-element.30), calls=%async_computation.4 | async-start | bytes 294912 | tf_op jit(solution)/shard_map/all_to_all | solution.py:342
  108.8 0.0 copy-done.13
  108.8 2.1 %collective-permute-start.1 = (bf16[512,128]{1,0:T(8,128)(2,1)S(1)}, bf16[512,128]{1,0:T(8,128)(2,1)S(1)}, u32[]{:S(2)}, u32[]{:S(2)}) collective-permute-start(bf16[512,128]{1,0:T(8,128)(2,1)S(1)} %copy-done.13), channel_id=1, source_target_pairs={{0,4},{4,0},{8,12},{12,8},{1,5},{5,1},{9,13},{13,9},{2,6},{6,2},{1... | collective-permute-start | bytes 393224 | tf_op jit(solution)/shard_map/ppermute | solution.py:336
  110.9 10.1 %all-to-all-done.4.in_ref.qr_ref = bf16[4,144,128]{2,1,0:T(8,128)(2,1)S(1)} async-done(((bf16[4,144,128]{2,1,0:T(8,128)(2,1)}), bf16[4,144,128]{2,1,0:T(8,128)(2,1)S(1)}, u32[]{:S(2)}, u32[]{:S(2)}) %all-to-all-start.4) | async-done | bytes 147488 | tf_op jit(solution)/shard_map/all_to_all | solution.py:342
  121.0 0.7 copy-done.1
  121.7 1.7 %from_q.1 = (bf16[64,128]{1,0:T(8,128)(2,1)}, bf16[8,48,128]{2,1,0:T(8,128)(2,1)}) custom-call(s32[1]{0:T(128)} %bitcast.ids, bf16[4,144,128]{2,1,0:T(8,128)(2,1)} %copy-done.1), custom_call_target="tpu_custom_call" | custom-call | tf_op jit(solution)/shard_map/from_q/pallas_call | solution.py:296
  123.4 5.2 %all-to-all-start.5 = ((bf16[8,48,128]{2,1,0:T(8,128)(2,1)}), bf16[8,48,128]{2,1,0:T(8,128)(2,1)S(1)}, u32[]{:S(2)}, u32[]{:S(2)}) async-start(bf16[8,48,128]{2,1,0:T(8,128)(2,1)} %get-tuple-element.32), calls=%async_computation.5 | async-start | bytes 196608 | tf_op jit(solution)/shard_map/all_to_all | solution.py:345
  128.6 0.0 copy-done.14
  128.6 4.9 %collective-permute-start.4 = (bf16[256,128]{1,0:T(8,128)(2,1)S(1)}, bf16[256,128]{1,0:T(8,128)(2,1)S(1)}, u32[]{:S(2)}, u32[]{:S(2)}) collective-permute-start(bf16[256,128]{1,0:T(8,128)(2,1)S(1)} %copy-done.14), channel_id=1, source_target_pairs={{0,16},{16,0},{32,48},{48,32},{1,17},{17,1},{33,49},{49,33},{2,18}... | collective-permute-start | bytes 196616 | tf_op jit(solution)/shard_map/ppermute | solution.py:341
  133.5 0.0 copy-done.16
  133.5 3.4 %collective-permute-start.5 = (bf16[64,128]{1,0:T(8,128)(2,1)S(1)}, bf16[64,128]{1,0:T(8,128)(2,1)S(1)}, u32[]{:S(2)}, u32[]{:S(2)}) collective-permute-start(bf16[64,128]{1,0:T(8,128)(2,1)S(1)} %copy-done.16), channel_id=1, source_target_pairs={{0,64},{64,0},{128,192},{192,128},{1,65},{65,1},{129,193},{193,129... | collective-permute-start | bytes 49160 | tf_op jit(solution)/shard_map/ppermute | solution.py:344
  136.9 0.0 all-to-all-done.5.xy_ref.in_ref
  136.9 0.0 copy-start.2
  136.9 0.6 copy-done.2
  137.5 1.5 scale_sum.1
  139.0 2.2 %collective-permute-start.7 = (f32[8,128]{1,0:T(8,128)}, f32[8,128]{1,0:T(8,128)S(1)}, u32[]{:S(2)}, u32[]{:S(2)}) collective-permute-start(f32[8,128]{1,0:T(8,128)} %scale_sum.1), channel_id=1, source_target_pairs={{0,2},{1,3},{2,0},{3,1},{4,6},{5,7},{6,4},{7,5},{8,10},{9,11},{10,... | collective-permute-start | bytes 12296 | tf_op jit(solution)/shard_map/ppermute | solution.py:347
  141.2 8.6 %collective-permute-start.8 = (f32[8,128]{1,0:T(8,128)}, f32[8,128]{1,0:T(8,128)S(1)}, u32[]{:S(2)}, u32[]{:S(2)}) collective-permute-start(f32[8,128]{1,0:T(8,128)} %scale_sum.1), channel_id=1, source_target_pairs={{0,3},{1,2},{2,1},{3,0},{4,7},{5,6},{6,5},{7,4},{8,11},{9,10},{10,... | collective-permute-start | bytes 12296 | tf_op jit(solution)/shard_map/ppermute | solution.py:347
  149.8 0.0 collective-permute-done.1.g1_ref
  149.9 0.0 copy-start.5
  149.9 1.9 %collective-permute-start.6 = (f32[8,128]{1,0:T(8,128)}, f32[8,128]{1,0:T(8,128)S(1)}, u32[]{:S(2)}, u32[]{:S(2)}) collective-permute-start(f32[8,128]{1,0:T(8,128)} %scale_sum.1), channel_id=1, source_target_pairs={{0,1},{1,0},{2,3},{3,2},{4,5},{5,4},{6,7},{7,6},{8,9},{9,8},{10,11... | collective-permute-start | bytes 12296 | tf_op jit(solution)/shard_map/ppermute | solution.py:347
  151.8 0.0 collective-permute-done.4.g3_ref
  151.8 0.0 copy-start.7
  151.8 0.0 collective-permute-done.5.g5_ref
  151.8 0.6 copy-done.7
  152.4 0.0 copy-done.9
  152.4 3.1 %unpack.1 = (bf16[128,2048]{1,0:T(8,128)(2,1)}, bf16[128,2048]{1,0:T(8,128)(2,1)}, bf16[128,2048]{1,0:T(8,128)(2,1)}, bf16[128,2048]{1,0:T(8,128)(2,1)}) custom-call(s32[1]{0:T(128)} %bitcast.ids, bf16[512,256]{1,0:T(8,128)(2,1)} %get-tuple-element.22.z0_ref, bf16[512,128]{1,0:T(8,128)(2,1)} %get-tuple-element.23.own_ref, bf16[512,128]{1,0:T(8,128)(2,1)} %copy-done.5, ...), custom_call_target="tpu_custom_call" | custom-call | tf_op jit(solution)/shard_map/unpack/pallas_call | solution.py:296
  155.5 0.0 collective-permute-done.7
  155.5 0.0 collective-permute-done.8
  155.5 0.0 collective-permute-done.6
  155.5 0.0 copy-done.11
  155.6 0.5 slice_bitcast_fusion
  (19 shorter events, 0.1 us)
Async XLA Ops:
  3.1 7.6 %copy-start.17 = (bf16[64,128]{1,0:T(8,128)(2,1)S(1)}, bf16[64,128]{1,0:T(8,128)(2,1)}, u32[]{:S(2)}) copy-start(bf16[64,128]{1,0:T(8,128)(2,1)} %get-tuple-element.26) | copy-start | bytes 49156
  3.1 14.3 %all-to-all-start = ((bf16[8,32,128]{2,1,0:T(8,128)(2,1)}), bf16[8,32,128]{2,1,0:T(8,128)(2,1)S(1)}, u32[]{:S(2)}, u32[]{:S(2)}) async-start(bf16[8,32,128]{2,1,0:T(8,128)(2,1)} %get-tuple-element.27), calls=%async_computation | async-start | bytes 131072 | tf_op jit(solution)/shard_map/all_to_all | solution.py:327
  10.7 4.5 %collective-permute-start.3 = (bf16[64,128]{1,0:T(8,128)(2,1)S(1)}, bf16[64,128]{1,0:T(8,128)(2,1)S(1)}, u32[]{:S(2)}, u32[]{:S(2)}) collective-permute-start(bf16[64,128]{1,0:T(8,128)(2,1)S(1)} %copy-done.17), channel_id=1, source_target_pairs={{0,64},{64,0},{128,192},{192,128},{1,65},{65,1},{129,193},{193,129... | collective-permute-start | bytes 49160 | tf_op jit(solution)/shard_map/ppermute | solution.py:325
  15.2 2.2 %copy-start.10 = (bf16[64,128]{1,0:T(8,128)(2,1)}, bf16[64,128]{1,0:T(8,128)(2,1)S(1)}, u32[]{:S(2)}) copy-start(bf16[64,128]{1,0:T(8,128)(2,1)S(1)} %collective-permute-done.3.g5_ref) | copy-start | bytes 49156
  17.4 0.6 copy-start.4
  20.1 14.9 %copy-start.15 = (bf16[256,128]{1,0:T(8,128)(2,1)S(1)}, bf16[256,128]{1,0:T(8,128)(2,1)}, u32[]{:S(2)}) copy-start(bf16[256,128]{1,0:T(8,128)(2,1)} %get-tuple-element.25) | copy-start | bytes 196612
  20.1 32.5 %all-to-all-start.1 = ((bf16[4,128,128]{2,1,0:T(8,128)(2,1)}), bf16[4,128,128]{2,1,0:T(8,128)(2,1)S(1)}, u32[]{:S(2)}, u32[]{:S(2)}) async-start(bf16[4,128,128]{2,1,0:T(8,128)(2,1)} %to_q.1), calls=%async_computation.1 | async-start | bytes 262144 | tf_op jit(solution)/shard_map/all_to_all | solution.py:329
  35.0 17.6 %collective-permute-start.2 = (bf16[256,128]{1,0:T(8,128)(2,1)S(1)}, bf16[256,128]{1,0:T(8,128)(2,1)S(1)}, u32[]{:S(2)}, u32[]{:S(2)}) collective-permute-start(bf16[256,128]{1,0:T(8,128)(2,1)S(1)} %copy-done.15), channel_id=1, source_target_pairs={{0,16},{16,0},{32,48},{48,32},{1,17},{17,1},{33,49},{49,33},{2,18}... | collective-permute-start | bytes 196616 | tf_op jit(solution)/shard_map/ppermute | solution.py:324
  52.6 0.6 copy-start.8
  53.2 0.7 copy-start.3
  56.0 3.6 %copy-start.12 = (bf16[512,128]{1,0:T(8,128)(2,1)S(1)}, bf16[512,128]{1,0:T(8,128)(2,1)}, u32[]{:S(2)}) copy-start(bf16[512,128]{1,0:T(8,128)(2,1)} %get-tuple-element.21) | copy-start | bytes 393220
  56.0 19.2 %all-to-all-start.2 = ((bf16[4,512,128]{2,1,0:T(8,128)(2,1)}), bf16[4,512,128]{2,1,0:T(8,128)(2,1)S(1)}, u32[]{:S(2)}, u32[]{:S(2)}) async-start(bf16[4,512,128]{2,1,0:T(8,128)(2,1)} %to_r.1), calls=%async_computation.2 | async-start | bytes 1048576 | tf_op jit(solution)/shard_map/all_to_all | solution.py:337
  59.6 3.5 %copy-start.18 = (s32[1,8]{1,0:T(1,128)S(1)}, s32[1,8]{1,0:T(1,128)}, u32[]{:S(2)}) copy-start(s32[1,8]{1,0:T(1,128)} %param.11) | copy-start | bytes 100
  59.6 10.6 %collective-permute-start = (bf16[512,128]{1,0:T(8,128)(2,1)S(1)}, bf16[512,128]{1,0:T(8,128)(2,1)S(1)}, u32[]{:S(2)}, u32[]{:S(2)}) collective-permute-start(bf16[512,128]{1,0:T(8,128)(2,1)S(1)} %copy-done.12), channel_id=1, source_target_pairs={{0,4},{4,0},{8,12},{12,8},{1,5},{5,1},{9,13},{13,9},{2,6},{6,2},{1... | collective-permute-start | bytes 393224 | tf_op jit(solution)/shard_map/ppermute | solution.py:326
  70.2 0.7 copy-start.6
  75.2 0.8 copy-start
  101.7 7.1 %copy-start.13 = (bf16[512,128]{1,0:T(8,128)(2,1)S(1)}, bf16[512,128]{1,0:T(8,128)(2,1)}, u32[]{:S(2)}) copy-start(bf16[512,128]{1,0:T(8,128)(2,1)} %get-tuple-element.24) | copy-start | bytes 393220
  101.7 19.3 %all-to-all-start.4 = ((bf16[4,144,128]{2,1,0:T(8,128)(2,1)}), bf16[4,144,128]{2,1,0:T(8,128)(2,1)S(1)}, u32[]{:S(2)}, u32[]{:S(2)}) async-start(bf16[4,144,128]{2,1,0:T(8,128)(2,1)} %get-tuple-element.30), calls=%async_computation.4 | async-start | bytes 294912 | tf_op jit(solution)/shard_map/all_to_all | solution.py:342
  108.8 41.1 %collective-permute-start.1 = (bf16[512,128]{1,0:T(8,128)(2,1)S(1)}, bf16[512,128]{1,0:T(8,128)(2,1)S(1)}, u32[]{:S(2)}, u32[]{:S(2)}) collective-permute-start(bf16[512,128]{1,0:T(8,128)(2,1)S(1)} %copy-done.13), channel_id=1, source_target_pairs={{0,4},{4,0},{8,12},{12,8},{1,5},{5,1},{9,13},{13,9},{2,6},{6,2},{1... | collective-permute-start | bytes 393224 | tf_op jit(solution)/shard_map/ppermute | solution.py:336
  121.0 0.7 copy-start.1
  123.4 5.2 %copy-start.14 = (bf16[256,128]{1,0:T(8,128)(2,1)S(1)}, bf16[256,128]{1,0:T(8,128)(2,1)}, u32[]{:S(2)}) copy-start(bf16[256,128]{1,0:T(8,128)(2,1)} %get-tuple-element.29) | copy-start | bytes 196612
  123.4 10.1 %copy-start.16 = (bf16[64,128]{1,0:T(8,128)(2,1)S(1)}, bf16[64,128]{1,0:T(8,128)(2,1)}, u32[]{:S(2)}) copy-start(bf16[64,128]{1,0:T(8,128)(2,1)} %get-tuple-element.31) | copy-start | bytes 49156
  123.4 13.5 %all-to-all-start.5 = ((bf16[8,48,128]{2,1,0:T(8,128)(2,1)}), bf16[8,48,128]{2,1,0:T(8,128)(2,1)S(1)}, u32[]{:S(2)}, u32[]{:S(2)}) async-start(bf16[8,48,128]{2,1,0:T(8,128)(2,1)} %get-tuple-element.32), calls=%async_computation.5 | async-start | bytes 196608 | tf_op jit(solution)/shard_map/all_to_all | solution.py:345
  128.6 23.2 %collective-permute-start.4 = (bf16[256,128]{1,0:T(8,128)(2,1)S(1)}, bf16[256,128]{1,0:T(8,128)(2,1)S(1)}, u32[]{:S(2)}, u32[]{:S(2)}) collective-permute-start(bf16[256,128]{1,0:T(8,128)(2,1)S(1)} %copy-done.14), channel_id=1, source_target_pairs={{0,16},{16,0},{32,48},{48,32},{1,17},{17,1},{33,49},{49,33},{2,18}... | collective-permute-start | bytes 196616 | tf_op jit(solution)/shard_map/ppermute | solution.py:341
  133.5 18.3 %collective-permute-start.5 = (bf16[64,128]{1,0:T(8,128)(2,1)S(1)}, bf16[64,128]{1,0:T(8,128)(2,1)S(1)}, u32[]{:S(2)}, u32[]{:S(2)}) collective-permute-start(bf16[64,128]{1,0:T(8,128)(2,1)S(1)} %copy-done.16), channel_id=1, source_target_pairs={{0,64},{64,0},{128,192},{192,128},{1,65},{65,1},{129,193},{193,129... | collective-permute-start | bytes 49160 | tf_op jit(solution)/shard_map/ppermute | solution.py:344
  136.9 0.6 copy-start.2
  139.0 16.5 %collective-permute-start.7 = (f32[8,128]{1,0:T(8,128)}, f32[8,128]{1,0:T(8,128)S(1)}, u32[]{:S(2)}, u32[]{:S(2)}) collective-permute-start(f32[8,128]{1,0:T(8,128)} %scale_sum.1), channel_id=1, source_target_pairs={{0,2},{1,3},{2,0},{3,1},{4,6},{5,7},{6,4},{7,5},{8,10},{9,11},{10,... | collective-permute-start | bytes 12296 | tf_op jit(solution)/shard_map/ppermute | solution.py:347
  141.2 14.3 %collective-permute-start.8 = (f32[8,128]{1,0:T(8,128)}, f32[8,128]{1,0:T(8,128)S(1)}, u32[]{:S(2)}, u32[]{:S(2)}) collective-permute-start(f32[8,128]{1,0:T(8,128)} %scale_sum.1), channel_id=1, source_target_pairs={{0,3},{1,2},{2,1},{3,0},{4,7},{5,6},{6,5},{7,4},{8,11},{9,10},{10,... | collective-permute-start | bytes 12296 | tf_op jit(solution)/shard_map/ppermute | solution.py:347
  149.9 2.0 %copy-start.5 = (bf16[512,128]{1,0:T(8,128)(2,1)}, bf16[512,128]{1,0:T(8,128)(2,1)S(1)}, u32[]{:S(2)}) copy-start(bf16[512,128]{1,0:T(8,128)(2,1)S(1)} %collective-permute-done.1.g1_ref) | copy-start | bytes 393220
  149.9 5.7 %collective-permute-start.6 = (f32[8,128]{1,0:T(8,128)}, f32[8,128]{1,0:T(8,128)S(1)}, u32[]{:S(2)}, u32[]{:S(2)}) collective-permute-start(f32[8,128]{1,0:T(8,128)} %scale_sum.1), channel_id=1, source_target_pairs={{0,1},{1,0},{2,3},{3,2},{4,5},{5,4},{6,7},{7,6},{8,9},{9,8},{10,11... | collective-permute-start | bytes 12296 | tf_op jit(solution)/shard_map/ppermute | solution.py:347
  151.8 0.6 copy-start.7
  151.8 0.6 copy-start.9
  152.4 3.1 %copy-start.11 = (f32[8,128]{1,0:T(8,128)S(1)}, f32[8,128]{1,0:T(8,128)}, u32[]{:S(2)}) copy-start(f32[8,128]{1,0:T(8,128)} %scale_sum.1) | copy-start | bytes 12292

commit v2 on v1

v2 whole, which is shorter than its diff:
```python
import math

import jax
import jax.numpy as jnp
from jax import lax
from jax.experimental import pallas as pl
from jax.experimental.pallas import tpu as pltpu
from jax.sharding import Mesh, PartitionSpec as P

D = 128
BF = jnp.bfloat16
F32 = jnp.float32
DIL = (1, 1, 1, 2, 4, 8, 16, 32)
SEQ = ("x", "y", "q", "r")


def off(level, j):
    dil = DIL[level]
    return (5 + j * (dil // 2)) % dil


def iota(shape, dim):
    return lax.broadcasted_iota(jnp.int32, shape, dim)


def onehot(cond):
    return cond.astype(F32).astype(BF)


def mm(a, b):
    return jnp.dot(a, b, preferred_element_type=F32)


def mm_nt(a, b):
    return lax.dot_general(a, b, (((1,), (1,)), ((), ())), preferred_element_type=F32)


def mm_tn(a, b):
    return lax.dot_general(a, b, (((0,), (0,)), ((), ())), preferred_element_type=F32)


def pick(level, j, rows=128):
    n = 128 // DIL[level]
    return onehot(iota((n, 128), 1) == iota((n, 128), 0) * DIL[level] + off(level, j))


def cols(ref, head, first=0):
    return ref[:, pl.ds(pl.multiple_of((head - first) * D, D), D)]


def xyqr(dev):
    return dev >> 6, (dev >> 4) & 3, (dev >> 2) & 3, dev & 3


def xy_col(x, y, row):
    t, m = row >> 5, row & 31
    six = (x * 4 + (m >> 3)) * 32 + t * 8 + (m & 7)
    seven = (m >> 2) * 32 + t * 4 + (m & 3)
    return jnp.where(y < 2, six, jnp.where(y == 2, seven, -1))


def pack_kernel(ids, q_ref, k_ref, v_ref, u_ref, xy_ref):
    x, y, q, r = xyqr(ids[0])
    srcs = (q_ref, k_ref, v_ref, u_ref)
    j5 = 1 - (y & 1)
    s5 = pick(5, j5)
    xy_ref[...] = jnp.zeros(xy_ref.shape, BF)
    for t, ref in enumerate(srcs):
        xy_ref[x * 4 + (y ^ 1), 32 + t * 16 : 48 + t * 16] = mm(s5, cols(ref, 2 + j5)).astype(BF)
    for j in range(2):
        acc6 = jnp.zeros((32, D), F32)
        acc7 = jnp.zeros((32, D), F32)
        ri, ci = iota((32, 128), 0), iota((32, 128), 1)
        for t, ref in enumerate(srcs):
            w6 = onehot((ci == (ri - t * 8) * 16 + off(6, j)))
            w7 = onehot((ci == (ri - t * 4) * 32 + off(7, j)))
            acc6 += mm(w6, ref[:, (4 + j) * D : (5 + j) * D])
            acc7 += mm(w7, ref[:, (6 + j) * D : (7 + j) * D])
        xy_ref[x * 4 + j, 0:32] = acc6.astype(BF)
        xy_ref[j * 4 + 2, 0:32] = acc7.astype(BF)


def pairs_kernel(ids, q_ref, k_ref, v_ref, u_ref, g3_ref):
    x, y, q, r = xyqr(ids[0])
    j3 = 1 - (q & 1)
    s3 = pick(3, j3)
    for t, ref in enumerate((q_ref, k_ref, v_ref, u_ref)):
        g3_ref[t * 64 : (t + 1) * 64] = mm(s3, cols(ref, 6 + j3)).astype(BF)


def to_q_kernel(ids, q_ref, k_ref, v_ref, u_ref, xy_ref, own_ref, s1_ref, s2_ref, s3_ref, tmp):
    x, y, q, r = xyqr(ids[0])
    j5 = y & 1
    s40, s41, s5 = pick(4, 0), pick(4, 1), pick(5, j5)
    for t, ref in enumerate((q_ref, k_ref, v_ref, u_ref)):
        tmp[0, t * 32 : (t + 1) * 32] = mm(s40, ref[:, 8 * D : 9 * D]).astype(BF)
        tmp[1, t * 32 : (t + 1) * 32] = mm(s41, ref[:, 9 * D : 10 * D]).astype(BF)
        tmp[2, t * 32 : t * 32 + 16] = mm(s5, cols(ref, 10 + j5)).astype(BF)
        tmp[2, t * 32 + 16 : t * 32 + 32] = xy_ref[x * 4 + (y ^ 1), 32 + t * 16 : 48 + t * 16]
    want = xy_col(x, y, iota((128, 256), 0))
    perm = onehot(want == iota((128, 256), 1))
    tmp[3] = mm(perm, xy_ref[:, 0:32].reshape(256, D)).astype(BF)
    for v, ref in enumerate((own_ref, s1_ref, s2_ref, s3_ref)):
        ref[...] = tmp[q ^ v]


def to_r_kernel(ids, q_ref, k_ref, v_ref, u_ref, g3_ref, q0, q1, q2, q3, own_ref, t1_ref, t2_ref, t3_ref, tmp):
    x, y, q, r = xyqr(ids[0])
    j3 = q & 1
    h1 = 3 - (r & 1)
    s3 = pick(3, j3)
    for t, ref in enumerate((q_ref, k_ref, v_ref, u_ref)):
        lo = t * 128
        tmp[0, lo : lo + 128] = ref[:, 4 * D : 5 * D]
        tmp[1, lo : lo + 128] = ref[:, 5 * D : 6 * D]
        tmp[2, lo : lo + 64] = mm(s3, cols(ref, 6 + j3)).astype(BF)
        tmp[2, lo + 64 : lo + 128] = g3_ref[t * 64 : (t + 1) * 64]
        for v, src in enumerate((q0, q1, q2, q3)):
            tmp[3, lo + v * 32 : lo + v * 32 + 32] = src[t * 32 : (t + 1) * 32]
        t1_ref[512 + lo : 640 + lo] = cols(ref, h1)
    for v, ref in enumerate((own_ref, t1_ref, t2_ref, t3_ref)):
        ref[0:512] = tmp[r ^ v]


def attention(qs, ks, vs, us, docs, mult):
    nb = len(qs)
    keys, vals = jnp.concatenate(ks, 0), jnp.concatenate(vs, 0)
    doc_all = jnp.concatenate(docs, 0)
    outs, dqs, dk, dv, term = [], [], None, None, jnp.zeros((1, 1), F32)
    for b in range(nb):
        raw = mm_nt(qs[b], keys)
        allowed = mm_nt(docs[b], doc_all) > 0.5
        scores = jnp.where(allowed, raw * mult, -1e30)
        expo = jnp.exp(scores - jnp.max(scores, axis=1, keepdims=True))
        probs = expo * (1.0 / jnp.sum(expo, axis=1, keepdims=True))
        low = probs.astype(BF)
        att = mm(low, vals)
        delta = jnp.sum(us[b].astype(F32) * att, axis=1, keepdims=True)
        ds = probs * (mm_nt(us[b], vals) - delta)
        term += jnp.sum(jnp.sum(ds * raw, axis=1, keepdims=True), axis=0, keepdims=True)
        ds_low = ds.astype(BF)
        outs.append(att.astype(BF))
        dqs.append((mm(ds_low, keys) * mult).astype(BF))
        dk_b, dv_b = mm_tn(ds_low, qs[b]), mm_tn(low, us[b])
        dk, dv = (dk_b, dv_b) if dk is None else (dk + dk_b, dv + dv_b)
    dk = (dk * mult).astype(BF)
    dv = dv.astype(BF)
    part = lambda z: [z[b * 128 : (b + 1) * 128] for b in range(nb)]
    return outs, dqs, part(dk), part(dv), term * (1.0 / math.sqrt(D))


def doc_onehot(pos, bounds_ref):
    return onehot((pos >= bounds_ref[0:1]) & (pos < bounds_ref[1:2]))


def at_lane(term, head):
    return jnp.where(iota((1, 128), 1) == head, term, 0.0)


def near_kernel(ids, sharp, q_ref, k_ref, v_ref, u_ref, bounds_ref, g1_ref, z0_ref, own_ref, back_ref, terms_ref):
    dev = ids[0]
    x, y, q, r = xyqr(dev)
    row = iota((128, 128), 0)
    here = doc_onehot(dev * 128 + row, bounds_ref)
    there = doc_onehot((dev ^ 1) * 128 + row, bounds_ref)
    inv = 1.0 / math.sqrt(D)
    refs = (q_ref, k_ref, v_ref, u_ref)
    total = jnp.zeros((1, 128), F32)
    for h in range(2):
        blocks = [[ref[:, h * D : (h + 1) * D]] for ref in refs]
        *res, term = attention(*blocks, [here], sharp[h] * inv)
        for t in range(4):
            z0_ref[t * 128 : (t + 1) * 128, h * D : (h + 1) * D] = res[t][0]
        total += at_lane(term, h)
    h = 2 + (r & 1)
    blocks = [[cols(ref, h), g1_ref[512 + t * 128 : 640 + t * 128]] for t, ref in enumerate(refs)]
    *res, term = attention(*blocks, [here, there], sharp[h] * inv)
    for t in range(4):
        own_ref[t * 128 : (t + 1) * 128] = res[t][0]
        back_ref[t * 128 : (t + 1) * 128] = res[t][1]
    terms_ref[...] = jnp.broadcast_to(total + at_lane(term, h), (8, 128))


def pieces(v):
    hi = v.astype(BF).astype(F32)
    mid = (v - hi).astype(BF).astype(F32)
    lo = v - hi - mid
    row = iota((16, 128), 0)
    return jnp.where(row == 0, hi, jnp.where(row == 1, mid, jnp.where(row == 2, lo, 0.0))).astype(BF)


def task_kernel(ids, sharp, i0, i1, i2, i3, bounds_ref, terms_ref, back_ref, o0, o1, o2, o3):
    ins, outs = (i0, i1, i2, i3), (o0, o1, o2, o3)
    x, y, q, r = xyqr(ids[0])
    m = iota((128, 128), 0)
    j4, j5 = q, y & 1
    near, r3 = r < 2, r == 2
    far = r == 3
    q3 = q == 3
    u_m = jnp.where(near, q, q ^ jnp.where(r3, m >> 6, m >> 5))
    y_m = jnp.where(far & (q == 2), y ^ ((m >> 4) & 1), jnp.where(far & q3, jnp.where(y < 2, (m >> 3) & 3, (m >> 2) & 3), y))
    x_m = jnp.where(far & q3 & (y >= 2), (m >> 4) & 1, x)
    level = jnp.where(near, 2, jnp.where(r3, 3, jnp.where(q < 2, 4, jnp.where(q == 2, 5, jnp.where(y < 2, 6, 7)))))
    j = jnp.where(near, r, jnp.where(r3, q & 1, jnp.where(q < 2, q, jnp.where(q == 2, y & 1, jnp.where(y < 2, y, x)))))
    sh = level - 2
    dil = jnp.left_shift(1, sh)
    offset = (5 + j * (dil >> 1)) & (dil - 1)
    i_m = m & (jnp.right_shift(128, sh) - 1)
    low = (x_m * 64 + y_m * 16 + u_m * 4) * 128 + i_m * dil + offset
    docs = [doc_onehot(low + (r ^ v) * 128, bounds_ref) for v in range(4)]
    head = level * 2 + j
    blocks = [[ref[t * 128 : (t + 1) * 128] for ref in ins] for t in range(4)]
    *res, term = attention(*blocks, docs, sharp[head] * (1.0 / math.sqrt(D)))
    extra = pieces(terms_ref[0:1] + at_lane(term, head))
    for v, ref in enumerate(outs):
        for t in range(4):
            ref[t * 128 : (t + 1) * 128] = res[t][v]
        ref[512:528] = extra
    o1[528:1040] = back_ref[...]


def total4(blocks):
    a, b, c, d = [jnp.sum(z.astype(F32), axis=0, keepdims=True) for z in blocks]
    return (a + b) + (c + d)


def from_r_kernel(ids, i0, i1, i2, i3, own_ref, p1_ref, p2_ref, p3_ref):
    x, y, q, r = xyqr(ids[0])
    ins, outs = (i0, i1, i2, i3), (own_ref, p1_ref, p2_ref, p3_ref)
    for v, ref in enumerate(ins):

        @pl.when((r ^ v) == 2)
        def _():
            for t in range(4):
                p1_ref[144 + t * 64 : 208 + t * 64] = ref[t * 128 + 64 : t * 128 + 128]

        @pl.when((r ^ v) == 3)
        def _():
            for t in range(4):
                for w, out in enumerate(outs):
                    out[t * 32 : (t + 1) * 32] = ref[t * 128 + w * 32 : t * 128 + w * 32 + 32]

    extra = pieces(total4([ref[512:528] for ref in ins]))
    for out in outs:
        out[128:144] = extra


def from_q_kernel(ids, i0, i1, i2, i3, g5_ref, out_ref):
    x, y, q, r = xyqr(ids[0])
    dp = ids[1]
    ins = (i0, i1, i2, i3)
    want = xy_col(x, y, iota((256, 128), 1))
    perm = onehot(want == iota((256, 128), 0))
    extra = pieces(total4([ref[128:144] for ref in ins]))
    for d in range(32):
        out_ref[d, 0:32] = jnp.zeros((32, D), BF)
        out_ref[d, 32:48] = extra
    for v, ref in enumerate(ins):

        @pl.when((q ^ v) == 2)
        def _():
            for t in range(4):
                g5_ref[t * 16 : (t + 1) * 16] = ref[t * 32 + 16 : t * 32 + 32]

        @pl.when((q ^ v) == 3)
        def _():
            rows = mm(perm, ref[0:128]).astype(BF)
            for d in range(8):
                out_ref[d * 4 + dp, 0:32] = rows[d * 32 : (d + 1) * 32]


def spread(level, j):
    n = 128 // DIL[level]
    return onehot(iota((128, n), 0) == iota((128, n), 1) * DIL[level] + off(level, j))


def put(ref, head, value):
    ref[:, pl.ds(pl.multiple_of(head * D, D), D)] = value.astype(BF)


def unpack_low_kernel(ids, z0_ref, own_ref, r0, r1, r2, r3, q1, o_ref, dq_ref, dk_ref, dv_ref):
    x, y, q, r = xyqr(ids[0])
    res = (o_ref, dq_ref, dk_ref, dv_ref)
    j1, j3 = r & 1, q & 1
    w3b = spread(3, 1 - j3)
    for t, ref in enumerate(res):
        lo = t * 128
        ref[:, : 2 * D] = z0_ref[lo : lo + 128]
        put(ref, 2 + j1, own_ref[lo : lo + 128])
        put(ref, 3 - j1, r1[528 + lo : 656 + lo])
        put(ref, 7 - j3, mm(w3b, q1[144 + t * 64 : 208 + t * 64]))
    for v, src in enumerate((r0, r1, r2, r3)):
        role = r ^ v

        @pl.when(role < 2)
        def _():
            for t, ref in enumerate(res):
                put(ref, 4 + role, src[t * 128 : (t + 1) * 128])

        @pl.when(role == 2)
        def _():
            w3 = spread(3, j3)
            for t, ref in enumerate(res):
                put(ref, 6 + j3, mm(w3, src[t * 128 : t * 128 + 64]))


def unpack_high_kernel(ids, l0, l1, l2, l3, q0, q1, q2, q3, g5_ref, xy_ref, o_ref, dq_ref, dk_ref, dv_ref, terms_ref):
    x, y, q, r = xyqr(ids[0])
    dp = ids[1]
    res = (o_ref, dq_ref, dk_ref, dv_ref)
    j5 = y & 1
    w5b = spread(5, 1 - j5)
    pi, ci = iota((128, 32), 0), iota((128, 32), 1)
    for t, ref in enumerate(res):
        put(ref, 3 - j5, mm(w5b, g5_ref[t * 16 : (t + 1) * 16]))
        for j in range(2):
            w6 = onehot(pi == (ci - t * 8) * 16 + off(6, j))
            w7 = onehot(pi == (ci - t * 4) * 32 + off(7, j))
            put(ref, 4 + j, mm(w6, xy_ref[(x * 4 + j) * 4 + dp, 0:32]))
            put(ref, 6 + j, mm(w7, xy_ref[(j * 4 + 2) * 4 + dp, 0:32]))
    for v, src in enumerate((q0, q1, q2, q3)):
        role = q ^ v

        @pl.when(role < 2)
        def _():
            w4 = spread(4, role)
            for t, ref in enumerate(res):
                put(ref, role, mm(w4, src[t * 32 : (t + 1) * 32]))

        @pl.when(role == 2)
        def _():
            w5 = spread(5, j5)
            for t, ref in enumerate(res):
                put(ref, 2 + j5, mm(w5, src[t * 32 : t * 32 + 16]))

    acc = xy_ref[0, 32:48].astype(F32)
    for d in range(1, 32):
        acc += xy_ref[d, 32:48].astype(F32)
    terms_ref[...] = jnp.broadcast_to(jnp.sum(acc, axis=0, keepdims=True), (8, 128))


SMEM = pl.BlockSpec(memory_space=pltpu.SMEM)
VMEM = pl.BlockSpec(memory_space=pltpu.VMEM)
LIMIT = pltpu.CompilerParams(vmem_limit_bytes=20 << 20)


def stay(array):
    return pltpu.with_memory_space_constraint(array, pltpu.VMEM)


def call(kernel, outs, scalars, params, rest, name, scratch=(), out_space=pltpu.VMEM):
    shapes = [out_space(s, d) for s, d in outs]
    single = len(shapes) == 1
    return pl.pallas_call(
        kernel,
        in_specs=[SMEM] * len(scalars) + [VMEM] * (len(params) + len(rest)),
        out_specs=VMEM if single else [VMEM] * len(shapes),
        out_shape=shapes[0] if single else shapes,
        scratch_shapes=list(scratch),
        compiler_params=LIMIT,
        name=name,
    )(*scalars, *params, *[stay(a) for a in rest])


def swap(array, axis, v):
    return lax.ppermute(array, axis, [(i, i ^ v) for i in range(4)])


def body(asking_vectors, lookup_vectors, payload_vectors, incoming_sensitivity, learned_sharpness, reply_list_sizes):
    raw = [a[0] for a in (asking_vectors, lookup_vectors, payload_vectors, incoming_sensitivity)]
    ids = jnp.stack([lax.axis_index(SEQ), lax.axis_index("dp")]).astype(jnp.int32)
    block = lambda n: ((n, D), BF)
    xy = pl.pallas_call(
        pack_kernel,
        grid=(1,),
        in_specs=[SMEM] + [pl.BlockSpec((128, 8 * D), lambda i: (0, 1))] * 4,
        out_specs=pl.BlockSpec((8, 96, D), lambda i: (0, 0, 0)),
        out_shape=jax.ShapeDtypeStruct((8, 96, D), BF),
        compiler_params=LIMIT,
        name="pack",
    )(ids, *raw)
    xy = lax.all_to_all(xy, ("x", "y"), 0, 0)
    four = [stay(a) for a in raw]
    ends = jnp.cumsum(reply_list_sizes[0])
    n_docs = ends.shape[0]
    starts = jnp.concatenate([jnp.zeros((1,), jnp.int32), ends[:-1]])
    ends = jnp.concatenate([ends[:-1], jnp.full((1,), 1 << 30, jnp.int32)])
    bounds = jnp.pad(jnp.stack([starts, ends]), ((0, 6), (0, 128 - n_docs)))

    g3 = swap(call(pairs_kernel, [block(256)], [ids], four, [], "pairs"), "q", 1)
    q0, q1, q2, q3 = call(
        to_q_kernel, [block(128)] * 4, [ids], four, [xy], "to_q", [pltpu.VMEM((4, 128, D), BF)]
    )
    q2, q1, q3 = swap(q2, "q", 2), swap(q1, "q", 1), swap(q3, "q", 3)
    r0, r1, r2, r3 = call(
        to_r_kernel, [block(512), block(1024), block(512), block(512)], [ids], four, [g3, q0, q1, q2, q3], "to_r",
        [pltpu.VMEM((4, 512, D), BF)],
    )
    r1, r3, r2 = swap(r1, "r", 1), swap(r3, "r", 3), swap(r2, "r", 2)
    z0, own1, back1, terms = call(
        near_kernel,
        [((512, 2 * D), BF), block(512), block(512), ((8, 128), F32)],
        [ids, learned_sharpness], four, [bounds, r1], "near",
    )
    r0, r1, r2, r3 = call(
        task_kernel, [block(528), block(1040), block(528), block(528)], [ids, learned_sharpness], [],
        [r0, r1, r2, r3, bounds, terms, back1], "task",
    )
    r3, r2, r1 = swap(r3, "r", 3), swap(r2, "r", 2), swap(r1, "r", 1)
    q0, q1, q2, q3 = call(
        from_r_kernel, [block(144), block(400), block(144), block(144)], [ids], [], [r0, r1, r2, r3], "from_r"
    )
    q2, q1, q3 = swap(q2, "q", 2), swap(q1, "q", 1), swap(q3, "q", 3)
    back5, xy = call(from_q_kernel, [block(64), ((32, 48, D), BF)], [ids], [], [q0, q1, q2, q3], "from_q")
    xy = lax.all_to_all(xy, ("x", "y", "dp"), 0, 0)
    back5 = swap(back5, "y", 1)
    half = lambda i: pl.BlockSpec((128, 8 * D), lambda _: (0, i))
    result = jax.ShapeDtypeStruct((128, 16 * D), BF)
    args = [z0, own1, r0, r1, r2, r3, q1]
    outs = pl.pallas_call(
        unpack_low_kernel,
        grid=(1,),
        in_specs=[SMEM] + [VMEM] * len(args),
        out_specs=[half(0)] * 4,
        out_shape=[result] * 4,
        compiler_params=LIMIT,
        name="unpack_low",
    )(ids, *[stay(a) for a in args])
    args = [q0, q1, q2, q3, back5, xy]
    *outs, terms = pl.pallas_call(
        unpack_high_kernel,
        grid=(1,),
        in_specs=[SMEM] + [pl.BlockSpec(memory_space=pl.ANY)] * 4 + [VMEM] * len(args),
        out_specs=[half(1)] * 4 + [pl.BlockSpec((8, 128), lambda _: (0, 0))],
        out_shape=[result] * 4 + [jax.ShapeDtypeStruct((8, 128), F32)],
        input_output_aliases={1: 0, 2: 1, 3: 2, 4: 3},
        compiler_params=LIMIT,
        name="unpack_high",
    )(ids, *outs, *[stay(a) for a in args])
    return (*[o[None] for o in outs], terms[0, :16])


def solution(mesh):
    fine = Mesh(mesh.devices.reshape(2, 4, 4, 4, 4), SEQ + ("dp",))
    rows = P("dp", SEQ, None)
    in_specs = (rows, rows, rows, rows, P(), P("dp", None))
    out_specs = (rows, rows, rows, rows, P())
    return jax.shard_map(body, mesh=fine, in_specs=in_specs, out_specs=out_specs, check_vma=False)
```

time: 157 us -> 134 us (0.85)
  blocking collectives: 19 us -> 0 us
  starting transfers between devices: 75.6 us -> 87.2 us
  waiting for transfers between devices: 30 us -> 21.5 us
  Pallas kernels: 24 us -> 16.9 us
    ppermute x9 -> x14, starting transfers between devices: 37.2 us -> 65.9 us  [swap(): return lax.ppermute(array, axis, [(i, i ^ v) for i in range(4)])]
    all_to_all x1 -> x0, blocking collectives: 19 us -> none  [body(): rs = lax.all_to_all(rs, 'r', 0, 0)]
    all_to_all x3 -> x1, starting transfers between devices: 25.6 us -> 13.8 us  [body(): xy = lax.all_to_all(xy, ('x', 'y', 'dp'), 0, 0)]
    pallas_call x9 -> x10, Pallas kernels: 24 us -> 16.9 us  [the longest x7 11 us: call(): pl.pallas_call(kernel, in_specs=[SMEM] * len(scalars) + [VMEM] * (len(par...]
    all_to_all x3 -> x1, waiting for transfers between devices: 10.1 us -> 4.54 us  [body(): xy = lax.all_to_all(xy, ('x', 'y', 'dp'), 0, 0)]
    all_to_all x2 -> x1, starting transfers between devices: 12.8 us -> 7.47 us  [body(): xy = lax.all_to_all(xy, ('x', 'y'), 0, 0)]
    all_to_all x2 -> x1, waiting for transfers between devices: 2.21 us -> 0.01 us  [body(): xy = lax.all_to_all(xy, ('x', 'y'), 0, 0)]
    ppermute x9 -> x14, waiting for transfers between devices: 17.6 us -> 17 us  [swap(): return lax.ppermute(array, axis, [(i, i ^ v) for i in range(4)])]
  transfers between devices with their start and end apart: 14 -> 16, of which waited for: 5 -> 8; matrix products, arithmetic and copies ran while one was open for 1% -> 0% of each run, Pallas kernels for 7% -> 5%
where the time goes in v2:
time: 134 us; the launch traced here: 132 us
  starting transfers between devices  87.2 us (65%)
  waiting for transfers between devices  21.5 us (16%)
  Pallas kernels  16.9 us (13%)
  local copies, waits for them, and re-layouts  5.33 us (4%)
    ppermute x14, starting transfers between devices, swap(): return lax.ppermute(array, axis, [(i, i ^ v) for i in range(4)])  65.9 us
    ppermute x14, waiting for transfers between devices, swap(): return lax.ppermute(array, axis, [(i, i ^ v) for i in range(4)])  17 us
    all_to_all x1, starting transfers between devices, body(): xy = lax.all_to_all(xy, ('x', 'y', 'dp'), 0, 0)  13.8 us
    pallas_call x7, Pallas kernels, call(): pl.pallas_call(kernel, in_specs=[SMEM] * len(scalars) + [VMEM] * (len(par...  11 us
    all_to_all x1, starting transfers between devices, body(): xy = lax.all_to_all(xy, ('x', 'y'), 0, 0)  7.47 us
    unnamed x20, local copies, waits for them, and re-layouts  4.81 us
    all_to_all x1, waiting for transfers between devices, body(): xy = lax.all_to_all(xy, ('x', 'y', 'dp'), 0, 0)  4.54 us
  transfers between devices with their start and end apart: 16, of which 8 were waited for; matrix products, arithmetic and copies ran while one was open for 0% of the time, Pallas kernels for 5%

profile of v2, /device:TPU:1, one launch (start us, length us, event | category | flops | bytes accessed | tf_op | source)
XLA Modules:
  0.0 132.2 jit_solution(9931103717115086900)
XLA Ops:
  0.6 0.1 pad_add_fusion.1.ids
  0.7 0.0 copy-start
  0.7 1.0 copy-done
  1.8 0.0 copy-start.2
  1.8 1.0 copy-done.2
  2.8 0.0 copy-start.4
  2.8 1.0 copy-done.4
  3.8 0.0 copy-start.6
  3.8 1.0 copy-done.6
  4.9 0.0 copy-start.1
  4.9 0.0 copy-start.3
  4.9 1.5 %pack.1 = bf16[8,96,128]{2,1,0:T(8,128)(2,1)} custom-call(s32[2]{0:T(128)S(1)} %pad_add_fusion.1.ids, bf16[128,2048]{1,0:T(8,128)(2,1)S(1)} %bitcast.19, bf16[128,2048]{1,0:T(8,128)(2,1)S(1)} %bitcast.24, bf16[128,2048]{1,0:T(8,128)(2,1)S(1)} %bitcast.29, bf16[128,2048]{1,0:T(8,128)(2,1)S(1)} %bitcast.34), custom_call_target="tpu_custom_call" | custom-call | tf_op jit(solution)/shard_map/pack/pallas_call | solution.py:373
  6.4 7.5 %all-to-all-start = ((bf16[8,96,128]{2,1,0:T(8,128)(2,1)}), bf16[8,96,128]{2,1,0:T(8,128)(2,1)S(1)}, u32[]{:S(2)}, u32[]{:S(2)}) async-start(bf16[8,96,128]{2,1,0:T(8,128)(2,1)} %pack.1), calls=%async_computation | async-start | bytes 393216 | tf_op jit(solution)/shard_map/all_to_all | solution.py:382
  13.9 0.0 copy-done.1
  13.9 0.0 copy-done.3
  13.9 0.0 copy-done.5
  13.9 0.0 copy-done.7
  13.9 0.7 pairs.1
  14.6 8.8 %collective-permute-start = (bf16[256,128]{1,0:T(8,128)(2,1)S(1)}, bf16[256,128]{1,0:T(8,128)(2,1)S(1)}, u32[]{:S(2)}, u32[]{:S(2)}) collective-permute-start(bf16[256,128]{1,0:T(8,128)(2,1)S(1)} %pairs.1), channel_id=1, source_target_pairs={{0,16},{16,0},{32,48},{48,32},{1,17},{17,1},{33,49},{49,33},{2,18}... | collective-permute-start | bytes 196616 | tf_op jit(solution)/shard_map/ppermute | solution.py:366
  23.5 0.0 all-to-all-done.xy_ref
  23.5 0.8 to_q.1
  24.3 6.5 %collective-permute-start.1 = (bf16[128,128]{1,0:T(8,128)(2,1)S(1)}, bf16[128,128]{1,0:T(8,128)(2,1)S(1)}, u32[]{:S(2)}, u32[]{:S(2)}) collective-permute-start(bf16[128,128]{1,0:T(8,128)(2,1)S(1)} %get-tuple-element.37), channel_id=1, source_target_pairs={{0,16},{16,0},{32,48},{48,32},{1,17},{17,1},{33,49},{49,33},{2,18}... | collective-permute-start | bytes 98312 | tf_op jit(solution)/shard_map/ppermute | solution.py:366
  30.8 10.6 %collective-permute-start.2 = (bf16[128,128]{1,0:T(8,128)(2,1)S(1)}, bf16[128,128]{1,0:T(8,128)(2,1)S(1)}, u32[]{:S(2)}, u32[]{:S(2)}) collective-permute-start(bf16[128,128]{1,0:T(8,128)(2,1)S(1)} %get-tuple-element.38), channel_id=1, source_target_pairs={{0,32},{16,48},{32,0},{48,16},{1,33},{17,49},{33,1},{49,17},{2,34}... | collective-permute-start | bytes 98312 | tf_op jit(solution)/shard_map/ppermute | solution.py:366
  41.5 0.0 copy-start.9
  41.5 1.9 %collective-permute-start.3 = (bf16[128,128]{1,0:T(8,128)(2,1)S(1)}, bf16[128,128]{1,0:T(8,128)(2,1)S(1)}, u32[]{:S(2)}, u32[]{:S(2)}) collective-permute-start(bf16[128,128]{1,0:T(8,128)(2,1)S(1)} %get-tuple-element.39), channel_id=1, source_target_pairs={{0,48},{16,32},{32,16},{48,0},{1,49},{17,33},{33,17},{49,1},{2,50}... | collective-permute-start | bytes 98312 | tf_op jit(solution)/shard_map/ppermute | solution.py:366
  43.4 0.0 copy-done.9
  43.4 0.2 reduce-window.4
  43.6 0.0 collective-permute-done.g3_ref
  43.6 0.0 collective-permute-done.1.q1
  43.6 0.6 collective-permute-done.2.q2
  44.2 6.1 %collective-permute-done.3.q3 = bf16[128,128]{1,0:T(8,128)(2,1)S(1)} collective-permute-done((bf16[128,128]{1,0:T(8,128)(2,1)S(1)}, bf16[128,128]{1,0:T(8,128)(2,1)S(1)}, u32[]{:S(2)}, u32[]{:S(2)}) %collective-permute-start.3) | collective-permute-done | bytes 32800 | tf_op jit(solution)/shard_map/ppermute | solution.py:366
  50.3 0.8 to_r.1
  51.1 2.4 %collective-permute-start.4 = (bf16[1024,128]{1,0:T(8,128)(2,1)S(1)}, bf16[1024,128]{1,0:T(8,128)(2,1)S(1)}, u32[]{:S(2)}, u32[]{:S(2)}) collective-permute-start(bf16[1024,128]{1,0:T(8,128)(2,1)S(1)} %get-tuple-element.40), channel_id=1, source_target_pairs={{0,4},{4,0},{8,12},{12,8},{1,5},{5,1},{9,13},{13,9},{2,6},{6,2},{1... | collective-permute-start | bytes 786440 | tf_op jit(solution)/shard_map/ppermute | solution.py:366
  53.5 3.1 %collective-permute-start.5 = (bf16[512,128]{1,0:T(8,128)(2,1)S(1)}, bf16[512,128]{1,0:T(8,128)(2,1)S(1)}, u32[]{:S(2)}, u32[]{:S(2)}) collective-permute-start(bf16[512,128]{1,0:T(8,128)(2,1)S(1)} %get-tuple-element.44), channel_id=1, source_target_pairs={{0,8},{4,12},{8,0},{12,4},{1,9},{5,13},{9,1},{13,5},{2,10},{6,14},... | collective-permute-start | bytes 393224 | tf_op jit(solution)/shard_map/ppermute | solution.py:366
  56.6 3.8 %collective-permute-start.6 = (bf16[512,128]{1,0:T(8,128)(2,1)S(1)}, bf16[512,128]{1,0:T(8,128)(2,1)S(1)}, u32[]{:S(2)}, u32[]{:S(2)}) collective-permute-start(bf16[512,128]{1,0:T(8,128)(2,1)S(1)} %get-tuple-element.45), channel_id=1, source_target_pairs={{0,12},{4,8},{8,4},{12,0},{1,13},{5,9},{9,5},{13,1},{2,14},{6,10},... | collective-permute-start | bytes 393224 | tf_op jit(solution)/shard_map/ppermute | solution.py:366
  60.4 0.1 add_bitcast_fusion
  60.5 0.0 copy-start.8
  60.5 0.0 collective-permute-done.4.g1_ref.i1
  60.5 0.6 copy-done.8
  61.1 3.0 %near.1 = (bf16[512,256]{1,0:T(8,128)(2,1)S(1)}, bf16[512,128]{1,0:T(8,128)(2,1)S(1)}, bf16[512,128]{1,0:T(8,128)(2,1)S(1)}, f32[8,128]{1,0:T(8,128)S(1)}) custom-call(s32[2]{0:T(128)S(1)} %pad_add_fusion.1.ids, f32[16]{0:T(128)S(1)} %copy-done.8, bf16[128,2048]{1,0:T(8,128)(2,1)S(1)} %bitcast.23, bf16[128,2048]{1,0:T(8,128)(2,1)S(1)} %bitcast.28, ...), custom_call_target="tpu_custom_call" | custom-call | tf_op jit(solution)/shard_map/near/pallas_call | solution.py:354
  64.2 0.0 collective-permute-done.5.i2
  64.2 1.4 %collective-permute-done.6.i3 = bf16[512,128]{1,0:T(8,128)(2,1)S(1)} collective-permute-done((bf16[512,128]{1,0:T(8,128)(2,1)S(1)}, bf16[512,128]{1,0:T(8,128)(2,1)S(1)}, u32[]{:S(2)}, u32[]{:S(2)}) %collective-permute-start.6) | collective-permute-done | bytes 131104 | tf_op jit(solution)/shard_map/ppermute | solution.py:366
  65.6 3.6 %task.1 = (bf16[528,128]{1,0:T(8,128)(2,1)S(1)}, bf16[1040,128]{1,0:T(8,128)(2,1)S(1)}, bf16[528,128]{1,0:T(8,128)(2,1)S(1)}, bf16[528,128]{1,0:T(8,128)(2,1)S(1)}) custom-call(s32[2]{0:T(128)S(1)} %pad_add_fusion.1.ids, f32[16]{0:T(128)S(1)} %copy-done.8, bf16[512,128]{1,0:T(8,128)(2,1)S(1)} %get-tuple-element.43.i0, ...), custom_call_target="tpu_custom_call" | custom-call | tf_op jit(solution)/shard_map/task/pallas_call | solution.py:354
  69.2 1.9 %collective-permute-start.7 = (bf16[1040,128]{1,0:T(8,128)(2,1)S(1)}, bf16[1040,128]{1,0:T(8,128)(2,1)S(1)}, u32[]{:S(2)}, u32[]{:S(2)}) collective-permute-start(bf16[1040,128]{1,0:T(8,128)(2,1)S(1)} %get-tuple-element.49), channel_id=1, source_target_pairs={{0,4},{4,0},{8,12},{12,8},{1,5},{5,1},{9,13},{13,9},{2,6},{6,2},{1... | collective-permute-start | bytes 798728 | tf_op jit(solution)/shard_map/ppermute | solution.py:366
  71.1 4.1 %collective-permute-start.8 = (bf16[528,128]{1,0:T(8,128)(2,1)S(1)}, bf16[528,128]{1,0:T(8,128)(2,1)S(1)}, u32[]{:S(2)}, u32[]{:S(2)}) collective-permute-start(bf16[528,128]{1,0:T(8,128)(2,1)S(1)} %get-tuple-element.50), channel_id=1, source_target_pairs={{0,8},{4,12},{8,0},{12,4},{1,9},{5,13},{9,1},{13,5},{2,10},{6,14},... | collective-permute-start | bytes 405512 | tf_op jit(solution)/shard_map/ppermute | solution.py:366
  75.2 3.3 %collective-permute-start.9 = (bf16[528,128]{1,0:T(8,128)(2,1)S(1)}, bf16[528,128]{1,0:T(8,128)(2,1)S(1)}, u32[]{:S(2)}, u32[]{:S(2)}) collective-permute-start(bf16[528,128]{1,0:T(8,128)(2,1)S(1)} %get-tuple-element.51), channel_id=1, source_target_pairs={{0,12},{4,8},{8,4},{12,0},{1,13},{5,9},{9,5},{13,1},{2,14},{6,10},... | collective-permute-start | bytes 405512 | tf_op jit(solution)/shard_map/ppermute | solution.py:366
  78.5 0.8 collective-permute-done.8.i2.r2
  79.3 5.0 %collective-permute-done.9.i3.r3 = bf16[528,128]{1,0:T(8,128)(2,1)S(1)} collective-permute-done((bf16[528,128]{1,0:T(8,128)(2,1)S(1)}, bf16[528,128]{1,0:T(8,128)(2,1)S(1)}, u32[]{:S(2)}, u32[]{:S(2)}) %collective-permute-start.9) | collective-permute-done | bytes 135200 | tf_op jit(solution)/shard_map/ppermute | solution.py:366
  84.3 0.0 collective-permute-done.7.i1.r1
  84.3 0.6 from_r.1
  84.9 5.0 %collective-permute-start.10 = (bf16[400,128]{1,0:T(8,128)(2,1)S(1)}, bf16[400,128]{1,0:T(8,128)(2,1)S(1)}, u32[]{:S(2)}, u32[]{:S(2)}) collective-permute-start(bf16[400,128]{1,0:T(8,128)(2,1)S(1)} %get-tuple-element.52), channel_id=1, source_target_pairs={{0,16},{16,0},{32,48},{48,32},{1,17},{17,1},{33,49},{49,33},{2,18}... | collective-permute-start | bytes 307208 | tf_op jit(solution)/shard_map/ppermute | solution.py:366
  89.8 5.4 %collective-permute-start.11 = (bf16[144,128]{1,0:T(8,128)(2,1)S(1)}, bf16[144,128]{1,0:T(8,128)(2,1)S(1)}, u32[]{:S(2)}, u32[]{:S(2)}) collective-permute-start(bf16[144,128]{1,0:T(8,128)(2,1)S(1)} %get-tuple-element.58), channel_id=1, source_target_pairs={{0,32},{16,48},{32,0},{48,16},{1,33},{17,49},{33,1},{49,17},{2,34}... | collective-permute-start | bytes 110600 | tf_op jit(solution)/shard_map/ppermute | solution.py:366
  95.3 5.8 %collective-permute-start.12 = (bf16[144,128]{1,0:T(8,128)(2,1)S(1)}, bf16[144,128]{1,0:T(8,128)(2,1)S(1)}, u32[]{:S(2)}, u32[]{:S(2)}) collective-permute-start(bf16[144,128]{1,0:T(8,128)(2,1)S(1)} %get-tuple-element.59), channel_id=1, source_target_pairs={{0,48},{16,32},{32,16},{48,0},{1,49},{17,33},{33,17},{49,1},{2,50}... | collective-permute-start | bytes 110600 | tf_op jit(solution)/shard_map/ppermute | solution.py:366
  101.1 2.2 %collective-permute-done.11.i2.q2 = bf16[144,128]{1,0:T(8,128)(2,1)S(1)} collective-permute-done((bf16[144,128]{1,0:T(8,128)(2,1)S(1)}, bf16[144,128]{1,0:T(8,128)(2,1)S(1)}, u32[]{:S(2)}, u32[]{:S(2)}) %collective-permute-start.11) | collective-permute-done | bytes 36896 | tf_op jit(solution)/shard_map/ppermute | solution.py:366
  103.3 0.9 collective-permute-done.12.i3.q3
  104.2 0.0 collective-permute-done.10.q1.i1
  104.2 1.5 %from_q.1 = (bf16[64,128]{1,0:T(8,128)(2,1)S(1)}, bf16[32,48,128]{2,1,0:T(8,128)(2,1)}) custom-call(s32[2]{0:T(128)S(1)} %pad_add_fusion.1.ids, bf16[144,128]{1,0:T(8,128)(2,1)S(1)} %get-tuple-element.57.i0.q0, bf16[400,128]{1,0:T(8,128)(2,1)S(1)} %collective-permute-done.10.q1.i1, bf16[144,128]{1,0:T(8,128)(2,1)S(1)} %collective-permute-done.11.i2.q2, ...), custom_call_target="tpu_custom_call" | custom-call | tf_op jit(solution)/shard_map/from_q/pallas_call | solution.py:354
  105.7 13.8 %all-to-all-start.1 = ((bf16[32,48,128]{2,1,0:T(8,128)(2,1)}), bf16[32,48,128]{2,1,0:T(8,128)(2,1)S(1)}, u32[]{:S(2)}, u32[]{:S(2)}) async-start(bf16[32,48,128]{2,1,0:T(8,128)(2,1)} %get-tuple-element.61), calls=%async_computation.1 | async-start | bytes 786432 | tf_op jit(solution)/shard_map/all_to_all | solution.py:415
  119.5 3.3 %collective-permute-start.13 = (bf16[64,128]{1,0:T(8,128)(2,1)S(1)}, bf16[64,128]{1,0:T(8,128)(2,1)S(1)}, u32[]{:S(2)}, u32[]{:S(2)}) collective-permute-start(bf16[64,128]{1,0:T(8,128)(2,1)S(1)} %get-tuple-element.60), channel_id=1, source_target_pairs={{0,64},{64,0},{128,192},{192,128},{1,65},{65,1},{129,193},{193,129... | collective-permute-start | bytes 49160 | tf_op jit(solution)/shard_map/ppermute | solution.py:366
  122.8 2.0 %unpack_low.1 = (bf16[128,2048]{1,0:T(8,128)(2,1)}, bf16[128,2048]{1,0:T(8,128)(2,1)}, bf16[128,2048]{1,0:T(8,128)(2,1)}, bf16[128,2048]{1,0:T(8,128)(2,1)}) custom-call(s32[2]{0:T(128)S(1)} %pad_add_fusion.1.ids, bf16[512,256]{1,0:T(8,128)(2,1)S(1)} %get-tuple-element.41.z0_ref, bf16[512,128]{1,0:T(8,128)(2,1)S(1)} %get-tuple-element.42.own_ref, ...), custom_call_target="tpu_custom_call" | custom-call | tf_op jit(solution)/shard_map/unpack_low/pallas_call | solution.py:420
  124.8 0.0 collective-permute-done.13.g5_ref
  124.8 4.5 %all-to-all-done.1.xy_ref = bf16[32,48,128]{2,1,0:T(8,128)(2,1)S(1)} async-done(((bf16[32,48,128]{2,1,0:T(8,128)(2,1)}), bf16[32,48,128]{2,1,0:T(8,128)(2,1)S(1)}, u32[]{:S(2)}, u32[]{:S(2)}) %all-to-all-start.1) | async-done | bytes 393248 | tf_op jit(solution)/shard_map/all_to_all | solution.py:415
  129.4 2.3 %unpack_high.1 = (bf16[128,2048]{1,0:T(8,128)(2,1)}, bf16[128,2048]{1,0:T(8,128)(2,1)}, bf16[128,2048]{1,0:T(8,128)(2,1)}, bf16[128,2048]{1,0:T(8,128)(2,1)}, f32[8,128]{1,0:T(8,128)S(1)}) custom-call(s32[2]{0:T(128)S(1)} %pad_add_fusion.1.ids, ...), custom_call_target="tpu_custom_call", output_to_operand_aliasing={{0}: (1, {}), {1}: (2, {}), {2}: (3, {}), {3}: (4, {})} | custom-call | tf_op jit(solution)/shard_map/unpack_high/pallas_call | solution.py:430
  131.7 0.5 slice_bitcast_fusion
  (5 shorter events, 0.0 us)
Async XLA Ops:
  0.7 1.0 copy-start
  1.8 1.0 copy-start.2
  2.8 1.0 copy-start.4
  3.8 1.0 copy-start.6
  4.9 9.0 %copy-start.1 = (bf16[1,128,2048]{2,1,0:T(8,128)(2,1)S(1)}, bf16[1,128,2048]{2,1,0:T(8,128)(2,1)}, u32[]{:S(2)}) copy-start(bf16[1,128,2048]{2,1,0:T(8,128)(2,1)} %param.6) | copy-start | bytes 1572868
  4.9 9.0 %copy-start.3 = (bf16[1,128,2048]{2,1,0:T(8,128)(2,1)S(1)}, bf16[1,128,2048]{2,1,0:T(8,128)(2,1)}, u32[]{:S(2)}) copy-start(bf16[1,128,2048]{2,1,0:T(8,128)(2,1)} %param.7) | copy-start | bytes 1572868
  4.9 9.0 %copy-start.5 = (bf16[1,128,2048]{2,1,0:T(8,128)(2,1)S(1)}, bf16[1,128,2048]{2,1,0:T(8,128)(2,1)}, u32[]{:S(2)}) copy-start(bf16[1,128,2048]{2,1,0:T(8,128)(2,1)} %param.8) | copy-start | bytes 1572868
  4.9 9.0 %copy-start.7 = (bf16[1,128,2048]{2,1,0:T(8,128)(2,1)S(1)}, bf16[1,128,2048]{2,1,0:T(8,128)(2,1)}, u32[]{:S(2)}) copy-start(bf16[1,128,2048]{2,1,0:T(8,128)(2,1)} %param.9) | copy-start | bytes 1572868
  6.4 17.0 %all-to-all-start = ((bf16[8,96,128]{2,1,0:T(8,128)(2,1)}), bf16[8,96,128]{2,1,0:T(8,128)(2,1)S(1)}, u32[]{:S(2)}, u32[]{:S(2)}) async-start(bf16[8,96,128]{2,1,0:T(8,128)(2,1)} %pack.1), calls=%async_computation | async-start | bytes 393216 | tf_op jit(solution)/shard_map/all_to_all | solution.py:382
  14.6 29.0 %collective-permute-start = (bf16[256,128]{1,0:T(8,128)(2,1)S(1)}, bf16[256,128]{1,0:T(8,128)(2,1)S(1)}, u32[]{:S(2)}, u32[]{:S(2)}) collective-permute-start(bf16[256,128]{1,0:T(8,128)(2,1)S(1)} %pairs.1), channel_id=1, source_target_pairs={{0,16},{16,0},{32,48},{48,32},{1,17},{17,1},{33,49},{49,33},{2,18}... | collective-permute-start | bytes 196616 | tf_op jit(solution)/shard_map/ppermute | solution.py:366
  24.3 19.3 %collective-permute-start.1 = (bf16[128,128]{1,0:T(8,128)(2,1)S(1)}, bf16[128,128]{1,0:T(8,128)(2,1)S(1)}, u32[]{:S(2)}, u32[]{:S(2)}) collective-permute-start(bf16[128,128]{1,0:T(8,128)(2,1)S(1)} %get-tuple-element.37), channel_id=1, source_target_pairs={{0,16},{16,0},{32,48},{48,32},{1,17},{17,1},{33,49},{49,33},{2,18}... | collective-permute-start | bytes 98312 | tf_op jit(solution)/shard_map/ppermute | solution.py:366
  30.8 13.4 %collective-permute-start.2 = (bf16[128,128]{1,0:T(8,128)(2,1)S(1)}, bf16[128,128]{1,0:T(8,128)(2,1)S(1)}, u32[]{:S(2)}, u32[]{:S(2)}) collective-permute-start(bf16[128,128]{1,0:T(8,128)(2,1)S(1)} %get-tuple-element.38), channel_id=1, source_target_pairs={{0,32},{16,48},{32,0},{48,16},{1,33},{17,49},{33,1},{49,17},{2,34}... | collective-permute-start | bytes 98312 | tf_op jit(solution)/shard_map/ppermute | solution.py:366
  41.5 1.9 %copy-start.9 = (s32[1,8]{1,0:T(1,128)S(1)}, s32[1,8]{1,0:T(1,128)}, u32[]{:S(2)}) copy-start(s32[1,8]{1,0:T(1,128)} %param.11) | copy-start | bytes 100
  41.5 8.8 %collective-permute-start.3 = (bf16[128,128]{1,0:T(8,128)(2,1)S(1)}, bf16[128,128]{1,0:T(8,128)(2,1)S(1)}, u32[]{:S(2)}, u32[]{:S(2)}) collective-permute-start(bf16[128,128]{1,0:T(8,128)(2,1)S(1)} %get-tuple-element.39), channel_id=1, source_target_pairs={{0,48},{16,32},{32,16},{48,0},{1,49},{17,33},{33,17},{49,1},{2,50}... | collective-permute-start | bytes 98312 | tf_op jit(solution)/shard_map/ppermute | solution.py:366
  51.1 9.4 %collective-permute-start.4 = (bf16[1024,128]{1,0:T(8,128)(2,1)S(1)}, bf16[1024,128]{1,0:T(8,128)(2,1)S(1)}, u32[]{:S(2)}, u32[]{:S(2)}) collective-permute-start(bf16[1024,128]{1,0:T(8,128)(2,1)S(1)} %get-tuple-element.40), channel_id=1, source_target_pairs={{0,4},{4,0},{8,12},{12,8},{1,5},{5,1},{9,13},{13,9},{2,6},{6,2},{1... | collective-permute-start | bytes 786440 | tf_op jit(solution)/shard_map/ppermute | solution.py:366
  53.5 10.7 %collective-permute-start.5 = (bf16[512,128]{1,0:T(8,128)(2,1)S(1)}, bf16[512,128]{1,0:T(8,128)(2,1)S(1)}, u32[]{:S(2)}, u32[]{:S(2)}) collective-permute-start(bf16[512,128]{1,0:T(8,128)(2,1)S(1)} %get-tuple-element.44), channel_id=1, source_target_pairs={{0,8},{4,12},{8,0},{12,4},{1,9},{5,13},{9,1},{13,5},{2,10},{6,14},... | collective-permute-start | bytes 393224 | tf_op jit(solution)/shard_map/ppermute | solution.py:366
  56.6 9.0 %collective-permute-start.6 = (bf16[512,128]{1,0:T(8,128)(2,1)S(1)}, bf16[512,128]{1,0:T(8,128)(2,1)S(1)}, u32[]{:S(2)}, u32[]{:S(2)}) collective-permute-start(bf16[512,128]{1,0:T(8,128)(2,1)S(1)} %get-tuple-element.45), channel_id=1, source_target_pairs={{0,12},{4,8},{8,4},{12,0},{1,13},{5,9},{9,5},{13,1},{2,14},{6,10},... | collective-permute-start | bytes 393224 | tf_op jit(solution)/shard_map/ppermute | solution.py:366
  60.5 0.7 copy-start.8
  69.2 15.1 %collective-permute-start.7 = (bf16[1040,128]{1,0:T(8,128)(2,1)S(1)}, bf16[1040,128]{1,0:T(8,128)(2,1)S(1)}, u32[]{:S(2)}, u32[]{:S(2)}) collective-permute-start(bf16[1040,128]{1,0:T(8,128)(2,1)S(1)} %get-tuple-element.49), channel_id=1, source_target_pairs={{0,4},{4,0},{8,12},{12,8},{1,5},{5,1},{9,13},{13,9},{2,6},{6,2},{1... | collective-permute-start | bytes 798728 | tf_op jit(solution)/shard_map/ppermute | solution.py:366
  71.1 8.2 %collective-permute-start.8 = (bf16[528,128]{1,0:T(8,128)(2,1)S(1)}, bf16[528,128]{1,0:T(8,128)(2,1)S(1)}, u32[]{:S(2)}, u32[]{:S(2)}) collective-permute-start(bf16[528,128]{1,0:T(8,128)(2,1)S(1)} %get-tuple-element.50), channel_id=1, source_target_pairs={{0,8},{4,12},{8,0},{12,4},{1,9},{5,13},{9,1},{13,5},{2,10},{6,14},... | collective-permute-start | bytes 405512 | tf_op jit(solution)/shard_map/ppermute | solution.py:366
  75.2 9.1 %collective-permute-start.9 = (bf16[528,128]{1,0:T(8,128)(2,1)S(1)}, bf16[528,128]{1,0:T(8,128)(2,1)S(1)}, u32[]{:S(2)}, u32[]{:S(2)}) collective-permute-start(bf16[528,128]{1,0:T(8,128)(2,1)S(1)} %get-tuple-element.51), channel_id=1, source_target_pairs={{0,12},{4,8},{8,4},{12,0},{1,13},{5,9},{9,5},{13,1},{2,14},{6,10},... | collective-permute-start | bytes 405512 | tf_op jit(solution)/shard_map/ppermute | solution.py:366
  84.9 19.3 %collective-permute-start.10 = (bf16[400,128]{1,0:T(8,128)(2,1)S(1)}, bf16[400,128]{1,0:T(8,128)(2,1)S(1)}, u32[]{:S(2)}, u32[]{:S(2)}) collective-permute-start(bf16[400,128]{1,0:T(8,128)(2,1)S(1)} %get-tuple-element.52), channel_id=1, source_target_pairs={{0,16},{16,0},{32,48},{48,32},{1,17},{17,1},{33,49},{49,33},{2,18}... | collective-permute-start | bytes 307208 | tf_op jit(solution)/shard_map/ppermute | solution.py:366
  89.8 13.5 %collective-permute-start.11 = (bf16[144,128]{1,0:T(8,128)(2,1)S(1)}, bf16[144,128]{1,0:T(8,128)(2,1)S(1)}, u32[]{:S(2)}, u32[]{:S(2)}) collective-permute-start(bf16[144,128]{1,0:T(8,128)(2,1)S(1)} %get-tuple-element.58), channel_id=1, source_target_pairs={{0,32},{16,48},{32,0},{48,16},{1,33},{17,49},{33,1},{49,17},{2,34}... | collective-permute-start | bytes 110600 | tf_op jit(solution)/shard_map/ppermute | solution.py:366
  95.3 8.9 %collective-permute-start.12 = (bf16[144,128]{1,0:T(8,128)(2,1)S(1)}, bf16[144,128]{1,0:T(8,128)(2,1)S(1)}, u32[]{:S(2)}, u32[]{:S(2)}) collective-permute-start(bf16[144,128]{1,0:T(8,128)(2,1)S(1)} %get-tuple-element.59), channel_id=1, source_target_pairs={{0,48},{16,32},{32,16},{48,0},{1,49},{17,33},{33,17},{49,1},{2,50}... | collective-permute-start | bytes 110600 | tf_op jit(solution)/shard_map/ppermute | solution.py:366
  105.7 23.7 %all-to-all-start.1 = ((bf16[32,48,128]{2,1,0:T(8,128)(2,1)}), bf16[32,48,128]{2,1,0:T(8,128)(2,1)S(1)}, u32[]{:S(2)}, u32[]{:S(2)}) async-start(bf16[32,48,128]{2,1,0:T(8,128)(2,1)} %get-tuple-element.61), calls=%async_computation.1 | async-start | bytes 786432 | tf_op jit(solution)/shard_map/all_to_all | solution.py:415
  119.5 5.3 %collective-permute-start.13 = (bf16[64,128]{1,0:T(8,128)(2,1)S(1)}, bf16[64,128]{1,0:T(8,128)(2,1)S(1)}, u32[]{:S(2)}, u32[]{:S(2)}) collective-permute-start(bf16[64,128]{1,0:T(8,128)(2,1)S(1)} %get-tuple-element.60), channel_id=1, source_target_pairs={{0,64},{64,0},{128,192},{192,128},{1,65},{65,1},{129,193},{193,129... | collective-permute-start | bytes 49160 | tf_op jit(solution)/shard_map/ppermute | solution.py:366

commit v3 on v2

--- a/solution.py
+++ b/solution.py
@@ -7,6 +7,7 @@
 from jax.experimental.pallas import tpu as pltpu
 from jax.sharding import Mesh, PartitionSpec as P
 
+
 D = 128
 BF = jnp.bfloat16
 F32 = jnp.float32
@@ -39,7 +40,7 @@
     return lax.dot_general(a, b, (((0,), (0,)), ((), ())), preferred_element_type=F32)
 
 
-def pick(level, j, rows=128):
+def pick(level, j):
     n = 128 // DIL[level]
     return onehot(iota((n, 128), 1) == iota((n, 128), 0) * DIL[level] + off(level, j))
 
@@ -60,7 +61,7 @@
 
 
 def pack_kernel(ids, q_ref, k_ref, v_ref, u_ref, xy_ref):
-    x, y, q, r = xyqr(ids[0])
+    x, y, _, _ = xyqr(ids[0])
     srcs = (q_ref, k_ref, v_ref, u_ref)
     j5 = 1 - (y & 1)
     s5 = pick(5, j5)
@@ -80,32 +81,25 @@
         xy_ref[j * 4 + 2, 0:32] = acc7.astype(BF)
 
 
-def pairs_kernel(ids, q_ref, k_ref, v_ref, u_ref, g3_ref):
-    x, y, q, r = xyqr(ids[0])
-    j3 = 1 - (q & 1)
-    s3 = pick(3, j3)
-    for t, ref in enumerate((q_ref, k_ref, v_ref, u_ref)):
-        g3_ref[t * 64 : (t + 1) * 64] = mm(s3, cols(ref, 6 + j3)).astype(BF)
-
-
 def to_q_kernel(ids, q_ref, k_ref, v_ref, u_ref, xy_ref, own_ref, s1_ref, s2_ref, s3_ref, tmp):
-    x, y, q, r = xyqr(ids[0])
-    j5 = y & 1
-    s40, s41, s5 = pick(4, 0), pick(4, 1), pick(5, j5)
+    x, y, q, _ = xyqr(ids[0])
+    j3, j5 = 1 - (q & 1), y & 1
+    s3, s40, s41, s5 = pick(3, j3), pick(4, 0), pick(4, 1), pick(5, j5)
     for t, ref in enumerate((q_ref, k_ref, v_ref, u_ref)):
         tmp[0, t * 32 : (t + 1) * 32] = mm(s40, ref[:, 8 * D : 9 * D]).astype(BF)
         tmp[1, t * 32 : (t + 1) * 32] = mm(s41, ref[:, 9 * D : 10 * D]).astype(BF)
         tmp[2, t * 32 : t * 32 + 16] = mm(s5, cols(ref, 10 + j5)).astype(BF)
         tmp[2, t * 32 + 16 : t * 32 + 32] = xy_ref[x * 4 + (y ^ 1), 32 + t * 16 : 48 + t * 16]
+        s1_ref[128 + t * 64 : 192 + t * 64] = mm(s3, cols(ref, 6 + j3)).astype(BF)
     want = xy_col(x, y, iota((128, 256), 0))
     perm = onehot(want == iota((128, 256), 1))
     tmp[3] = mm(perm, xy_ref[:, 0:32].reshape(256, D)).astype(BF)
     for v, ref in enumerate((own_ref, s1_ref, s2_ref, s3_ref)):
-        ref[...] = tmp[q ^ v]
-
-
-def to_r_kernel(ids, q_ref, k_ref, v_ref, u_ref, g3_ref, q0, q1, q2, q3, own_ref, t1_ref, t2_ref, t3_ref, tmp):
-    x, y, q, r = xyqr(ids[0])
+        ref[0:128] = tmp[q ^ v]
+
+
+def to_r_kernel(ids, q_ref, k_ref, v_ref, u_ref, q0, q1, q2, q3, own_ref, t1_ref, t2_ref, t3_ref, tmp):
+    _, _, q, r = xyqr(ids[0])
     j3 = q & 1
     h1 = 3 - (r & 1)
     s3 = pick(3, j3)
@@ -114,7 +108,7 @@
         tmp[0, lo : lo + 128] = ref[:, 4 * D : 5 * D]
         tmp[1, lo : lo + 128] = ref[:, 5 * D : 6 * D]
         tmp[2, lo : lo + 64] = mm(s3, cols(ref, 6 + j3)).astype(BF)
-        tmp[2, lo + 64 : lo + 128] = g3_ref[t * 64 : (t + 1) * 64]
+        tmp[2, lo + 64 : lo + 128] = q1[128 + t * 64 : 192 + t * 64]
         for v, src in enumerate((q0, q1, q2, q3)):
             tmp[3, lo + v * 32 : lo + v * 32 + 32] = src[t * 32 : (t + 1) * 32]
         t1_ref[512 + lo : 640 + lo] = cols(ref, h1)
@@ -149,36 +143,52 @@
     return outs, dqs, part(dk), part(dv), term * (1.0 / math.sqrt(D))
 
 
-def doc_onehot(pos, bounds_ref):
-    return onehot((pos >= bounds_ref[0:1]) & (pos < bounds_ref[1:2]))
+def doc_bounds(sizes):
+    lane = iota((1, 128), 1)
+    first, end = jnp.zeros((1, 128), jnp.int32), jnp.zeros((1, 128), jnp.int32)
+    at = jnp.int32(0)
+    for c in range(8):
+        nxt = at + sizes[c] if c < 7 else jnp.int32(1 << 30)
+        first, end = jnp.where(lane == c, at, first), jnp.where(lane == c, nxt, end)
+        at = nxt
+    return first, end
+
+
+def doc_onehot(pos, bounds):
+    return onehot((pos >= bounds[0]) & (pos < bounds[1]))
 
 
 def at_lane(term, head):
     return jnp.where(iota((1, 128), 1) == head, term, 0.0)
 
 
-def near_kernel(ids, sharp, q_ref, k_ref, v_ref, u_ref, bounds_ref, g1_ref, z0_ref, own_ref, back_ref, terms_ref):
-    dev = ids[0]
-    x, y, q, r = xyqr(dev)
-    row = iota((128, 128), 0)
-    here = doc_onehot(dev * 128 + row, bounds_ref)
-    there = doc_onehot((dev ^ 1) * 128 + row, bounds_ref)
-    inv = 1.0 / math.sqrt(D)
-    refs = (q_ref, k_ref, v_ref, u_ref)
+def local_kernel(ids, sharp, sizes, q_ref, k_ref, v_ref, u_ref, z0_ref, terms_ref):
+    here = doc_onehot(ids[0] * 128 + iota((128, 128), 0), doc_bounds(sizes))
     total = jnp.zeros((1, 128), F32)
     for h in range(2):
-        blocks = [[ref[:, h * D : (h + 1) * D]] for ref in refs]
-        *res, term = attention(*blocks, [here], sharp[h] * inv)
+        blocks = [[ref[:, h * D : (h + 1) * D]] for ref in (q_ref, k_ref, v_ref, u_ref)]
+        *res, term = attention(*blocks, [here], sharp[h] * (1.0 / math.sqrt(D)))
         for t in range(4):
             z0_ref[t * 128 : (t + 1) * 128, h * D : (h + 1) * D] = res[t][0]
         total += at_lane(term, h)
+    terms_ref[...] = jnp.broadcast_to(total, (8, 128))
+
+
+def near_kernel(ids, sharp, sizes, q_ref, k_ref, v_ref, u_ref, g1_ref, before_ref, own_ref, back_ref, terms_ref):
+    dev = ids[0]
+    _, _, _, r = xyqr(dev)
+    row = iota((128, 128), 0)
+    bounds = doc_bounds(sizes)
+    here = doc_onehot(dev * 128 + row, bounds)
+    there = doc_onehot((dev ^ 1) * 128 + row, bounds)
+    refs = (q_ref, k_ref, v_ref, u_ref)
     h = 2 + (r & 1)
     blocks = [[cols(ref, h), g1_ref[512 + t * 128 : 640 + t * 128]] for t, ref in enumerate(refs)]
-    *res, term = attention(*blocks, [here, there], sharp[h] * inv)
+    *res, term = attention(*blocks, [here, there], sharp[h] * (1.0 / math.sqrt(D)))
     for t in range(4):
         own_ref[t * 128 : (t + 1) * 128] = res[t][0]
         back_ref[t * 128 : (t + 1) * 128] = res[t][1]
-    terms_ref[...] = jnp.broadcast_to(total + at_lane(term, h), (8, 128))
+    terms_ref[...] = before_ref[...] + jnp.broadcast_to(at_lane(term, h), (8, 128))
 
 
 def pieces(v):
@@ -189,11 +199,10 @@
     return jnp.where(row == 0, hi, jnp.where(row == 1, mid, jnp.where(row == 2, lo, 0.0))).astype(BF)
 
 
-def task_kernel(ids, sharp, i0, i1, i2, i3, bounds_ref, terms_ref, back_ref, o0, o1, o2, o3):
+def task_kernel(ids, sharp, sizes, i0, i1, i2, i3, terms_ref, back_ref, o0, o1, o2, o3):
     ins, outs = (i0, i1, i2, i3), (o0, o1, o2, o3)
     x, y, q, r = xyqr(ids[0])
     m = iota((128, 128), 0)
-    j4, j5 = q, y & 1
     near, r3 = r < 2, r == 2
     far = r == 3
     q3 = q == 3
@@ -207,7 +216,8 @@
     offset = (5 + j * (dil >> 1)) & (dil - 1)
     i_m = m & (jnp.right_shift(128, sh) - 1)
     low = (x_m * 64 + y_m * 16 + u_m * 4) * 128 + i_m * dil + offset
-    docs = [doc_onehot(low + (r ^ v) * 128, bounds_ref) for v in range(4)]
+    bounds = doc_bounds(sizes)
+    docs = [doc_onehot(low + (r ^ v) * 128, bounds) for v in range(4)]
     head = level * 2 + j
     blocks = [[ref[t * 128 : (t + 1) * 128] for ref in ins] for t in range(4)]
     *res, term = attention(*blocks, docs, sharp[head] * (1.0 / math.sqrt(D)))
@@ -225,7 +235,7 @@
 
 
 def from_r_kernel(ids, i0, i1, i2, i3, own_ref, p1_ref, p2_ref, p3_ref):
-    x, y, q, r = xyqr(ids[0])
+    _, _, _, r = xyqr(ids[0])
     ins, outs = (i0, i1, i2, i3), (own_ref, p1_ref, p2_ref, p3_ref)
     for v, ref in enumerate(ins):
 
@@ -246,7 +256,7 @@
 
 
 def from_q_kernel(ids, i0, i1, i2, i3, g5_ref, out_ref):
-    x, y, q, r = xyqr(ids[0])
+    x, y, q, _ = xyqr(ids[0])
     dp = ids[1]
     ins = (i0, i1, i2, i3)
     want = xy_col(x, y, iota((256, 128), 1))
@@ -279,7 +289,7 @@
 
 
 def unpack_low_kernel(ids, z0_ref, own_ref, r0, r1, r2, r3, q1, o_ref, dq_ref, dk_ref, dv_ref):
-    x, y, q, r = xyqr(ids[0])
+    _, _, q, r = xyqr(ids[0])
     res = (o_ref, dq_ref, dk_ref, dv_ref)
     j1, j3 = r & 1, q & 1
     w3b = spread(3, 1 - j3)
@@ -305,7 +315,7 @@
 
 
 def unpack_high_kernel(ids, l0, l1, l2, l3, q0, q1, q2, q3, g5_ref, xy_ref, o_ref, dq_ref, dk_ref, dv_ref, terms_ref):
-    x, y, q, r = xyqr(ids[0])
+    x, y, q, _ = xyqr(ids[0])
     dp = ids[1]
     res = (o_ref, dq_ref, dk_ref, dv_ref)
     j5 = y & 1
@@ -336,7 +346,7 @@
     acc = xy_ref[0, 32:48].astype(F32)
     for d in range(1, 32):
         acc += xy_ref[d, 32:48].astype(F32)
-    terms_ref[...] = jnp.broadcast_to(jnp.sum(acc, axis=0, keepdims=True), (8, 128))
+    terms_ref[...] = jnp.sum(acc, axis=0, keepdims=True)[:, :16]
 
 
 SMEM = pl.BlockSpec(memory_space=pltpu.SMEM)
@@ -348,18 +358,19 @@
     return pltpu.with_memory_space_constraint(array, pltpu.VMEM)
 
 
-def call(kernel, outs, scalars, params, rest, name, scratch=(), out_space=pltpu.VMEM):
+def call(kernel, outs, scalars, params, rest, scratch=(), out_space=pltpu.VMEM):
     shapes = [out_space(s, d) for s, d in outs]
     single = len(shapes) == 1
-    return pl.pallas_call(
+    run = pl.pallas_call(
         kernel,
         in_specs=[SMEM] * len(scalars) + [VMEM] * (len(params) + len(rest)),
         out_specs=VMEM if single else [VMEM] * len(shapes),
         out_shape=shapes[0] if single else shapes,
         scratch_shapes=list(scratch),
         compiler_params=LIMIT,
-        name=name,
-    )(*scalars, *params, *[stay(a) for a in rest])
+    )
+    args = [*params, *[stay(a) for a in rest]]
+    return run(*scalars, *args)
 
 
 def swap(array, axis, v):
@@ -378,40 +389,31 @@
         out_shape=jax.ShapeDtypeStruct((8, 96, D), BF),
         compiler_params=LIMIT,
         name="pack",
-    )(ids, *raw)
+    )(ids, *[pltpu.with_memory_space_constraint(a, pltpu.HBM) for a in raw])
     xy = lax.all_to_all(xy, ("x", "y"), 0, 0)
     four = [stay(a) for a in raw]
-    ends = jnp.cumsum(reply_list_sizes[0])
-    n_docs = ends.shape[0]
-    starts = jnp.concatenate([jnp.zeros((1,), jnp.int32), ends[:-1]])
-    ends = jnp.concatenate([ends[:-1], jnp.full((1,), 1 << 30, jnp.int32)])
-    bounds = jnp.pad(jnp.stack([starts, ends]), ((0, 6), (0, 128 - n_docs)))
-
-    g3 = swap(call(pairs_kernel, [block(256)], [ids], four, [], "pairs"), "q", 1)
+    sizes = reply_list_sizes[0]
+    z0, terms = call(local_kernel, [((512, 2 * D), BF), ((8, 128), F32)], [ids, learned_sharpness, sizes], four, [])
     q0, q1, q2, q3 = call(
-        to_q_kernel, [block(128)] * 4, [ids], four, [xy], "to_q", [pltpu.VMEM((4, 128, D), BF)]
+        to_q_kernel, [block(128), block(384), block(128), block(128)], [ids], four, [xy], [pltpu.VMEM((4, 128, D), BF)]
     )
     q2, q1, q3 = swap(q2, "q", 2), swap(q1, "q", 1), swap(q3, "q", 3)
     r0, r1, r2, r3 = call(
-        to_r_kernel, [block(512), block(1024), block(512), block(512)], [ids], four, [g3, q0, q1, q2, q3], "to_r",
+        to_r_kernel, [block(512), block(1024), block(512), block(512)], [ids], four, [q0, q1, q2, q3],
         [pltpu.VMEM((4, 512, D), BF)],
     )
     r1, r3, r2 = swap(r1, "r", 1), swap(r3, "r", 3), swap(r2, "r", 2)
-    z0, own1, back1, terms = call(
-        near_kernel,
-        [((512, 2 * D), BF), block(512), block(512), ((8, 128), F32)],
-        [ids, learned_sharpness], four, [bounds, r1], "near",
+    own1, back1, terms = call(
+        near_kernel, [block(512), block(512), ((8, 128), F32)], [ids, learned_sharpness, sizes], four, [r1, terms]
     )
     r0, r1, r2, r3 = call(
-        task_kernel, [block(528), block(1040), block(528), block(528)], [ids, learned_sharpness], [],
-        [r0, r1, r2, r3, bounds, terms, back1], "task",
+        task_kernel, [block(528), block(1040), block(528), block(528)], [ids, learned_sharpness, sizes], [],
+        [r0, r1, r2, r3, terms, back1],
     )
     r3, r2, r1 = swap(r3, "r", 3), swap(r2, "r", 2), swap(r1, "r", 1)
-    q0, q1, q2, q3 = call(
-        from_r_kernel, [block(144), block(400), block(144), block(144)], [ids], [], [r0, r1, r2, r3], "from_r"
-    )
+    q0, q1, q2, q3 = call(from_r_kernel, [block(144), block(400), block(144), block(144)], [ids], [], [r0, r1, r2, r3])
     q2, q1, q3 = swap(q2, "q", 2), swap(q1, "q", 1), swap(q3, "q", 3)
-    back5, xy = call(from_q_kernel, [block(64), ((32, 48, D), BF)], [ids], [], [q0, q1, q2, q3], "from_q")
+    back5, xy = call(from_q_kernel, [block(64), ((32, 48, D), BF)], [ids], [], [q0, q1, q2, q3])
     xy = lax.all_to_all(xy, ("x", "y", "dp"), 0, 0)
     back5 = swap(back5, "y", 1)
     half = lambda i: pl.BlockSpec((128, 8 * D), lambda _: (0, i))
@@ -431,13 +433,13 @@
         unpack_high_kernel,
         grid=(1,),
         in_specs=[SMEM] + [pl.BlockSpec(memory_space=pl.ANY)] * 4 + [VMEM] * len(args),
-        out_specs=[half(1)] * 4 + [pl.BlockSpec((8, 128), lambda _: (0, 0))],
-        out_shape=[result] * 4 + [jax.ShapeDtypeStruct((8, 128), F32)],
+        out_specs=[half(1)] * 4 + [pl.BlockSpec((1, 16), lambda _: (0, 0))],
+        out_shape=[result] * 4 + [jax.ShapeDtypeStruct((1, 16), F32)],
         input_output_aliases={1: 0, 2: 1, 3: 2, 4: 3},
         compiler_params=LIMIT,
         name="unpack_high",
     )(ids, *outs, *[stay(a) for a in args])
-    return (*[o[None] for o in outs], terms[0, :16])
+    return (*[o[None] for o in outs], terms[0])
 
 
 def solution(mesh):

time: 134 us -> 127 us (0.948)
  starting transfers between devices: 87.2 us -> 70 us
  blocking collectives: 0 us -> 14.6 us
  local copies, waits for them, and re-layouts: 5.33 us -> 0.03 us
  waiting for transfers between devices: 21.5 us -> 23.2 us
    all_to_all x0 -> x1, blocking collectives: none -> 14.6 us  [body(): xy = lax.all_to_all(xy, ('x', 'y'), 0, 0)]
    all_to_all x1 -> x0, starting transfers between devices: 7.47 us -> none  [body(): xy = lax.all_to_all(xy, ('x', 'y'), 0, 0)]
    ppermute x14 -> x13, starting transfers between devices: 65.9 us -> 60.1 us  [swap(): return lax.ppermute(array, axis, [(i, i ^ v) for i in range(4)])]
    unnamed x20 -> x12, local copies, waits for them, and re-layouts: 4.81 us -> 0.03 us
    all_to_all x1, starting transfers between devices: 13.8 us -> 9.88 us  [body(): xy = lax.all_to_all(xy, ('x', 'y', 'dp'), 0, 0)]
    ppermute x14 -> x13, waiting for transfers between devices: 17 us -> 18.6 us  [swap(): return lax.ppermute(array, axis, [(i, i ^ v) for i in range(4)])]
  transfers between devices with their start and end apart: 16 -> 14, of which waited for: 8 -> 6; matrix products, arithmetic and copies ran while one was open for 0% -> 0% of each run, Pallas kernels for 5% -> 5%
where the time goes in v3:
time: 127 us; the launch traced here: 126 us
  starting transfers between devices  70 us (55%)
  waiting for transfers between devices  23.2 us (18%)
  Pallas kernels  17.1 us (13%)
  blocking collectives  14.6 us (11%)
    ppermute x13, starting transfers between devices, swap(): return lax.ppermute(array, axis, [(i, i ^ v) for i in range(4)])  60.1 us
    ppermute x13, waiting for transfers between devices, swap(): return lax.ppermute(array, axis, [(i, i ^ v) for i in range(4)])  18.6 us
    all_to_all x1, blocking collectives, body(): xy = lax.all_to_all(xy, ('x', 'y'), 0, 0)  14.6 us
    pallas_call x7, Pallas kernels, call(): return run(*scalars, *args)  11.1 us
    all_to_all x1, starting transfers between devices, body(): xy = lax.all_to_all(xy, ('x', 'y', 'dp'), 0, 0)  9.88 us
    all_to_all x1, waiting for transfers between devices, body(): xy = lax.all_to_all(xy, ('x', 'y', 'dp'), 0, 0)  4.54 us
  transfers between devices with their start and end apart: 14, of which 6 were waited for; matrix products, arithmetic and copies ran while one was open for 0% of the time, Pallas kernels for 5%

profile of v3, /device:TPU:1, one launch (start us, length us, event | category | flops | bytes accessed | tf_op | source)
XLA Modules:
  0.0 125.8 jit_solution(13173166089167781699)
XLA Ops:
  0.6 0.1 pad_add_fusion.ids
  0.7 0.0 copy-start
  0.7 0.0 copy-start.1
  0.7 0.0 copy-start.2
  0.7 0.0 copy-start.3
  0.7 1.6 %pack.1 = bf16[8,96,128]{2,1,0:T(8,128)(2,1)S(1)} custom-call(s32[2]{0:T(128)S(1)} %pad_add_fusion.ids, bf16[128,2048]{1,0:T(8,128)(2,1)} %bitcast.12, bf16[128,2048]{1,0:T(8,128)(2,1)} %bitcast.17, bf16[128,2048]{1,0:T(8,128)(2,1)} %bitcast.22, bf16[128,2048]{1,0:T(8,128)(2,1)} %bitcast.27), custom_call_target="tpu_custom_call" | custom-call | tf_op jit(solution)/shard_map/pack/pallas_call | solution.py:384
  2.4 14.6 %all_to_all.10.xy_ref = bf16[8,96,128]{2,1,0:T(8,128)(2,1)S(1)} all-to-all(bf16[8,96,128]{2,1,0:T(8,128)(2,1)S(1)} %pack.1), channel_id=1, replica_groups=mesh['x'=2,'y'=4,'q'=4,'r'=4,'dp'=4] {'x','y'}, dimensions={0} | all-to-all | bytes 393216 | tf_op jit(solution)/shard_map/all_to_all | solution.py:393
  17.0 0.0 copy-done
  17.0 0.0 copy-done.1
  17.0 0.0 copy-done.2
  17.0 0.0 copy-done.3
  17.0 0.8 shard_map.102
  17.8 8.8 %collective-permute-start = (bf16[384,128]{1,0:T(8,128)(2,1)S(1)}, bf16[384,128]{1,0:T(8,128)(2,1)S(1)}, u32[]{:S(2)}, u32[]{:S(2)}) collective-permute-start(bf16[384,128]{1,0:T(8,128)(2,1)S(1)} %get-tuple-element.39), channel_id=1, source_target_pairs={{0,16},{16,0},{32,48},{48,32},{1,17},{17,1},{33,49},{49,33},{2,18}... | collective-permute-start | bytes 294920 | tf_op jit(solution)/shard_map/ppermute | solution.py:377
  26.6 10.6 %collective-permute-start.1 = (bf16[128,128]{1,0:T(8,128)(2,1)S(1)}, bf16[128,128]{1,0:T(8,128)(2,1)S(1)}, u32[]{:S(2)}, u32[]{:S(2)}) collective-permute-start(bf16[128,128]{1,0:T(8,128)(2,1)S(1)} %get-tuple-element.40), channel_id=1, source_target_pairs={{0,32},{16,48},{32,0},{48,16},{1,33},{17,49},{33,1},{49,17},{2,34}... | collective-permute-start | bytes 98312 | tf_op jit(solution)/shard_map/ppermute | solution.py:377
  37.3 1.9 %collective-permute-start.2 = (bf16[128,128]{1,0:T(8,128)(2,1)S(1)}, bf16[128,128]{1,0:T(8,128)(2,1)S(1)}, u32[]{:S(2)}, u32[]{:S(2)}) collective-permute-start(bf16[128,128]{1,0:T(8,128)(2,1)S(1)} %get-tuple-element.41), channel_id=1, source_target_pairs={{0,48},{16,32},{32,16},{48,0},{1,49},{17,33},{33,17},{49,1},{2,50}... | collective-permute-start | bytes 98312 | tf_op jit(solution)/shard_map/ppermute | solution.py:377
  39.2 1.2 collective-permute-done.1.q2
  40.4 5.6 %collective-permute-done.2.q3 = bf16[128,128]{1,0:T(8,128)(2,1)S(1)} collective-permute-done((bf16[128,128]{1,0:T(8,128)(2,1)S(1)}, bf16[128,128]{1,0:T(8,128)(2,1)S(1)}, u32[]{:S(2)}, u32[]{:S(2)}) %collective-permute-start.2) | collective-permute-done | bytes 32800 | tf_op jit(solution)/shard_map/ppermute | solution.py:377
  46.0 0.0 collective-permute-done.q1
  46.0 0.8 shard_map.103
  46.8 2.5 %collective-permute-start.3 = (bf16[1024,128]{1,0:T(8,128)(2,1)S(1)}, bf16[1024,128]{1,0:T(8,128)(2,1)S(1)}, u32[]{:S(2)}, u32[]{:S(2)}) collective-permute-start(bf16[1024,128]{1,0:T(8,128)(2,1)S(1)} %get-tuple-element.42), channel_id=1, source_target_pairs={{0,4},{4,0},{8,12},{12,8},{1,5},{5,1},{9,13},{13,9},{2,6},{6,2},{1... | collective-permute-start | bytes 786440 | tf_op jit(solution)/shard_map/ppermute | solution.py:377
  49.3 3.4 %collective-permute-start.4 = (bf16[512,128]{1,0:T(8,128)(2,1)S(1)}, bf16[512,128]{1,0:T(8,128)(2,1)S(1)}, u32[]{:S(2)}, u32[]{:S(2)}) collective-permute-start(bf16[512,128]{1,0:T(8,128)(2,1)S(1)} %get-tuple-element.46), channel_id=1, source_target_pairs={{0,8},{4,12},{8,0},{12,4},{1,9},{5,13},{9,1},{13,5},{2,10},{6,14},... | collective-permute-start | bytes 393224 | tf_op jit(solution)/shard_map/ppermute | solution.py:377
  52.7 0.0 copy-start.4
  52.7 0.0 copy-start.5
  52.7 3.4 %collective-permute-start.5 = (bf16[512,128]{1,0:T(8,128)(2,1)S(1)}, bf16[512,128]{1,0:T(8,128)(2,1)S(1)}, u32[]{:S(2)}, u32[]{:S(2)}) collective-permute-start(bf16[512,128]{1,0:T(8,128)(2,1)S(1)} %get-tuple-element.47), channel_id=1, source_target_pairs={{0,12},{4,8},{8,4},{12,0},{1,13},{5,9},{9,5},{13,1},{2,14},{6,10},... | collective-permute-start | bytes 393224 | tf_op jit(solution)/shard_map/ppermute | solution.py:377
  56.1 0.0 copy-done.4
  56.1 0.0 copy-done.5
  56.1 1.9 %shard_map.101 = (bf16[512,256]{1,0:T(8,128)(2,1)S(1)}, f32[8,128]{1,0:T(8,128)S(1)}) custom-call(s32[2]{0:T(128)S(1)} %pad_add_fusion.ids, f32[16]{0:T(128)S(1)} %copy-done.4, s32[8]{0:T(128)S(1)} %bitcast.32, bf16[128,2048]{1,0:T(8,128)(2,1)S(1)} %bitcast.15, bf16[128,2048]{1,0:T(8,128)(2,1)S(1)} %bitcast.20, bf16[128,2048]{1,0:T(8,128)(2,1)S(1)} %bitcast.25, ...), custom_call_target="tpu_custom_call" | custom-call | tf_op jit(solution)/shard_map/pallas_call | solution.py:373
  58.0 0.0 collective-permute-done.3.g1_ref.i1
  58.1 1.9 %shard_map.104 = (bf16[512,128]{1,0:T(8,128)(2,1)S(1)}, bf16[512,128]{1,0:T(8,128)(2,1)S(1)}, f32[8,128]{1,0:T(8,128)S(1)}) custom-call(s32[2]{0:T(128)S(1)} %pad_add_fusion.ids, f32[16]{0:T(128)S(1)} %copy-done.4, s32[8]{0:T(128)S(1)} %bitcast.33, bf16[128,2048]{1,0:T(8,128)(2,1)S(1)} %bitcast.16, bf16[128,2048]{1,0:T(8,128)(2,1)S(1)} %bitcast.21, ...), custom_call_target="tpu_custom_call" | custom-call | tf_op jit(solution)/shard_map/pallas_call | solution.py:373
  59.9 0.0 collective-permute-done.4.i2
  59.9 1.8 %collective-permute-done.5.i3 = bf16[512,128]{1,0:T(8,128)(2,1)S(1)} collective-permute-done((bf16[512,128]{1,0:T(8,128)(2,1)S(1)}, bf16[512,128]{1,0:T(8,128)(2,1)S(1)}, u32[]{:S(2)}, u32[]{:S(2)}) %collective-permute-start.5) | collective-permute-done | bytes 131104 | tf_op jit(solution)/shard_map/ppermute | solution.py:377
  61.7 3.6 %shard_map.105 = (bf16[528,128]{1,0:T(8,128)(2,1)S(1)}, bf16[1040,128]{1,0:T(8,128)(2,1)S(1)}, bf16[528,128]{1,0:T(8,128)(2,1)S(1)}, bf16[528,128]{1,0:T(8,128)(2,1)S(1)}) custom-call(s32[2]{0:T(128)S(1)} %pad_add_fusion.ids, f32[16]{0:T(128)S(1)} %copy-done.4, s32[8]{0:T(128)S(1)} %bitcast.34, bf16[512,128]{1,0:T(8,128)(2,1)S(1)} %get-tuple-element.45.i0, ...), custom_call_target="tpu_custom_call" | custom-call | tf_op jit(solution)/shard_map/pallas_call | solution.py:373
  65.3 1.9 %collective-permute-start.6 = (bf16[1040,128]{1,0:T(8,128)(2,1)S(1)}, bf16[1040,128]{1,0:T(8,128)(2,1)S(1)}, u32[]{:S(2)}, u32[]{:S(2)}) collective-permute-start(bf16[1040,128]{1,0:T(8,128)(2,1)S(1)} %get-tuple-element.51), channel_id=1, source_target_pairs={{0,4},{4,0},{8,12},{12,8},{1,5},{5,1},{9,13},{13,9},{2,6},{6,2},{1... | collective-permute-start | bytes 798728 | tf_op jit(solution)/shard_map/ppermute | solution.py:377
  67.2 3.7 %collective-permute-start.7 = (bf16[528,128]{1,0:T(8,128)(2,1)S(1)}, bf16[528,128]{1,0:T(8,128)(2,1)S(1)}, u32[]{:S(2)}, u32[]{:S(2)}) collective-permute-start(bf16[528,128]{1,0:T(8,128)(2,1)S(1)} %get-tuple-element.52), channel_id=1, source_target_pairs={{0,8},{4,12},{8,0},{12,4},{1,9},{5,13},{9,1},{13,5},{2,10},{6,14},... | collective-permute-start | bytes 405512 | tf_op jit(solution)/shard_map/ppermute | solution.py:377
  70.9 3.7 %collective-permute-start.8 = (bf16[528,128]{1,0:T(8,128)(2,1)S(1)}, bf16[528,128]{1,0:T(8,128)(2,1)S(1)}, u32[]{:S(2)}, u32[]{:S(2)}) collective-permute-start(bf16[528,128]{1,0:T(8,128)(2,1)S(1)} %get-tuple-element.53), channel_id=1, source_target_pairs={{0,12},{4,8},{8,4},{12,0},{1,13},{5,9},{9,5},{13,1},{2,14},{6,10},... | collective-permute-start | bytes 405512 | tf_op jit(solution)/shard_map/ppermute | solution.py:377
  74.6 0.0 collective-permute-done.7.i2.r2
  74.6 5.3 %collective-permute-done.8.i3.r3 = bf16[528,128]{1,0:T(8,128)(2,1)S(1)} collective-permute-done((bf16[528,128]{1,0:T(8,128)(2,1)S(1)}, bf16[528,128]{1,0:T(8,128)(2,1)S(1)}, u32[]{:S(2)}, u32[]{:S(2)}) %collective-permute-start.8) | collective-permute-done | bytes 135200 | tf_op jit(solution)/shard_map/ppermute | solution.py:377
  79.9 0.0 collective-permute-done.6.i1.r1
  79.9 0.6 shard_map.106
  80.6 8.1 %collective-permute-start.9 = (bf16[400,128]{1,0:T(8,128)(2,1)S(1)}, bf16[400,128]{1,0:T(8,128)(2,1)S(1)}, u32[]{:S(2)}, u32[]{:S(2)}) collective-permute-start(bf16[400,128]{1,0:T(8,128)(2,1)S(1)} %get-tuple-element.54), channel_id=1, source_target_pairs={{0,16},{16,0},{32,48},{48,32},{1,17},{17,1},{33,49},{49,33},{2,18}... | collective-permute-start | bytes 307208 | tf_op jit(solution)/shard_map/ppermute | solution.py:377
  88.7 2.8 %collective-permute-start.10 = (bf16[144,128]{1,0:T(8,128)(2,1)S(1)}, bf16[144,128]{1,0:T(8,128)(2,1)S(1)}, u32[]{:S(2)}, u32[]{:S(2)}) collective-permute-start(bf16[144,128]{1,0:T(8,128)(2,1)S(1)} %get-tuple-element.60), channel_id=1, source_target_pairs={{0,32},{16,48},{32,0},{48,16},{1,33},{17,49},{33,1},{49,17},{2,34}... | collective-permute-start | bytes 110600 | tf_op jit(solution)/shard_map/ppermute | solution.py:377
  91.5 6.1 %collective-permute-start.11 = (bf16[144,128]{1,0:T(8,128)(2,1)S(1)}, bf16[144,128]{1,0:T(8,128)(2,1)S(1)}, u32[]{:S(2)}, u32[]{:S(2)}) collective-permute-start(bf16[144,128]{1,0:T(8,128)(2,1)S(1)} %get-tuple-element.61), channel_id=1, source_target_pairs={{0,48},{16,32},{32,16},{48,0},{1,49},{17,33},{33,17},{49,1},{2,50}... | collective-permute-start | bytes 110600 | tf_op jit(solution)/shard_map/ppermute | solution.py:377
  97.6 4.7 %collective-permute-done.10.i2.q2 = bf16[144,128]{1,0:T(8,128)(2,1)S(1)} collective-permute-done((bf16[144,128]{1,0:T(8,128)(2,1)S(1)}, bf16[144,128]{1,0:T(8,128)(2,1)S(1)}, u32[]{:S(2)}, u32[]{:S(2)}) %collective-permute-start.10) | collective-permute-done | bytes 36896 | tf_op jit(solution)/shard_map/ppermute | solution.py:377
  102.3 0.0 collective-permute-done.11.i3.q3
  102.3 0.0 collective-permute-done.9.q1.i1
  102.3 1.5 %shard_map.107 = (bf16[64,128]{1,0:T(8,128)(2,1)S(1)}, bf16[32,48,128]{2,1,0:T(8,128)(2,1)}) custom-call(s32[2]{0:T(128)S(1)} %pad_add_fusion.ids, bf16[144,128]{1,0:T(8,128)(2,1)S(1)} %get-tuple-element.59.i0.q0, bf16[400,128]{1,0:T(8,128)(2,1)S(1)} %collective-permute-done.9.q1.i1, bf16[144,128]{1,0:T(8,128)(2,1)S(1)} %collective-permute-done.10.i2.q2, ...), custom_call_target="tpu_custom_call" | custom-call | tf_op jit(solution)/shard_map/pallas_call | solution.py:373
  103.8 9.9 %all-to-all-start.1 = ((bf16[32,48,128]{2,1,0:T(8,128)(2,1)}), bf16[32,48,128]{2,1,0:T(8,128)(2,1)S(1)}, u32[]{:S(2)}, u32[]{:S(2)}) async-start(bf16[32,48,128]{2,1,0:T(8,128)(2,1)} %get-tuple-element.63), calls=%async_computation.1 | async-start | bytes 786432 | tf_op jit(solution)/shard_map/all_to_all | solution.py:417
  113.7 3.3 %collective-permute-start.12 = (bf16[64,128]{1,0:T(8,128)(2,1)S(1)}, bf16[64,128]{1,0:T(8,128)(2,1)S(1)}, u32[]{:S(2)}, u32[]{:S(2)}) collective-permute-start(bf16[64,128]{1,0:T(8,128)(2,1)S(1)} %get-tuple-element.62), channel_id=1, source_target_pairs={{0,64},{64,0},{128,192},{192,128},{1,65},{65,1},{129,193},{193,129... | collective-permute-start | bytes 49160 | tf_op jit(solution)/shard_map/ppermute | solution.py:377
  117.0 2.0 %unpack_low.1 = (bf16[128,2048]{1,0:T(8,128)(2,1)}, bf16[128,2048]{1,0:T(8,128)(2,1)}, bf16[128,2048]{1,0:T(8,128)(2,1)}, bf16[128,2048]{1,0:T(8,128)(2,1)}) custom-call(s32[2]{0:T(128)S(1)} %pad_add_fusion.ids, bf16[512,256]{1,0:T(8,128)(2,1)S(1)} %get-tuple-element.37.z0_ref, bf16[512,128]{1,0:T(8,128)(2,1)S(1)} %get-tuple-element.44.own_ref, ...), custom_call_target="tpu_custom_call" | custom-call | tf_op jit(solution)/shard_map/unpack_low/pallas_call | solution.py:422
  119.0 0.0 collective-permute-done.12.g5_ref
  119.0 4.5 %all-to-all-done.1.xy_ref = bf16[32,48,128]{2,1,0:T(8,128)(2,1)S(1)} async-done(((bf16[32,48,128]{2,1,0:T(8,128)(2,1)}), bf16[32,48,128]{2,1,0:T(8,128)(2,1)S(1)}, u32[]{:S(2)}, u32[]{:S(2)}) %all-to-all-start.1) | async-done | bytes 393248 | tf_op jit(solution)/shard_map/all_to_all | solution.py:417
  123.5 2.3 %unpack_high.1 = (bf16[128,2048]{1,0:T(8,128)(2,1)}, bf16[128,2048]{1,0:T(8,128)(2,1)}, bf16[128,2048]{1,0:T(8,128)(2,1)}, bf16[128,2048]{1,0:T(8,128)(2,1)}, f32[1,16]{1,0:T(1,128)}) custom-call(s32[2]{0:T(128)S(1)} %pad_add_fusion.ids, ...), custom_call_target="tpu_custom_call", output_to_operand_aliasing={{0}: (1, {}), {1}: (2, {}), {2}: (3, {}), {3}: (4, {})} | custom-call | tf_op jit(solution)/shard_map/unpack_high/pallas_call | solution.py:432
Async XLA Ops:
  0.7 16.2 %copy-start = (bf16[1,128,2048]{2,1,0:T(8,128)(2,1)S(1)}, bf16[1,128,2048]{2,1,0:T(8,128)(2,1)}, u32[]{:S(2)}) copy-start(bf16[1,128,2048]{2,1,0:T(8,128)(2,1)} %param.6) | copy-start | bytes 1572868
  0.7 16.2 %copy-start.1 = (bf16[1,128,2048]{2,1,0:T(8,128)(2,1)S(1)}, bf16[1,128,2048]{2,1,0:T(8,128)(2,1)}, u32[]{:S(2)}) copy-start(bf16[1,128,2048]{2,1,0:T(8,128)(2,1)} %param.7) | copy-start | bytes 1572868
  0.7 16.2 %copy-start.2 = (bf16[1,128,2048]{2,1,0:T(8,128)(2,1)S(1)}, bf16[1,128,2048]{2,1,0:T(8,128)(2,1)}, u32[]{:S(2)}) copy-start(bf16[1,128,2048]{2,1,0:T(8,128)(2,1)} %param.8) | copy-start | bytes 1572868
  0.7 16.2 %copy-start.3 = (bf16[1,128,2048]{2,1,0:T(8,128)(2,1)S(1)}, bf16[1,128,2048]{2,1,0:T(8,128)(2,1)}, u32[]{:S(2)}) copy-start(bf16[1,128,2048]{2,1,0:T(8,128)(2,1)} %param.9) | copy-start | bytes 1572868
  17.8 28.2 %collective-permute-start = (bf16[384,128]{1,0:T(8,128)(2,1)S(1)}, bf16[384,128]{1,0:T(8,128)(2,1)S(1)}, u32[]{:S(2)}, u32[]{:S(2)}) collective-permute-start(bf16[384,128]{1,0:T(8,128)(2,1)S(1)} %get-tuple-element.39), channel_id=1, source_target_pairs={{0,16},{16,0},{32,48},{48,32},{1,17},{17,1},{33,49},{49,33},{2,18}... | collective-permute-start | bytes 294920 | tf_op jit(solution)/shard_map/ppermute | solution.py:377
  26.6 13.8 %collective-permute-start.1 = (bf16[128,128]{1,0:T(8,128)(2,1)S(1)}, bf16[128,128]{1,0:T(8,128)(2,1)S(1)}, u32[]{:S(2)}, u32[]{:S(2)}) collective-permute-start(bf16[128,128]{1,0:T(8,128)(2,1)S(1)} %get-tuple-element.40), channel_id=1, source_target_pairs={{0,32},{16,48},{32,0},{48,16},{1,33},{17,49},{33,1},{49,17},{2,34}... | collective-permute-start | bytes 98312 | tf_op jit(solution)/shard_map/ppermute | solution.py:377
  37.3 8.8 %collective-permute-start.2 = (bf16[128,128]{1,0:T(8,128)(2,1)S(1)}, bf16[128,128]{1,0:T(8,128)(2,1)S(1)}, u32[]{:S(2)}, u32[]{:S(2)}) collective-permute-start(bf16[128,128]{1,0:T(8,128)(2,1)S(1)} %get-tuple-element.41), channel_id=1, source_target_pairs={{0,48},{16,32},{32,16},{48,0},{1,49},{17,33},{33,17},{49,1},{2,50}... | collective-permute-start | bytes 98312 | tf_op jit(solution)/shard_map/ppermute | solution.py:377
  46.8 11.2 %collective-permute-start.3 = (bf16[1024,128]{1,0:T(8,128)(2,1)S(1)}, bf16[1024,128]{1,0:T(8,128)(2,1)S(1)}, u32[]{:S(2)}, u32[]{:S(2)}) collective-permute-start(bf16[1024,128]{1,0:T(8,128)(2,1)S(1)} %get-tuple-element.42), channel_id=1, source_target_pairs={{0,4},{4,0},{8,12},{12,8},{1,5},{5,1},{9,13},{13,9},{2,6},{6,2},{1... | collective-permute-start | bytes 786440 | tf_op jit(solution)/shard_map/ppermute | solution.py:377
  49.3 10.7 %collective-permute-start.4 = (bf16[512,128]{1,0:T(8,128)(2,1)S(1)}, bf16[512,128]{1,0:T(8,128)(2,1)S(1)}, u32[]{:S(2)}, u32[]{:S(2)}) collective-permute-start(bf16[512,128]{1,0:T(8,128)(2,1)S(1)} %get-tuple-element.46), channel_id=1, source_target_pairs={{0,8},{4,12},{8,0},{12,4},{1,9},{5,13},{9,1},{13,5},{2,10},{6,14},... | collective-permute-start | bytes 393224 | tf_op jit(solution)/shard_map/ppermute | solution.py:377
  52.7 3.5 %copy-start.4 = (f32[16]{0:T(128)S(1)}, f32[16]{0:T(128)}, u32[]{:S(2)}) copy-start(f32[16]{0:T(128)} %sharp.5) | copy-start | bytes 196
  52.7 3.5 %copy-start.5 = (s32[1,8]{1,0:T(1,128)S(1)}, s32[1,8]{1,0:T(1,128)}, u32[]{:S(2)}) copy-start(s32[1,8]{1,0:T(1,128)} %param.11) | copy-start | bytes 100
  52.7 9.0 %collective-permute-start.5 = (bf16[512,128]{1,0:T(8,128)(2,1)S(1)}, bf16[512,128]{1,0:T(8,128)(2,1)S(1)}, u32[]{:S(2)}, u32[]{:S(2)}) collective-permute-start(bf16[512,128]{1,0:T(8,128)(2,1)S(1)} %get-tuple-element.47), channel_id=1, source_target_pairs={{0,12},{4,8},{8,4},{12,0},{1,13},{5,9},{9,5},{13,1},{2,14},{6,10},... | collective-permute-start | bytes 393224 | tf_op jit(solution)/shard_map/ppermute | solution.py:377
  65.3 14.6 %collective-permute-start.6 = (bf16[1040,128]{1,0:T(8,128)(2,1)S(1)}, bf16[1040,128]{1,0:T(8,128)(2,1)S(1)}, u32[]{:S(2)}, u32[]{:S(2)}) collective-permute-start(bf16[1040,128]{1,0:T(8,128)(2,1)S(1)} %get-tuple-element.51), channel_id=1, source_target_pairs={{0,4},{4,0},{8,12},{12,8},{1,5},{5,1},{9,13},{13,9},{2,6},{6,2},{1... | collective-permute-start | bytes 798728 | tf_op jit(solution)/shard_map/ppermute | solution.py:377
  67.2 7.4 %collective-permute-start.7 = (bf16[528,128]{1,0:T(8,128)(2,1)S(1)}, bf16[528,128]{1,0:T(8,128)(2,1)S(1)}, u32[]{:S(2)}, u32[]{:S(2)}) collective-permute-start(bf16[528,128]{1,0:T(8,128)(2,1)S(1)} %get-tuple-element.52), channel_id=1, source_target_pairs={{0,8},{4,12},{8,0},{12,4},{1,9},{5,13},{9,1},{13,5},{2,10},{6,14},... | collective-permute-start | bytes 405512 | tf_op jit(solution)/shard_map/ppermute | solution.py:377
  70.9 9.0 %collective-permute-start.8 = (bf16[528,128]{1,0:T(8,128)(2,1)S(1)}, bf16[528,128]{1,0:T(8,128)(2,1)S(1)}, u32[]{:S(2)}, u32[]{:S(2)}) collective-permute-start(bf16[528,128]{1,0:T(8,128)(2,1)S(1)} %get-tuple-element.53), channel_id=1, source_target_pairs={{0,12},{4,8},{8,4},{12,0},{1,13},{5,9},{9,5},{13,1},{2,14},{6,10},... | collective-permute-start | bytes 405512 | tf_op jit(solution)/shard_map/ppermute | solution.py:377
  80.6 21.7 %collective-permute-start.9 = (bf16[400,128]{1,0:T(8,128)(2,1)S(1)}, bf16[400,128]{1,0:T(8,128)(2,1)S(1)}, u32[]{:S(2)}, u32[]{:S(2)}) collective-permute-start(bf16[400,128]{1,0:T(8,128)(2,1)S(1)} %get-tuple-element.54), channel_id=1, source_target_pairs={{0,16},{16,0},{32,48},{48,32},{1,17},{17,1},{33,49},{49,33},{2,18}... | collective-permute-start | bytes 307208 | tf_op jit(solution)/shard_map/ppermute | solution.py:377
  88.7 13.6 %collective-permute-start.10 = (bf16[144,128]{1,0:T(8,128)(2,1)S(1)}, bf16[144,128]{1,0:T(8,128)(2,1)S(1)}, u32[]{:S(2)}, u32[]{:S(2)}) collective-permute-start(bf16[144,128]{1,0:T(8,128)(2,1)S(1)} %get-tuple-element.60), channel_id=1, source_target_pairs={{0,32},{16,48},{32,0},{48,16},{1,33},{17,49},{33,1},{49,17},{2,34}... | collective-permute-start | bytes 110600 | tf_op jit(solution)/shard_map/ppermute | solution.py:377
  91.5 10.8 %collective-permute-start.11 = (bf16[144,128]{1,0:T(8,128)(2,1)S(1)}, bf16[144,128]{1,0:T(8,128)(2,1)S(1)}, u32[]{:S(2)}, u32[]{:S(2)}) collective-permute-start(bf16[144,128]{1,0:T(8,128)(2,1)S(1)} %get-tuple-element.61), channel_id=1, source_target_pairs={{0,48},{16,32},{32,16},{48,0},{1,49},{17,33},{33,17},{49,1},{2,50}... | collective-permute-start | bytes 110600 | tf_op jit(solution)/shard_map/ppermute | solution.py:377
  103.8 19.7 %all-to-all-start.1 = ((bf16[32,48,128]{2,1,0:T(8,128)(2,1)}), bf16[32,48,128]{2,1,0:T(8,128)(2,1)S(1)}, u32[]{:S(2)}, u32[]{:S(2)}) async-start(bf16[32,48,128]{2,1,0:T(8,128)(2,1)} %get-tuple-element.63), calls=%async_computation.1 | async-start | bytes 786432 | tf_op jit(solution)/shard_map/all_to_all | solution.py:417
  113.7 5.3 %collective-permute-start.12 = (bf16[64,128]{1,0:T(8,128)(2,1)S(1)}, bf16[64,128]{1,0:T(8,128)(2,1)S(1)}, u32[]{:S(2)}, u32[]{:S(2)}) collective-permute-start(bf16[64,128]{1,0:T(8,128)(2,1)S(1)} %get-tuple-element.62), channel_id=1, source_target_pairs={{0,64},{64,0},{128,192},{192,128},{1,65},{65,1},{129,193},{193,129... | collective-permute-start | bytes 49160 | tf_op jit(solution)/shard_map/ppermute | solution.py:377

commit v4 on v3

--- a/solution.py
+++ b/solution.py
@@ -60,11 +60,15 @@
     return jnp.where(y < 2, six, jnp.where(y == 2, seven, -1))
 
 
-def pack_kernel(ids, q_ref, k_ref, v_ref, u_ref, xy_ref):
-    x, y, _, _ = xyqr(ids[0])
+def pack_kernel(ids, q6_ref, k6_ref, v6_ref, u6_ref, q_ref, k_ref, v_ref, u_ref, g3_ref, xy_ref):
+    x, y, q, _ = xyqr(ids[0])
     srcs = (q_ref, k_ref, v_ref, u_ref)
     j5 = 1 - (y & 1)
     s5 = pick(5, j5)
+    j3 = 1 - (q & 1)
+    s3 = pick(3, j3)
+    for t, ref in enumerate((q6_ref, k6_ref, v6_ref, u6_ref)):
+        g3_ref[t * 64 : (t + 1) * 64] = mm(s3, cols(ref, j3)).astype(BF)
     xy_ref[...] = jnp.zeros(xy_ref.shape, BF)
     for t, ref in enumerate(srcs):
         xy_ref[x * 4 + (y ^ 1), 32 + t * 16 : 48 + t * 16] = mm(s5, cols(ref, 2 + j5)).astype(BF)
@@ -81,24 +85,21 @@
         xy_ref[j * 4 + 2, 0:32] = acc7.astype(BF)
 
 
-def to_q_kernel(ids, q_ref, k_ref, v_ref, u_ref, xy_ref, own_ref, s1_ref, s2_ref, s3_ref, tmp):
-    x, y, q, _ = xyqr(ids[0])
-    j3, j5 = 1 - (q & 1), y & 1
-    s3, s40, s41, s5 = pick(3, j3), pick(4, 0), pick(4, 1), pick(5, j5)
+def to_q_kernel(ids, q_ref, k_ref, v_ref, u_ref, xy_ref, out_ref):
+    x, y, _, _ = xyqr(ids[0])
+    j5 = y & 1
+    s40, s41, s5 = pick(4, 0), pick(4, 1), pick(5, j5)
     for t, ref in enumerate((q_ref, k_ref, v_ref, u_ref)):
-        tmp[0, t * 32 : (t + 1) * 32] = mm(s40, ref[:, 8 * D : 9 * D]).astype(BF)
-        tmp[1, t * 32 : (t + 1) * 32] = mm(s41, ref[:, 9 * D : 10 * D]).astype(BF)
-        tmp[2, t * 32 : t * 32 + 16] = mm(s5, cols(ref, 10 + j5)).astype(BF)
-        tmp[2, t * 32 + 16 : t * 32 + 32] = xy_ref[x * 4 + (y ^ 1), 32 + t * 16 : 48 + t * 16]
-        s1_ref[128 + t * 64 : 192 + t * 64] = mm(s3, cols(ref, 6 + j3)).astype(BF)
+        out_ref[0, t * 32 : (t + 1) * 32] = mm(s40, ref[:, 8 * D : 9 * D]).astype(BF)
+        out_ref[1, t * 32 : (t + 1) * 32] = mm(s41, ref[:, 9 * D : 10 * D]).astype(BF)
+        out_ref[2, t * 32 : t * 32 + 16] = mm(s5, cols(ref, 10 + j5)).astype(BF)
+        out_ref[2, t * 32 + 16 : t * 32 + 32] = xy_ref[x * 4 + (y ^ 1), 32 + t * 16 : 48 + t * 16]
     want = xy_col(x, y, iota((128, 256), 0))
     perm = onehot(want == iota((128, 256), 1))
-    tmp[3] = mm(perm, xy_ref[:, 0:32].reshape(256, D)).astype(BF)
-    for v, ref in enumerate((own_ref, s1_ref, s2_ref, s3_ref)):
-        ref[0:128] = tmp[q ^ v]
-
-
-def to_r_kernel(ids, q_ref, k_ref, v_ref, u_ref, q0, q1, q2, q3, own_ref, t1_ref, t2_ref, t3_ref, tmp):
+    out_ref[3] = mm(perm, xy_ref[:, 0:32].reshape(256, D)).astype(BF)
+
+
+def to_r_kernel(ids, q_ref, k_ref, v_ref, u_ref, g3_ref, qr_ref, own_ref, t1_ref, t2_ref, t3_ref, tmp):
     _, _, q, r = xyqr(ids[0])
     j3 = q & 1
     h1 = 3 - (r & 1)
@@ -108,9 +109,9 @@
         tmp[0, lo : lo + 128] = ref[:, 4 * D : 5 * D]
         tmp[1, lo : lo + 128] = ref[:, 5 * D : 6 * D]
         tmp[2, lo : lo + 64] = mm(s3, cols(ref, 6 + j3)).astype(BF)
-        tmp[2, lo + 64 : lo + 128] = q1[128 + t * 64 : 192 + t * 64]
-        for v, src in enumerate((q0, q1, q2, q3)):
-            tmp[3, lo + v * 32 : lo + v * 32 + 32] = src[t * 32 : (t + 1) * 32]
+        tmp[2, lo + 64 : lo + 128] = g3_ref[t * 64 : (t + 1) * 64]
+        for u in range(4):
+            tmp[3, lo + u * 32 : lo + u * 32 + 32] = qr_ref[u, t * 32 : (t + 1) * 32]
         t1_ref[512 + lo : 640 + lo] = cols(ref, h1)
     for v, ref in enumerate((own_ref, t1_ref, t2_ref, t3_ref)):
         ref[0:512] = tmp[r ^ v]
@@ -206,7 +207,7 @@
     near, r3 = r < 2, r == 2
     far = r == 3
     q3 = q == 3
-    u_m = jnp.where(near, q, q ^ jnp.where(r3, m >> 6, m >> 5))
+    u_m = jnp.where(near, q, jnp.where(r3, q ^ (m >> 6), m >> 5))
     y_m = jnp.where(far & (q == 2), y ^ ((m >> 4) & 1), jnp.where(far & q3, jnp.where(y < 2, (m >> 3) & 3, (m >> 2) & 3), y))
     x_m = jnp.where(far & q3 & (y >= 2), (m >> 4) & 1, x)
     level = jnp.where(near, 2, jnp.where(r3, 3, jnp.where(q < 2, 4, jnp.where(q == 2, 5, jnp.where(y < 2, 6, 7)))))
@@ -234,49 +235,41 @@
     return (a + b) + (c + d)
 
 
-def from_r_kernel(ids, i0, i1, i2, i3, own_ref, p1_ref, p2_ref, p3_ref):
+def from_r_kernel(ids, i0, i1, i2, i3, g3_ref, out_ref):
     _, _, _, r = xyqr(ids[0])
-    ins, outs = (i0, i1, i2, i3), (own_ref, p1_ref, p2_ref, p3_ref)
+    ins = (i0, i1, i2, i3)
     for v, ref in enumerate(ins):
 
         @pl.when((r ^ v) == 2)
         def _():
             for t in range(4):
-                p1_ref[144 + t * 64 : 208 + t * 64] = ref[t * 128 + 64 : t * 128 + 128]
+                g3_ref[t * 64 : (t + 1) * 64] = ref[t * 128 + 64 : t * 128 + 128]
 
         @pl.when((r ^ v) == 3)
         def _():
             for t in range(4):
-                for w, out in enumerate(outs):
-                    out[t * 32 : (t + 1) * 32] = ref[t * 128 + w * 32 : t * 128 + w * 32 + 32]
+                for u in range(4):
+                    out_ref[u, t * 32 : (t + 1) * 32] = ref[t * 128 + u * 32 : t * 128 + u * 32 + 32]
 
     extra = pieces(total4([ref[512:528] for ref in ins]))
-    for out in outs:
-        out[128:144] = extra
-
-
-def from_q_kernel(ids, i0, i1, i2, i3, g5_ref, out_ref):
-    x, y, q, _ = xyqr(ids[0])
+    for u in range(4):
+        out_ref[u, 128:144] = extra
+
+
+def from_q_kernel(ids, in_ref, g5_ref, out_ref):
+    x, y, _, _ = xyqr(ids[0])
     dp = ids[1]
-    ins = (i0, i1, i2, i3)
     want = xy_col(x, y, iota((256, 128), 1))
     perm = onehot(want == iota((256, 128), 0))
-    extra = pieces(total4([ref[128:144] for ref in ins]))
+    extra = pieces(total4([in_ref[u, 128:144] for u in range(4)]))
     for d in range(32):
         out_ref[d, 0:32] = jnp.zeros((32, D), BF)
         out_ref[d, 32:48] = extra
-    for v, ref in enumerate(ins):
-
-        @pl.when((q ^ v) == 2)
-        def _():
-            for t in range(4):
-                g5_ref[t * 16 : (t + 1) * 16] = ref[t * 32 + 16 : t * 32 + 32]
-
-        @pl.when((q ^ v) == 3)
-        def _():
-            rows = mm(perm, ref[0:128]).astype(BF)
-            for d in range(8):
-                out_ref[d * 4 + dp, 0:32] = rows[d * 32 : (d + 1) * 32]
+    for t in range(4):
+        g5_ref[t * 16 : (t + 1) * 16] = in_ref[2, t * 32 + 16 : t * 32 + 32]
+    rows = mm(perm, in_ref[3, 0:128]).astype(BF)
+    for d in range(8):
+        out_ref[d * 4 + dp, 0:32] = rows[d * 32 : (d + 1) * 32]
 
 
 def spread(level, j):
@@ -288,17 +281,15 @@
     ref[:, pl.ds(pl.multiple_of(head * D, D), D)] = value.astype(BF)
 
 
-def unpack_low_kernel(ids, z0_ref, own_ref, r0, r1, r2, r3, q1, o_ref, dq_ref, dk_ref, dv_ref):
+def unpack_low_kernel(ids, z0_ref, own_ref, r0, r1, r2, r3, o_ref, dq_ref, dk_ref, dv_ref, mine_ref):
     _, _, q, r = xyqr(ids[0])
     res = (o_ref, dq_ref, dk_ref, dv_ref)
     j1, j3 = r & 1, q & 1
-    w3b = spread(3, 1 - j3)
     for t, ref in enumerate(res):
         lo = t * 128
         ref[:, : 2 * D] = z0_ref[lo : lo + 128]
         put(ref, 2 + j1, own_ref[lo : lo + 128])
         put(ref, 3 - j1, r1[528 + lo : 656 + lo])
-        put(ref, 7 - j3, mm(w3b, q1[144 + t * 64 : 208 + t * 64]))
     for v, src in enumerate((r0, r1, r2, r3)):
         role = r ^ v
 
@@ -310,39 +301,30 @@
         @pl.when(role == 2)
         def _():
             w3 = spread(3, j3)
-            for t, ref in enumerate(res):
-                put(ref, 6 + j3, mm(w3, src[t * 128 : t * 128 + 64]))
-
-
-def unpack_high_kernel(ids, l0, l1, l2, l3, q0, q1, q2, q3, g5_ref, xy_ref, o_ref, dq_ref, dk_ref, dv_ref, terms_ref):
+            for t in range(4):
+                mine_ref[t] = mm(w3, src[t * 128 : t * 128 + 64]).astype(BF)
+
+
+def unpack_high_kernel(ids, l0, l1, l2, l3, mine_ref, g3_ref, qr_ref, g5_ref, xy_ref, o_ref, dq_ref, dk_ref, dv_ref, terms_ref):
     x, y, q, _ = xyqr(ids[0])
     dp = ids[1]
     res = (o_ref, dq_ref, dk_ref, dv_ref)
-    j5 = y & 1
-    w5b = spread(5, 1 - j5)
+    j3, j5 = q & 1, y & 1
+    w3b = spread(3, 1 - j3)
+    w40, w41, w5, w5b = spread(4, 0), spread(4, 1), spread(5, j5), spread(5, 1 - j5)
     pi, ci = iota((128, 32), 0), iota((128, 32), 1)
     for t, ref in enumerate(res):
-        put(ref, 3 - j5, mm(w5b, g5_ref[t * 16 : (t + 1) * 16]))
+        put(ref, j3, mine_ref[t])
+        put(ref, 1 - j3, mm(w3b, g3_ref[t * 64 : (t + 1) * 64]))
+        put(ref, 2, mm(w40, qr_ref[0, t * 32 : (t + 1) * 32]))
+        put(ref, 3, mm(w41, qr_ref[1, t * 32 : (t + 1) * 32]))
+        put(ref, 4 + j5, mm(w5, qr_ref[2, t * 32 : t * 32 + 16]))
+        put(ref, 5 - j5, mm(w5b, g5_ref[t * 16 : (t + 1) * 16]))
         for j in range(2):
             w6 = onehot(pi == (ci - t * 8) * 16 + off(6, j))
             w7 = onehot(pi == (ci - t * 4) * 32 + off(7, j))
-            put(ref, 4 + j, mm(w6, xy_ref[(x * 4 + j) * 4 + dp, 0:32]))
-            put(ref, 6 + j, mm(w7, xy_ref[(j * 4 + 2) * 4 + dp, 0:32]))
-    for v, src in enumerate((q0, q1, q2, q3)):
-        role = q ^ v
-
-        @pl.when(role < 2)
-        def _():
-            w4 = spread(4, role)
-            for t, ref in enumerate(res):
-                put(ref, role, mm(w4, src[t * 32 : (t + 1) * 32]))
-
-        @pl.when(role == 2)
-        def _():
-            w5 = spread(5, j5)
-            for t, ref in enumerate(res):
-                put(ref, 2 + j5, mm(w5, src[t * 32 : t * 32 + 16]))
-
+            put(ref, 6 + j, mm(w6, xy_ref[(x * 4 + j) * 4 + dp, 0:32]))
+            put(ref, 8 + j, mm(w7, xy_ref[(j * 4 + 2) * 4 + dp, 0:32]))
     acc = xy_ref[0, 32:48].astype(F32)
     for d in range(1, 32):
         acc += xy_ref[d, 32:48].astype(F32)
@@ -381,25 +363,27 @@
     raw = [a[0] for a in (asking_vectors, lookup_vectors, payload_vectors, incoming_sensitivity)]
     ids = jnp.stack([lax.axis_index(SEQ), lax.axis_index("dp")]).astype(jnp.int32)
     block = lambda n: ((n, D), BF)
-    xy = pl.pallas_call(
+    held = [pltpu.with_memory_space_constraint(a, pltpu.HBM) for a in raw]
+    g3, xy = pl.pallas_call(
         pack_kernel,
         grid=(1,),
-        in_specs=[SMEM] + [pl.BlockSpec((128, 8 * D), lambda i: (0, 1))] * 4,
-        out_specs=pl.BlockSpec((8, 96, D), lambda i: (0, 0, 0)),
-        out_shape=jax.ShapeDtypeStruct((8, 96, D), BF),
+        in_specs=[SMEM]
+        + [pl.BlockSpec((128, 2 * D), lambda i: (0, 3))] * 4
+        + [pl.BlockSpec((128, 8 * D), lambda i: (0, 1))] * 4,
+        out_specs=[pl.BlockSpec((256, D), lambda i: (0, 0)), pl.BlockSpec((8, 96, D), lambda i: (0, 0, 0))],
+        out_shape=[jax.ShapeDtypeStruct((256, D), BF), jax.ShapeDtypeStruct((8, 96, D), BF)],
         compiler_params=LIMIT,
         name="pack",
-    )(ids, *[pltpu.with_memory_space_constraint(a, pltpu.HBM) for a in raw])
+    )(ids, *held, *held)
+    g3 = swap(g3, "q", 1)
     xy = lax.all_to_all(xy, ("x", "y"), 0, 0)
     four = [stay(a) for a in raw]
     sizes = reply_list_sizes[0]
     z0, terms = call(local_kernel, [((512, 2 * D), BF), ((8, 128), F32)], [ids, learned_sharpness, sizes], four, [])
-    q0, q1, q2, q3 = call(
-        to_q_kernel, [block(128), block(384), block(128), block(128)], [ids], four, [xy], [pltpu.VMEM((4, 128, D), BF)]
-    )
-    q2, q1, q3 = swap(q2, "q", 2), swap(q1, "q", 1), swap(q3, "q", 3)
+    qs = call(to_q_kernel, [((4, 128, D), BF)], [ids], four, [xy])
+    qs = lax.all_to_all(qs, "q", 0, 0)
     r0, r1, r2, r3 = call(
-        to_r_kernel, [block(512), block(1024), block(512), block(512)], [ids], four, [q0, q1, q2, q3],
+        to_r_kernel, [block(512), block(1024), block(512), block(512)], [ids], four, [g3, qs],
         [pltpu.VMEM((4, 512, D), BF)],
     )
     r1, r3, r2 = swap(r1, "r", 1), swap(r3, "r", 3), swap(r2, "r", 2)
@@ -411,34 +395,35 @@
         [r0, r1, r2, r3, terms, back1],
     )
     r3, r2, r1 = swap(r3, "r", 3), swap(r2, "r", 2), swap(r1, "r", 1)
-    q0, q1, q2, q3 = call(from_r_kernel, [block(144), block(400), block(144), block(144)], [ids], [], [r0, r1, r2, r3])
-    q2, q1, q3 = swap(q2, "q", 2), swap(q1, "q", 1), swap(q3, "q", 3)
-    back5, xy = call(from_q_kernel, [block(64), ((32, 48, D), BF)], [ids], [], [q0, q1, q2, q3])
+    back3, qs = call(from_r_kernel, [block(256), ((4, 144, D), BF)], [ids], [], [r0, r1, r2, r3])
+    qs = lax.all_to_all(qs, "q", 0, 0)
+    back3 = swap(back3, "q", 1)
+    back5, xy = call(from_q_kernel, [block(64), ((32, 48, D), BF)], [ids], [], [qs])
     xy = lax.all_to_all(xy, ("x", "y", "dp"), 0, 0)
     back5 = swap(back5, "y", 1)
-    half = lambda i: pl.BlockSpec((128, 8 * D), lambda _: (0, i))
     result = jax.ShapeDtypeStruct((128, 16 * D), BF)
-    args = [z0, own1, r0, r1, r2, r3, q1]
-    outs = pl.pallas_call(
+    args = [stay(a) for a in (z0, own1, r0, r1, r2, r3)]
+    *outs, mine = pl.pallas_call(
         unpack_low_kernel,
         grid=(1,),
         in_specs=[SMEM] + [VMEM] * len(args),
-        out_specs=[half(0)] * 4,
-        out_shape=[result] * 4,
+        out_specs=[pl.BlockSpec((128, 6 * D), lambda i: (0, 0))] * 4 + [pl.BlockSpec((4, 128, D), lambda i: (0, 0, 0))],
+        out_shape=[result] * 4 + [jax.ShapeDtypeStruct((4, 128, D), BF)],
         compiler_params=LIMIT,
         name="unpack_low",
-    )(ids, *[stay(a) for a in args])
-    args = [q0, q1, q2, q3, back5, xy]
+    )(ids, *args)
+    args = [stay(a) for a in (mine, back3, qs, back5, xy)]
+    high = pl.BlockSpec((pl.Element(128), pl.Element(10 * D)), lambda i: (0, 6 * D))
     *outs, terms = pl.pallas_call(
         unpack_high_kernel,
         grid=(1,),
         in_specs=[SMEM] + [pl.BlockSpec(memory_space=pl.ANY)] * 4 + [VMEM] * len(args),
-        out_specs=[half(1)] * 4 + [pl.BlockSpec((1, 16), lambda _: (0, 0))],
+        out_specs=[high] * 4 + [pl.BlockSpec((1, 16), lambda i: (0, 0))],
         out_shape=[result] * 4 + [jax.ShapeDtypeStruct((1, 16), F32)],
         input_output_aliases={1: 0, 2: 1, 3: 2, 4: 3},
         compiler_params=LIMIT,
         name="unpack_high",
-    )(ids, *outs, *[stay(a) for a in args])
+    )(ids, *outs, *args)
     return (*[o[None] for o in outs], terms[0])
 
 

time: 127 us -> 133 us (1.047)
  the two profiles are of different devices: /device:TPU:1 before, /device:TPU:37 now
where the time goes in v4:
time: 133 us; the launch traced here: 132 us
  starting transfers between devices  57 us (43%)
  blocking collectives  30.5 us (23%)
  waiting for transfers between devices  26.9 us (20%)
  Pallas kernels  17.1 us (13%)
    ppermute x9, starting transfers between devices, swap(): return lax.ppermute(array, axis, [(i, i ^ v) for i in range(4)])  32.1 us
    ppermute x9, waiting for transfers between devices, swap(): return lax.ppermute(array, axis, [(i, i ^ v) for i in range(4)])  26.9 us
    all_to_all x1, blocking collectives, body(): qs = lax.all_to_all(qs, 'q', 0, 0)  19.2 us
    all_to_all x1, starting transfers between devices, body(): qs = lax.all_to_all(qs, 'q', 0, 0)  13.9 us
    pallas_call x7, Pallas kernels, call(): return run(*scalars, *args)  11.6 us
    all_to_all x1, blocking collectives, body(): xy = lax.all_to_all(xy, ('x', 'y'), 0, 0)  11.3 us
    all_to_all x1, starting transfers between devices, body(): xy = lax.all_to_all(xy, ('x', 'y', 'dp'), 0, 0)  11 us
  transfers between devices with their start and end apart: 11, of which 5 were waited for; matrix products, arithmetic and copies ran while one was open for 0% of the time, Pallas kernels for 4%

profile of v4, /device:TPU:37, one launch (start us, length us, event | category | flops | bytes accessed | tf_op | source)
XLA Modules:
  0.0 132.5 jit_solution(2520838654541442016)
XLA Ops:
  0.6 0.1 pad_add_fusion.ids
  0.7 0.0 copy-start
  0.7 0.0 copy-start.1
  0.7 0.0 copy-start.2
  0.7 0.0 copy-start.3
  0.7 1.8 %pack.1 = (bf16[256,128]{1,0:T(8,128)(2,1)S(1)}, bf16[8,96,128]{2,1,0:T(8,128)(2,1)S(1)}) custom-call(s32[2]{0:T(128)S(1)} %pad_add_fusion.ids, bf16[128,2048]{1,0:T(8,128)(2,1)} %bitcast.12, bf16[128,2048]{1,0:T(8,128)(2,1)} %bitcast.18, bf16[128,2048]{1,0:T(8,128)(2,1)} %bitcast.24, bf16[128,2048]{1,0:T(8,128)(2,1)} %bitcast.30, ...), custom_call_target="tpu_custom_call" | custom-call | tf_op jit(solution)/shard_map/pack/pallas_call | solution.py:367
  2.5 11.3 %all_to_all.20.xy_ref = bf16[8,96,128]{2,1,0:T(8,128)(2,1)S(1)} all-to-all(bf16[8,96,128]{2,1,0:T(8,128)(2,1)S(1)} %get-tuple-element.36), channel_id=1, replica_groups=mesh['x'=2,'y'=4,'q'=4,'r'=4,'dp'=4] {'x','y'}, dimensions={0} | all-to-all | bytes 393216 | tf_op jit(solution)/shard_map/all_to_all | solution.py:379
  13.8 0.0 copy-done
  13.8 0.0 copy-done.1
  13.8 0.0 copy-done.2
  13.9 0.0 copy-done.3
  13.9 1.5 %shard_map.102 = bf16[4,128,128]{2,1,0:T(8,128)(2,1)} custom-call(s32[2]{0:T(128)S(1)} %pad_add_fusion.ids, bf16[128,2048]{1,0:T(8,128)(2,1)S(1)} %bitcast.14, bf16[128,2048]{1,0:T(8,128)(2,1)S(1)} %bitcast.20, bf16[128,2048]{1,0:T(8,128)(2,1)S(1)} %bitcast.26, bf16[128,2048]{1,0:T(8,128)(2,1)S(1)} %bitcast.32, bf16[8,96,128]{2,1,0:T(8,128)(2,1)S(1)} %all_to_all.20.xy_ref), custom_call_target="tpu_custom_call" | custom-call | tf_op jit(solution)/shard_map/pallas_call | solution.py:355
  15.3 13.9 %all-to-all-start.1 = ((bf16[4,128,128]{2,1,0:T(8,128)(2,1)}), bf16[4,128,128]{2,1,0:T(8,128)(2,1)S(1)}, u32[]{:S(2)}, u32[]{:S(2)}) async-start(bf16[4,128,128]{2,1,0:T(8,128)(2,1)} %shard_map.102), calls=%async_computation.1 | async-start | bytes 262144 | tf_op jit(solution)/shard_map/all_to_all | solution.py:384
  29.2 7.3 %collective-permute-start = (bf16[256,128]{1,0:T(8,128)(2,1)S(1)}, bf16[256,128]{1,0:T(8,128)(2,1)S(1)}, u32[]{:S(2)}, u32[]{:S(2)}) collective-permute-start(bf16[256,128]{1,0:T(8,128)(2,1)S(1)} %get-tuple-element.35), channel_id=1, source_target_pairs={{0,16},{16,0},{32,48},{48,32},{1,17},{17,1},{33,49},{49,33},{2,18}... | collective-permute-start | bytes 196616 | tf_op jit(solution)/shard_map/ppermute | solution.py:359
  36.5 6.8 %collective-permute-done.g3_ref = bf16[256,128]{1,0:T(8,128)(2,1)S(1)} collective-permute-done((bf16[256,128]{1,0:T(8,128)(2,1)S(1)}, bf16[256,128]{1,0:T(8,128)(2,1)S(1)}, u32[]{:S(2)}, u32[]{:S(2)}) %collective-permute-start) | collective-permute-done | bytes 65568 | tf_op jit(solution)/shard_map/ppermute | solution.py:359
  43.3 0.0 all-to-all-done.1.qr_ref
  43.3 0.8 shard_map.103
  44.1 6.1 %collective-permute-start.1 = (bf16[1024,128]{1,0:T(8,128)(2,1)S(1)}, bf16[1024,128]{1,0:T(8,128)(2,1)S(1)}, u32[]{:S(2)}, u32[]{:S(2)}) collective-permute-start(bf16[1024,128]{1,0:T(8,128)(2,1)S(1)} %get-tuple-element.37), channel_id=1, source_target_pairs={{0,4},{4,0},{8,12},{12,8},{1,5},{5,1},{9,13},{13,9},{2,6},{6,2},{1... | collective-permute-start | bytes 786440 | tf_op jit(solution)/shard_map/ppermute | solution.py:359
  50.2 1.9 %collective-permute-start.2 = (bf16[512,128]{1,0:T(8,128)(2,1)S(1)}, bf16[512,128]{1,0:T(8,128)(2,1)S(1)}, u32[]{:S(2)}, u32[]{:S(2)}) collective-permute-start(bf16[512,128]{1,0:T(8,128)(2,1)S(1)} %get-tuple-element.41), channel_id=1, source_target_pairs={{0,8},{4,12},{8,0},{12,4},{1,9},{5,13},{9,1},{13,5},{2,10},{6,14},... | collective-permute-start | bytes 393224 | tf_op jit(solution)/shard_map/ppermute | solution.py:359
  52.1 0.0 copy-start.4
  52.2 0.0 copy-start.5
  52.2 3.1 %collective-permute-start.3 = (bf16[512,128]{1,0:T(8,128)(2,1)S(1)}, bf16[512,128]{1,0:T(8,128)(2,1)S(1)}, u32[]{:S(2)}, u32[]{:S(2)}) collective-permute-start(bf16[512,128]{1,0:T(8,128)(2,1)S(1)} %get-tuple-element.42), channel_id=1, source_target_pairs={{0,12},{4,8},{8,4},{12,0},{1,13},{5,9},{9,5},{13,1},{2,14},{6,10},... | collective-permute-start | bytes 393224 | tf_op jit(solution)/shard_map/ppermute | solution.py:359
  55.3 0.0 copy-done.4
  55.3 0.0 copy-done.5
  55.3 1.9 %shard_map.101 = (bf16[512,256]{1,0:T(8,128)(2,1)S(1)}, f32[8,128]{1,0:T(8,128)S(1)}) custom-call(s32[2]{0:T(128)S(1)} %pad_add_fusion.ids, f32[16]{0:T(128)S(1)} %copy-done.4, s32[8]{0:T(128)S(1)} %bitcast.36, bf16[128,2048]{1,0:T(8,128)(2,1)S(1)} %bitcast.16, bf16[128,2048]{1,0:T(8,128)(2,1)S(1)} %bitcast.22, bf16[128,2048]{1,0:T(8,128)(2,1)S(1)} %bitcast.28, ...), custom_call_target="tpu_custom_call" | custom-call | tf_op jit(solution)/shard_map/pallas_call | solution.py:355
  57.2 0.0 collective-permute-done.1.g1_ref.i1
  57.2 1.9 %shard_map.104 = (bf16[512,128]{1,0:T(8,128)(2,1)S(1)}, bf16[512,128]{1,0:T(8,128)(2,1)S(1)}, f32[8,128]{1,0:T(8,128)S(1)}) custom-call(s32[2]{0:T(128)S(1)} %pad_add_fusion.ids, f32[16]{0:T(128)S(1)} %copy-done.4, s32[8]{0:T(128)S(1)} %bitcast.37, bf16[128,2048]{1,0:T(8,128)(2,1)S(1)} %bitcast.17, bf16[128,2048]{1,0:T(8,128)(2,1)S(1)} %bitcast.23, ...), custom_call_target="tpu_custom_call" | custom-call | tf_op jit(solution)/shard_map/pallas_call | solution.py:355
  59.1 0.0 collective-permute-done.2.i2
  59.1 5.4 %collective-permute-done.3.i3 = bf16[512,128]{1,0:T(8,128)(2,1)S(1)} collective-permute-done((bf16[512,128]{1,0:T(8,128)(2,1)S(1)}, bf16[512,128]{1,0:T(8,128)(2,1)S(1)}, u32[]{:S(2)}, u32[]{:S(2)}) %collective-permute-start.3) | collective-permute-done | bytes 131104 | tf_op jit(solution)/shard_map/ppermute | solution.py:359
  64.5 3.6 %shard_map.105 = (bf16[528,128]{1,0:T(8,128)(2,1)S(1)}, bf16[1040,128]{1,0:T(8,128)(2,1)S(1)}, bf16[528,128]{1,0:T(8,128)(2,1)S(1)}, bf16[528,128]{1,0:T(8,128)(2,1)S(1)}) custom-call(s32[2]{0:T(128)S(1)} %pad_add_fusion.ids, f32[16]{0:T(128)S(1)} %copy-done.4, s32[8]{0:T(128)S(1)} %bitcast.38, bf16[512,128]{1,0:T(8,128)(2,1)S(1)} %get-tuple-element.40.i0, ...), custom_call_target="tpu_custom_call" | custom-call | tf_op jit(solution)/shard_map/pallas_call | solution.py:355
  68.0 1.9 %collective-permute-start.4 = (bf16[1040,128]{1,0:T(8,128)(2,1)S(1)}, bf16[1040,128]{1,0:T(8,128)(2,1)S(1)}, u32[]{:S(2)}, u32[]{:S(2)}) collective-permute-start(bf16[1040,128]{1,0:T(8,128)(2,1)S(1)} %get-tuple-element.46), channel_id=1, source_target_pairs={{0,4},{4,0},{8,12},{12,8},{1,5},{5,1},{9,13},{13,9},{2,6},{6,2},{1... | collective-permute-start | bytes 798728 | tf_op jit(solution)/shard_map/ppermute | solution.py:359
  70.0 3.2 %collective-permute-start.5 = (bf16[528,128]{1,0:T(8,128)(2,1)S(1)}, bf16[528,128]{1,0:T(8,128)(2,1)S(1)}, u32[]{:S(2)}, u32[]{:S(2)}) collective-permute-start(bf16[528,128]{1,0:T(8,128)(2,1)S(1)} %get-tuple-element.47), channel_id=1, source_target_pairs={{0,8},{4,12},{8,0},{12,4},{1,9},{5,13},{9,1},{13,5},{2,10},{6,14},... | collective-permute-start | bytes 405512 | tf_op jit(solution)/shard_map/ppermute | solution.py:359
  73.1 3.3 %collective-permute-start.6 = (bf16[528,128]{1,0:T(8,128)(2,1)S(1)}, bf16[528,128]{1,0:T(8,128)(2,1)S(1)}, u32[]{:S(2)}, u32[]{:S(2)}) collective-permute-start(bf16[528,128]{1,0:T(8,128)(2,1)S(1)} %get-tuple-element.48), channel_id=1, source_target_pairs={{0,12},{4,8},{8,4},{12,0},{1,13},{5,9},{9,5},{13,1},{2,14},{6,10},... | collective-permute-start | bytes 405512 | tf_op jit(solution)/shard_map/ppermute | solution.py:359
  76.4 1.1 collective-permute-done.5.r2.i2
  77.6 8.1 %collective-permute-done.6.r3.i3 = bf16[528,128]{1,0:T(8,128)(2,1)S(1)} collective-permute-done((bf16[528,128]{1,0:T(8,128)(2,1)S(1)}, bf16[528,128]{1,0:T(8,128)(2,1)S(1)}, u32[]{:S(2)}, u32[]{:S(2)}) %collective-permute-start.6) | collective-permute-done | bytes 135200 | tf_op jit(solution)/shard_map/ppermute | solution.py:359
  85.7 0.0 collective-permute-done.4.r1.i1
  85.7 0.6 shard_map.106
  86.3 19.2 %all_to_all.21.in_ref.qr_ref = bf16[4,144,128]{2,1,0:T(8,128)(2,1)S(1)} all-to-all(bf16[4,144,128]{2,1,0:T(8,128)(2,1)S(1)} %get-tuple-element.55), channel_id=1, replica_groups=mesh['x'=2,'y'=4,'q'=4,'r'=4,'dp'=4] {'q'}, dimensions={0} | all-to-all | bytes 294912 | tf_op jit(solution)/shard_map/all_to_all | solution.py:399
  105.5 1.4 %shard_map.107 = (bf16[64,128]{1,0:T(8,128)(2,1)S(1)}, bf16[32,48,128]{2,1,0:T(8,128)(2,1)}) custom-call(s32[2]{0:T(128)S(1)} %pad_add_fusion.ids, bf16[4,144,128]{2,1,0:T(8,128)(2,1)S(1)} %all_to_all.21.in_ref.qr_ref), custom_call_target="tpu_custom_call" | custom-call | tf_op jit(solution)/shard_map/pallas_call | solution.py:355
  107.0 11.0 %all-to-all-start.3 = ((bf16[32,48,128]{2,1,0:T(8,128)(2,1)}), bf16[32,48,128]{2,1,0:T(8,128)(2,1)S(1)}, u32[]{:S(2)}, u32[]{:S(2)}) async-start(bf16[32,48,128]{2,1,0:T(8,128)(2,1)} %get-tuple-element.57), calls=%async_computation.3 | async-start | bytes 786432 | tf_op jit(solution)/shard_map/all_to_all | solution.py:402
  117.9 2.2 %collective-permute-start.7 = (bf16[256,128]{1,0:T(8,128)(2,1)S(1)}, bf16[256,128]{1,0:T(8,128)(2,1)S(1)}, u32[]{:S(2)}, u32[]{:S(2)}) collective-permute-start(bf16[256,128]{1,0:T(8,128)(2,1)S(1)} %get-tuple-element.54), channel_id=1, source_target_pairs={{0,16},{16,0},{32,48},{48,32},{1,17},{17,1},{33,49},{49,33},{2,18}... | collective-permute-start | bytes 196616 | tf_op jit(solution)/shard_map/ppermute | solution.py:359
  120.2 3.1 %collective-permute-start.8 = (bf16[64,128]{1,0:T(8,128)(2,1)S(1)}, bf16[64,128]{1,0:T(8,128)(2,1)S(1)}, u32[]{:S(2)}, u32[]{:S(2)}) collective-permute-start(bf16[64,128]{1,0:T(8,128)(2,1)S(1)} %get-tuple-element.56), channel_id=1, source_target_pairs={{0,64},{64,0},{128,192},{192,128},{1,65},{65,1},{129,193},{193,129... | collective-permute-start | bytes 49160 | tf_op jit(solution)/shard_map/ppermute | solution.py:359
  123.3 1.7 %unpack_low.1 = (bf16[128,2048]{1,0:T(8,128)(2,1)}, bf16[128,2048]{1,0:T(8,128)(2,1)}, bf16[128,2048]{1,0:T(8,128)(2,1)}, bf16[128,2048]{1,0:T(8,128)(2,1)}, bf16[4,128,128]{2,1,0:T(8,128)(2,1)S(1)}) custom-call(s32[2]{0:T(128)S(1)} %pad_add_fusion.ids, bf16[512,256]{1,0:T(8,128)(2,1)S(1)} %get-tuple-element.34.z0_ref, ...), custom_call_target="tpu_custom_call" | custom-call | tf_op jit(solution)/shard_map/unpack_low/pallas_call | solution.py:406
  125.0 5.5 %collective-permute-done.7.g3_ref = bf16[256,128]{1,0:T(8,128)(2,1)S(1)} collective-permute-done((bf16[256,128]{1,0:T(8,128)(2,1)S(1)}, bf16[256,128]{1,0:T(8,128)(2,1)S(1)}, u32[]{:S(2)}, u32[]{:S(2)}) %collective-permute-start.7) | collective-permute-done | bytes 65568 | tf_op jit(solution)/shard_map/ppermute | solution.py:359
  130.5 0.0 collective-permute-done.8.g5_ref
  130.5 0.0 all-to-all-done.3.xy_ref
  130.5 2.0 %unpack_high.1 = (bf16[128,2048]{1,0:T(8,128)(2,1)}, bf16[128,2048]{1,0:T(8,128)(2,1)}, bf16[128,2048]{1,0:T(8,128)(2,1)}, bf16[128,2048]{1,0:T(8,128)(2,1)}, f32[1,16]{1,0:T(1,128)}) custom-call(s32[2]{0:T(128)S(1)} %pad_add_fusion.ids, ...), custom_call_target="tpu_custom_call", output_to_operand_aliasing={{0}: (1, {}), {1}: (2, {}), {2}: (3, {}), {3}: (4, {})} | custom-call | tf_op jit(solution)/shard_map/unpack_high/pallas_call | solution.py:417
Async XLA Ops:
  0.7 13.1 %copy-start = (bf16[1,128,2048]{2,1,0:T(8,128)(2,1)S(1)}, bf16[1,128,2048]{2,1,0:T(8,128)(2,1)}, u32[]{:S(2)}) copy-start(bf16[1,128,2048]{2,1,0:T(8,128)(2,1)} %param.6) | copy-start | bytes 1572868
  0.7 13.1 %copy-start.1 = (bf16[1,128,2048]{2,1,0:T(8,128)(2,1)S(1)}, bf16[1,128,2048]{2,1,0:T(8,128)(2,1)}, u32[]{:S(2)}) copy-start(bf16[1,128,2048]{2,1,0:T(8,128)(2,1)} %param.7) | copy-start | bytes 1572868
  0.7 13.1 %copy-start.2 = (bf16[1,128,2048]{2,1,0:T(8,128)(2,1)S(1)}, bf16[1,128,2048]{2,1,0:T(8,128)(2,1)}, u32[]{:S(2)}) copy-start(bf16[1,128,2048]{2,1,0:T(8,128)(2,1)} %param.8) | copy-start | bytes 1572868
  0.7 13.1 %copy-start.3 = (bf16[1,128,2048]{2,1,0:T(8,128)(2,1)S(1)}, bf16[1,128,2048]{2,1,0:T(8,128)(2,1)}, u32[]{:S(2)}) copy-start(bf16[1,128,2048]{2,1,0:T(8,128)(2,1)} %param.9) | copy-start | bytes 1572868
  15.3 28.0 %all-to-all-start.1 = ((bf16[4,128,128]{2,1,0:T(8,128)(2,1)}), bf16[4,128,128]{2,1,0:T(8,128)(2,1)S(1)}, u32[]{:S(2)}, u32[]{:S(2)}) async-start(bf16[4,128,128]{2,1,0:T(8,128)(2,1)} %shard_map.102), calls=%async_computation.1 | async-start | bytes 262144 | tf_op jit(solution)/shard_map/all_to_all | solution.py:384
  29.2 14.1 %collective-permute-start = (bf16[256,128]{1,0:T(8,128)(2,1)S(1)}, bf16[256,128]{1,0:T(8,128)(2,1)S(1)}, u32[]{:S(2)}, u32[]{:S(2)}) collective-permute-start(bf16[256,128]{1,0:T(8,128)(2,1)S(1)} %get-tuple-element.35), channel_id=1, source_target_pairs={{0,16},{16,0},{32,48},{48,32},{1,17},{17,1},{33,49},{49,33},{2,18}... | collective-permute-start | bytes 196616 | tf_op jit(solution)/shard_map/ppermute | solution.py:359
  44.1 13.1 %collective-permute-start.1 = (bf16[1024,128]{1,0:T(8,128)(2,1)S(1)}, bf16[1024,128]{1,0:T(8,128)(2,1)S(1)}, u32[]{:S(2)}, u32[]{:S(2)}) collective-permute-start(bf16[1024,128]{1,0:T(8,128)(2,1)S(1)} %get-tuple-element.37), channel_id=1, source_target_pairs={{0,4},{4,0},{8,12},{12,8},{1,5},{5,1},{9,13},{13,9},{2,6},{6,2},{1... | collective-permute-start | bytes 786440 | tf_op jit(solution)/shard_map/ppermute | solution.py:359
  50.2 8.9 %collective-permute-start.2 = (bf16[512,128]{1,0:T(8,128)(2,1)S(1)}, bf16[512,128]{1,0:T(8,128)(2,1)S(1)}, u32[]{:S(2)}, u32[]{:S(2)}) collective-permute-start(bf16[512,128]{1,0:T(8,128)(2,1)S(1)} %get-tuple-element.41), channel_id=1, source_target_pairs={{0,8},{4,12},{8,0},{12,4},{1,9},{5,13},{9,1},{13,5},{2,10},{6,14},... | collective-permute-start | bytes 393224 | tf_op jit(solution)/shard_map/ppermute | solution.py:359
  52.1 3.1 %copy-start.4 = (f32[16]{0:T(128)S(1)}, f32[16]{0:T(128)}, u32[]{:S(2)}) copy-start(f32[16]{0:T(128)} %sharp.5) | copy-start | bytes 196
  52.2 3.1 %copy-start.5 = (s32[1,8]{1,0:T(1,128)S(1)}, s32[1,8]{1,0:T(1,128)}, u32[]{:S(2)}) copy-start(s32[1,8]{1,0:T(1,128)} %param.11) | copy-start | bytes 100
  52.2 12.3 %collective-permute-start.3 = (bf16[512,128]{1,0:T(8,128)(2,1)S(1)}, bf16[512,128]{1,0:T(8,128)(2,1)S(1)}, u32[]{:S(2)}, u32[]{:S(2)}) collective-permute-start(bf16[512,128]{1,0:T(8,128)(2,1)S(1)} %get-tuple-element.42), channel_id=1, source_target_pairs={{0,12},{4,8},{8,4},{12,0},{1,13},{5,9},{9,5},{13,1},{2,14},{6,10},... | collective-permute-start | bytes 393224 | tf_op jit(solution)/shard_map/ppermute | solution.py:359
  68.0 17.7 %collective-permute-start.4 = (bf16[1040,128]{1,0:T(8,128)(2,1)S(1)}, bf16[1040,128]{1,0:T(8,128)(2,1)S(1)}, u32[]{:S(2)}, u32[]{:S(2)}) collective-permute-start(bf16[1040,128]{1,0:T(8,128)(2,1)S(1)} %get-tuple-element.46), channel_id=1, source_target_pairs={{0,4},{4,0},{8,12},{12,8},{1,5},{5,1},{9,13},{13,9},{2,6},{6,2},{1... | collective-permute-start | bytes 798728 | tf_op jit(solution)/shard_map/ppermute | solution.py:359
  70.0 7.6 %collective-permute-start.5 = (bf16[528,128]{1,0:T(8,128)(2,1)S(1)}, bf16[528,128]{1,0:T(8,128)(2,1)S(1)}, u32[]{:S(2)}, u32[]{:S(2)}) collective-permute-start(bf16[528,128]{1,0:T(8,128)(2,1)S(1)} %get-tuple-element.47), channel_id=1, source_target_pairs={{0,8},{4,12},{8,0},{12,4},{1,9},{5,13},{9,1},{13,5},{2,10},{6,14},... | collective-permute-start | bytes 405512 | tf_op jit(solution)/shard_map/ppermute | solution.py:359
  73.1 12.6 %collective-permute-start.6 = (bf16[528,128]{1,0:T(8,128)(2,1)S(1)}, bf16[528,128]{1,0:T(8,128)(2,1)S(1)}, u32[]{:S(2)}, u32[]{:S(2)}) collective-permute-start(bf16[528,128]{1,0:T(8,128)(2,1)S(1)} %get-tuple-element.48), channel_id=1, source_target_pairs={{0,12},{4,8},{8,4},{12,0},{1,13},{5,9},{9,5},{13,1},{2,14},{6,10},... | collective-permute-start | bytes 405512 | tf_op jit(solution)/shard_map/ppermute | solution.py:359
  107.0 23.5 %all-to-all-start.3 = ((bf16[32,48,128]{2,1,0:T(8,128)(2,1)}), bf16[32,48,128]{2,1,0:T(8,128)(2,1)S(1)}, u32[]{:S(2)}, u32[]{:S(2)}) async-start(bf16[32,48,128]{2,1,0:T(8,128)(2,1)} %get-tuple-element.57), calls=%async_computation.3 | async-start | bytes 786432 | tf_op jit(solution)/shard_map/all_to_all | solution.py:402
  117.9 12.6 %collective-permute-start.7 = (bf16[256,128]{1,0:T(8,128)(2,1)S(1)}, bf16[256,128]{1,0:T(8,128)(2,1)S(1)}, u32[]{:S(2)}, u32[]{:S(2)}) collective-permute-start(bf16[256,128]{1,0:T(8,128)(2,1)S(1)} %get-tuple-element.54), channel_id=1, source_target_pairs={{0,16},{16,0},{32,48},{48,32},{1,17},{17,1},{33,49},{49,33},{2,18}... | collective-permute-start | bytes 196616 | tf_op jit(solution)/shard_map/ppermute | solution.py:359
  120.2 10.3 %collective-permute-start.8 = (bf16[64,128]{1,0:T(8,128)(2,1)S(1)}, bf16[64,128]{1,0:T(8,128)(2,1)S(1)}, u32[]{:S(2)}, u32[]{:S(2)}) collective-permute-start(bf16[64,128]{1,0:T(8,128)(2,1)S(1)} %get-tuple-element.56), channel_id=1, source_target_pairs={{0,64},{64,0},{128,192},{192,128},{1,65},{65,1},{129,193},{193,129... | collective-permute-start | bytes 49160 | tf_op jit(solution)/shard_map/ppermute | solution.py:359

commit v5 on v4

--- a/solution.py
+++ b/solution.py
@@ -60,15 +60,11 @@
     return jnp.where(y < 2, six, jnp.where(y == 2, seven, -1))
 
 
-def pack_kernel(ids, q6_ref, k6_ref, v6_ref, u6_ref, q_ref, k_ref, v_ref, u_ref, g3_ref, xy_ref):
-    x, y, q, _ = xyqr(ids[0])
+def pack_kernel(ids, q_ref, k_ref, v_ref, u_ref, xy_ref):
+    x, y, _, _ = xyqr(ids[0])
     srcs = (q_ref, k_ref, v_ref, u_ref)
     j5 = 1 - (y & 1)
     s5 = pick(5, j5)
-    j3 = 1 - (q & 1)
-    s3 = pick(3, j3)
-    for t, ref in enumerate((q6_ref, k6_ref, v6_ref, u6_ref)):
-        g3_ref[t * 64 : (t + 1) * 64] = mm(s3, cols(ref, j3)).astype(BF)
     xy_ref[...] = jnp.zeros(xy_ref.shape, BF)
     for t, ref in enumerate(srcs):
         xy_ref[x * 4 + (y ^ 1), 32 + t * 16 : 48 + t * 16] = mm(s5, cols(ref, 2 + j5)).astype(BF)
@@ -99,22 +95,31 @@
     out_ref[3] = mm(perm, xy_ref[:, 0:32].reshape(256, D)).astype(BF)
 
 
-def to_r_kernel(ids, q_ref, k_ref, v_ref, u_ref, g3_ref, qr_ref, own_ref, t1_ref, t2_ref, t3_ref, tmp):
+def early_kernel(ids, q_ref, k_ref, v_ref, u_ref, g3_ref, own_ref, e1_ref, e2_ref, e3_ref):
     _, _, q, r = xyqr(ids[0])
-    j3 = q & 1
+    j3 = 1 - (q & 1)
     h1 = 3 - (r & 1)
     s3 = pick(3, j3)
     for t, ref in enumerate((q_ref, k_ref, v_ref, u_ref)):
         lo = t * 128
-        tmp[0, lo : lo + 128] = ref[:, 4 * D : 5 * D]
-        tmp[1, lo : lo + 128] = ref[:, 5 * D : 6 * D]
-        tmp[2, lo : lo + 64] = mm(s3, cols(ref, 6 + j3)).astype(BF)
-        tmp[2, lo + 64 : lo + 128] = g3_ref[t * 64 : (t + 1) * 64]
+        g3_ref[t * 64 : (t + 1) * 64] = mm(s3, cols(ref, 6 + j3)).astype(BF)
+        for v, out in enumerate((own_ref, e1_ref, e2_ref, e3_ref)):
+            out[lo : lo + 128] = cols(ref, 4 + ((r ^ v) & 1))
+        e1_ref[512 + lo : 640 + lo] = cols(ref, h1)
+
+
+def to_r_kernel(ids, q_ref, k_ref, v_ref, u_ref, g3_ref, qr_ref, own_ref, t1_ref, t2_ref, t3_ref, tmp):
+    _, _, q, r = xyqr(ids[0])
+    j3 = q & 1
+    s3 = pick(3, j3)
+    for t, ref in enumerate((q_ref, k_ref, v_ref, u_ref)):
+        lo = t * 128
+        tmp[0, lo : lo + 64] = mm(s3, cols(ref, 6 + j3)).astype(BF)
+        tmp[0, lo + 64 : lo + 128] = g3_ref[t * 64 : (t + 1) * 64]
         for u in range(4):
-            tmp[3, lo + u * 32 : lo + u * 32 + 32] = qr_ref[u, t * 32 : (t + 1) * 32]
-        t1_ref[512 + lo : 640 + lo] = cols(ref, h1)
+            tmp[1, lo + u * 32 : lo + u * 32 + 32] = qr_ref[u, t * 32 : (t + 1) * 32]
     for v, ref in enumerate((own_ref, t1_ref, t2_ref, t3_ref)):
-        ref[0:512] = tmp[r ^ v]
+        ref[...] = tmp[(r ^ v) & 1]
 
 
 def attention(qs, ks, vs, us, docs, mult):
@@ -200,8 +205,8 @@
     return jnp.where(row == 0, hi, jnp.where(row == 1, mid, jnp.where(row == 2, lo, 0.0))).astype(BF)
 
 
-def task_kernel(ids, sharp, sizes, i0, i1, i2, i3, terms_ref, back_ref, o0, o1, o2, o3):
-    ins, outs = (i0, i1, i2, i3), (o0, o1, o2, o3)
+def task_kernel(ids, sharp, sizes, e0, e1, e2, e3, i0, i1, i2, i3, terms_ref, back_ref, o0, o1, o2, o3):
+    ins, outs = ((e0, i0), (e1, i1), (e2, i2), (e3, i3)), (o0, o1, o2, o3)
     x, y, q, r = xyqr(ids[0])
     m = iota((128, 128), 0)
     near, r3 = r < 2, r == 2
@@ -220,7 +225,8 @@
     bounds = doc_bounds(sizes)
     docs = [doc_onehot(low + (r ^ v) * 128, bounds) for v in range(4)]
     head = level * 2 + j
-    blocks = [[ref[t * 128 : (t + 1) * 128] for ref in ins] for t in range(4)]
+    at = lambda ref, t: ref[t * 128 : (t + 1) * 128]
+    blocks = [[jnp.where(r < 2, at(a, t), at(b, t)) for a, b in ins] for t in range(4)]
     *res, term = attention(*blocks, docs, sharp[head] * (1.0 / math.sqrt(D)))
     extra = pieces(terms_ref[0:1] + at_lane(term, head))
     for v, ref in enumerate(outs):
@@ -333,7 +339,7 @@
 
 SMEM = pl.BlockSpec(memory_space=pltpu.SMEM)
 VMEM = pl.BlockSpec(memory_space=pltpu.VMEM)
-LIMIT = pltpu.CompilerParams(vmem_limit_bytes=20 << 20)
+LIMIT = pltpu.CompilerParams(vmem_limit_bytes=12 << 20)
 
 
 def stay(array):
@@ -359,40 +365,43 @@
     return lax.ppermute(array, axis, [(i, i ^ v) for i in range(4)])
 
 
+def send(array, v, senders):
+    return lax.ppermute(array, "r", [(i, i ^ v) for i in senders])
+
+
 def body(asking_vectors, lookup_vectors, payload_vectors, incoming_sensitivity, learned_sharpness, reply_list_sizes):
     raw = [a[0] for a in (asking_vectors, lookup_vectors, payload_vectors, incoming_sensitivity)]
     ids = jnp.stack([lax.axis_index(SEQ), lax.axis_index("dp")]).astype(jnp.int32)
     block = lambda n: ((n, D), BF)
     held = [pltpu.with_memory_space_constraint(a, pltpu.HBM) for a in raw]
-    g3, xy = pl.pallas_call(
+    xy = pl.pallas_call(
         pack_kernel,
         grid=(1,),
-        in_specs=[SMEM]
-        + [pl.BlockSpec((128, 2 * D), lambda i: (0, 3))] * 4
-        + [pl.BlockSpec((128, 8 * D), lambda i: (0, 1))] * 4,
-        out_specs=[pl.BlockSpec((256, D), lambda i: (0, 0)), pl.BlockSpec((8, 96, D), lambda i: (0, 0, 0))],
-        out_shape=[jax.ShapeDtypeStruct((256, D), BF), jax.ShapeDtypeStruct((8, 96, D), BF)],
+        in_specs=[SMEM] + [pl.BlockSpec((128, 8 * D), lambda i: (0, 1))] * 4,
+        out_specs=pl.BlockSpec((8, 96, D), lambda i: (0, 0, 0)),
+        out_shape=jax.ShapeDtypeStruct((8, 96, D), BF),
         compiler_params=LIMIT,
         name="pack",
-    )(ids, *held, *held)
-    g3 = swap(g3, "q", 1)
+    )(ids, *held)
     xy = lax.all_to_all(xy, ("x", "y"), 0, 0)
     four = [stay(a) for a in raw]
     sizes = reply_list_sizes[0]
     z0, terms = call(local_kernel, [((512, 2 * D), BF), ((8, 128), F32)], [ids, learned_sharpness, sizes], four, [])
+    g3, e0, e1, e2, e3 = call(
+        early_kernel, [block(256), block(512), block(1024), block(512), block(512)], [ids], four, []
+    )
     qs = call(to_q_kernel, [((4, 128, D), BF)], [ids], four, [xy])
     qs = lax.all_to_all(qs, "q", 0, 0)
-    r0, r1, r2, r3 = call(
-        to_r_kernel, [block(512), block(1024), block(512), block(512)], [ids], four, [g3, qs],
-        [pltpu.VMEM((4, 512, D), BF)],
-    )
-    r1, r3, r2 = swap(r1, "r", 1), swap(r3, "r", 3), swap(r2, "r", 2)
+    g3 = swap(g3, "q", 1)
+    e1, e2, e3 = swap(e1, "r", 1), send(e2, 2, (2, 3)), send(e3, 3, (2, 3))
+    r0, r1, r2, r3 = call(to_r_kernel, [block(512)] * 4, [ids], four, [g3, qs], [pltpu.VMEM((2, 512, D), BF)])
+    r2, r3, r1 = send(r2, 2, (0, 1)), send(r3, 3, (0, 1)), send(r1, 1, (2, 3))
     own1, back1, terms = call(
-        near_kernel, [block(512), block(512), ((8, 128), F32)], [ids, learned_sharpness, sizes], four, [r1, terms]
+        near_kernel, [block(512), block(512), ((8, 128), F32)], [ids, learned_sharpness, sizes], four, [e1, terms]
     )
     r0, r1, r2, r3 = call(
         task_kernel, [block(528), block(1040), block(528), block(528)], [ids, learned_sharpness, sizes], [],
-        [r0, r1, r2, r3, terms, back1],
+        [e0, e1, e2, e3, r0, r1, r2, r3, terms, back1],
     )
     r3, r2, r1 = swap(r3, "r", 3), swap(r2, "r", 2), swap(r1, "r", 1)
     back3, qs = call(from_r_kernel, [block(256), ((4, 144, D), BF)], [ids], [], [r0, r1, r2, r3])

time: 133 us -> 139 us (1.045)
  the two profiles are of different devices: /device:TPU:37 before, /device:TPU:1 now
where the time goes in v5:
time: 139 us; the launch traced here: 138 us
  starting transfers between devices  72.4 us (52%)
  blocking collectives  33 us (24%)
  Pallas kernels  18.4 us (13%)
  waiting for transfers between devices  13.2 us (9%)
    ppermute x7, starting transfers between devices, swap(): return lax.ppermute(array, axis, [(i, i ^ v) for i in range(4)])  32.1 us
    all_to_all x1, blocking collectives, body(): qs = lax.all_to_all(qs, 'q', 0, 0)  18.4 us
    ppermute x5, starting transfers between devices, send(): return lax.ppermute(array, 'r', [(i, i ^ v) for i in senders])  15.5 us
    all_to_all x1, starting transfers between devices, body(): qs = lax.all_to_all(qs, 'q', 0, 0)  14.8 us
    all_to_all x1, blocking collectives, body(): xy = lax.all_to_all(xy, ('x', 'y'), 0, 0)  14.6 us
    ppermute x7, waiting for transfers between devices, swap(): return lax.ppermute(array, axis, [(i, i ^ v) for i in range(4)])  13.2 us
    pallas_call x8, Pallas kernels, call(): return run(*scalars, *args)  13 us
    all_to_all x1, starting transfers between devices, body(): xy = lax.all_to_all(xy, ('x', 'y', 'dp'), 0, 0)  10 us
  transfers between devices with their start and end apart: 14, of which 4 were waited for; matrix products, arithmetic and copies ran while one was open for 0% of the time, Pallas kernels for 6%

profile of v5, /device:TPU:1, one launch (start us, length us, event | category | flops | bytes accessed | tf_op | source)
XLA Modules:
  0.0 137.9 jit_solution(16850736705836646517)
XLA Ops:
  0.6 0.1 pad_add_fusion.ids
  0.7 0.0 copy-start
  0.7 0.0 copy-start.1
  0.7 0.0 copy-start.2
  0.7 0.0 copy-start.3
  0.7 1.6 %pack.1 = bf16[8,96,128]{2,1,0:T(8,128)(2,1)S(1)} custom-call(s32[2]{0:T(128)S(1)} %pad_add_fusion.ids, bf16[128,2048]{1,0:T(8,128)(2,1)} %bitcast.12, bf16[128,2048]{1,0:T(8,128)(2,1)} %bitcast.18, bf16[128,2048]{1,0:T(8,128)(2,1)} %bitcast.24, bf16[128,2048]{1,0:T(8,128)(2,1)} %bitcast.30), custom_call_target="tpu_custom_call" | custom-call | tf_op jit(solution)/shard_map/pack/pallas_call | solution.py:377
  2.4 14.6 %all_to_all.20.xy_ref = bf16[8,96,128]{2,1,0:T(8,128)(2,1)S(1)} all-to-all(bf16[8,96,128]{2,1,0:T(8,128)(2,1)S(1)} %pack.1), channel_id=1, replica_groups=mesh['x'=2,'y'=4,'q'=4,'r'=4,'dp'=4] {'x','y'}, dimensions={0} | all-to-all | bytes 393216 | tf_op jit(solution)/shard_map/all_to_all | solution.py:386
  17.0 0.0 copy-done
  17.0 0.0 copy-done.1
  17.0 0.0 copy-done.2
  17.0 0.0 copy-done.3
  17.0 1.5 %shard_map.104 = bf16[4,128,128]{2,1,0:T(8,128)(2,1)} custom-call(s32[2]{0:T(128)S(1)} %pad_add_fusion.ids, bf16[128,2048]{1,0:T(8,128)(2,1)S(1)} %bitcast.13, bf16[128,2048]{1,0:T(8,128)(2,1)S(1)} %bitcast.19, bf16[128,2048]{1,0:T(8,128)(2,1)S(1)} %bitcast.25, bf16[128,2048]{1,0:T(8,128)(2,1)S(1)} %bitcast.31, bf16[8,96,128]{2,1,0:T(8,128)(2,1)S(1)} %all_to_all.20.xy_ref), custom_call_target="tpu_custom_call" | custom-call | tf_op jit(solution)/shard_map/pallas_call | solution.py:361
  18.4 14.8 %all-to-all-start.1 = ((bf16[4,128,128]{2,1,0:T(8,128)(2,1)}), bf16[4,128,128]{2,1,0:T(8,128)(2,1)S(1)}, u32[]{:S(2)}, u32[]{:S(2)}) async-start(bf16[4,128,128]{2,1,0:T(8,128)(2,1)} %shard_map.104), calls=%async_computation.1 | async-start | bytes 262144 | tf_op jit(solution)/shard_map/all_to_all | solution.py:394
  33.2 1.4 %shard_map.102 = (bf16[256,128]{1,0:T(8,128)(2,1)S(1)}, bf16[512,128]{1,0:T(8,128)(2,1)S(1)}, bf16[1024,128]{1,0:T(8,128)(2,1)S(1)}, bf16[512,128]{1,0:T(8,128)(2,1)}, bf16[512,128]{1,0:T(8,128)(2,1)S(1)}) custom-call(s32[2]{0:T(128)S(1)} %pad_add_fusion.ids, bf16[128,2048]{1,0:T(8,128)(2,1)S(1)} %bitcast.14, bf16[128,2048]{1,0:T(8,128)(2,1)S(1)} %bitcast.20, ...), custom_call_target="tpu_custom_call" | custom-call | tf_op jit(solution)/shard_map/pallas_call | solution.py:361
  34.6 2.6 %collective-permute-start = (bf16[1024,128]{1,0:T(8,128)(2,1)S(1)}, bf16[1024,128]{1,0:T(8,128)(2,1)S(1)}, u32[]{:S(2)}, u32[]{:S(2)}) collective-permute-start(bf16[1024,128]{1,0:T(8,128)(2,1)S(1)} %get-tuple-element.38), channel_id=1, source_target_pairs={{0,4},{4,0},{8,12},{12,8},{1,5},{5,1},{9,13},{13,9},{2,6},{6,2},{1... | collective-permute-start | bytes 786440 | tf_op jit(solution)/shard_map/ppermute | solution.py:365
  37.2 7.3 %collective-permute-start.3 = (bf16[256,128]{1,0:T(8,128)(2,1)S(1)}, bf16[256,128]{1,0:T(8,128)(2,1)S(1)}, u32[]{:S(2)}, u32[]{:S(2)}) collective-permute-start(bf16[256,128]{1,0:T(8,128)(2,1)S(1)} %get-tuple-element.44), channel_id=1, source_target_pairs={{0,16},{16,0},{32,48},{48,32},{1,17},{17,1},{33,49},{49,33},{2,18}... | collective-permute-start | bytes 196616 | tf_op jit(solution)/shard_map/ppermute | solution.py:365
  44.5 1.3 collective-permute-start.1
  45.8 1.3 collective-permute-start.2
  47.1 0.5 collective-permute-done.3.g3_ref
  47.7 0.0 all-to-all-done.1.qr_ref
  47.7 0.7 shard_map.105
  48.4 0.7 collective-permute-start.4
  49.1 10.9 %collective-permute-start.5 = (bf16[512,128]{1,0:T(8,128)(2,1)S(1)}, bf16[512,128]{1,0:T(8,128)(2,1)S(1)}, u32[]{:S(2)}, u32[]{:S(2)}) collective-permute-start(bf16[512,128]{1,0:T(8,128)(2,1)S(1)} %get-tuple-element.47), channel_id=1, source_target_pairs={{0,8},{4,12},{1,9},{5,13},{2,10},{6,14},{3,11},{7,15},{16,24},{20,... | collective-permute-start | bytes 393224 | tf_op jit(solution)/shard_map/ppermute | solution.py:369
  60.0 0.0 collective-permute-done.g1_ref.e1
  60.1 0.0 copy-start.4
  60.1 0.0 copy-start.5
  60.1 1.3 collective-permute-start.6
  61.4 0.0 copy-done.4
  61.4 0.0 copy-done.5
  61.4 1.9 %shard_map.101 = (bf16[512,256]{1,0:T(8,128)(2,1)S(1)}, f32[8,128]{1,0:T(8,128)S(1)}) custom-call(s32[2]{0:T(128)S(1)} %pad_add_fusion.ids, f32[16]{0:T(128)S(1)} %copy-done.4, s32[8]{0:T(128)S(1)} %bitcast.36, bf16[128,2048]{1,0:T(8,128)(2,1)S(1)} %bitcast.16, bf16[128,2048]{1,0:T(8,128)(2,1)S(1)} %bitcast.22, bf16[128,2048]{1,0:T(8,128)(2,1)S(1)} %bitcast.28, ...), custom_call_target="tpu_custom_call" | custom-call | tf_op jit(solution)/shard_map/pallas_call | solution.py:361
  63.3 1.9 %shard_map.103 = (bf16[512,128]{1,0:T(8,128)(2,1)S(1)}, bf16[512,128]{1,0:T(8,128)(2,1)S(1)}, f32[8,128]{1,0:T(8,128)S(1)}) custom-call(s32[2]{0:T(128)S(1)} %pad_add_fusion.ids, f32[16]{0:T(128)S(1)} %copy-done.4, s32[8]{0:T(128)S(1)} %bitcast.37, bf16[128,2048]{1,0:T(8,128)(2,1)S(1)} %bitcast.17, bf16[128,2048]{1,0:T(8,128)(2,1)S(1)} %bitcast.23, ...), custom_call_target="tpu_custom_call" | custom-call | tf_op jit(solution)/shard_map/pallas_call | solution.py:361
  65.2 0.0 collective-permute-done.1.e2
  65.2 0.0 collective-permute-done.2.e3
  65.2 0.0 collective-permute-done.4.i1
  65.2 0.0 collective-permute-done.5.i2
  65.2 0.0 collective-permute-done.6.i3
  65.2 3.6 %shard_map.106 = (bf16[528,128]{1,0:T(8,128)(2,1)S(1)}, bf16[1040,128]{1,0:T(8,128)(2,1)S(1)}, bf16[528,128]{1,0:T(8,128)(2,1)S(1)}, bf16[528,128]{1,0:T(8,128)(2,1)S(1)}) custom-call(s32[2]{0:T(128)S(1)} %pad_add_fusion.ids, f32[16]{0:T(128)S(1)} %copy-done.4, s32[8]{0:T(128)S(1)} %bitcast.38, bf16[512,128]{1,0:T(8,128)(2,1)S(1)} %get-tuple-element.41.e0, ...), custom_call_target="tpu_custom_call" | custom-call | tf_op jit(solution)/shard_map/pallas_call | solution.py:361
  68.8 8.8 %collective-permute-start.7 = (bf16[1040,128]{1,0:T(8,128)(2,1)S(1)}, bf16[1040,128]{1,0:T(8,128)(2,1)S(1)}, u32[]{:S(2)}, u32[]{:S(2)}) collective-permute-start(bf16[1040,128]{1,0:T(8,128)(2,1)S(1)} %get-tuple-element.52), channel_id=1, source_target_pairs={{0,4},{4,0},{8,12},{12,8},{1,5},{5,1},{9,13},{13,9},{2,6},{6,2},{1... | collective-permute-start | bytes 798728 | tf_op jit(solution)/shard_map/ppermute | solution.py:365
  77.7 3.8 %collective-permute-start.8 = (bf16[528,128]{1,0:T(8,128)(2,1)S(1)}, bf16[528,128]{1,0:T(8,128)(2,1)S(1)}, u32[]{:S(2)}, u32[]{:S(2)}) collective-permute-start(bf16[528,128]{1,0:T(8,128)(2,1)S(1)} %get-tuple-element.53), channel_id=1, source_target_pairs={{0,8},{4,12},{8,0},{12,4},{1,9},{5,13},{9,1},{13,5},{2,10},{6,14},... | collective-permute-start | bytes 405512 | tf_op jit(solution)/shard_map/ppermute | solution.py:365
  81.5 3.1 %collective-permute-start.9 = (bf16[528,128]{1,0:T(8,128)(2,1)S(1)}, bf16[528,128]{1,0:T(8,128)(2,1)S(1)}, u32[]{:S(2)}, u32[]{:S(2)}) collective-permute-start(bf16[528,128]{1,0:T(8,128)(2,1)S(1)} %get-tuple-element.54), channel_id=1, source_target_pairs={{0,12},{4,8},{8,4},{12,0},{1,13},{5,9},{9,5},{13,1},{2,14},{6,10},... | collective-permute-start | bytes 405512 | tf_op jit(solution)/shard_map/ppermute | solution.py:365
  84.6 0.5 collective-permute-done.8.r2.i2
  85.1 6.5 %collective-permute-done.9.r3.i3 = bf16[528,128]{1,0:T(8,128)(2,1)S(1)} collective-permute-done((bf16[528,128]{1,0:T(8,128)(2,1)S(1)}, bf16[528,128]{1,0:T(8,128)(2,1)S(1)}, u32[]{:S(2)}, u32[]{:S(2)}) %collective-permute-start.9) | collective-permute-done | bytes 135200 | tf_op jit(solution)/shard_map/ppermute | solution.py:365
  91.7 0.0 collective-permute-done.7.r1.i1
  91.7 0.6 shard_map.107
  92.3 18.4 %all_to_all.21.in_ref.qr_ref = bf16[4,144,128]{2,1,0:T(8,128)(2,1)S(1)} all-to-all(bf16[4,144,128]{2,1,0:T(8,128)(2,1)S(1)} %get-tuple-element.61), channel_id=1, replica_groups=mesh['x'=2,'y'=4,'q'=4,'r'=4,'dp'=4] {'q'}, dimensions={0} | all-to-all | bytes 294912 | tf_op jit(solution)/shard_map/all_to_all | solution.py:408
  110.7 1.5 %shard_map.108 = (bf16[64,128]{1,0:T(8,128)(2,1)S(1)}, bf16[32,48,128]{2,1,0:T(8,128)(2,1)}) custom-call(s32[2]{0:T(128)S(1)} %pad_add_fusion.ids, bf16[4,144,128]{2,1,0:T(8,128)(2,1)S(1)} %all_to_all.21.in_ref.qr_ref), custom_call_target="tpu_custom_call" | custom-call | tf_op jit(solution)/shard_map/pallas_call | solution.py:361
  112.1 10.0 %all-to-all-start.3 = ((bf16[32,48,128]{2,1,0:T(8,128)(2,1)}), bf16[32,48,128]{2,1,0:T(8,128)(2,1)S(1)}, u32[]{:S(2)}, u32[]{:S(2)}) async-start(bf16[32,48,128]{2,1,0:T(8,128)(2,1)} %get-tuple-element.63), calls=%async_computation.3 | async-start | bytes 786432 | tf_op jit(solution)/shard_map/all_to_all | solution.py:411
  122.2 3.2 %collective-permute-start.10 = (bf16[256,128]{1,0:T(8,128)(2,1)S(1)}, bf16[256,128]{1,0:T(8,128)(2,1)S(1)}, u32[]{:S(2)}, u32[]{:S(2)}) collective-permute-start(bf16[256,128]{1,0:T(8,128)(2,1)S(1)} %get-tuple-element.60), channel_id=1, source_target_pairs={{0,16},{16,0},{32,48},{48,32},{1,17},{17,1},{33,49},{49,33},{2,18}... | collective-permute-start | bytes 196616 | tf_op jit(solution)/shard_map/ppermute | solution.py:365
  125.3 3.3 %collective-permute-start.11 = (bf16[64,128]{1,0:T(8,128)(2,1)S(1)}, bf16[64,128]{1,0:T(8,128)(2,1)S(1)}, u32[]{:S(2)}, u32[]{:S(2)}) collective-permute-start(bf16[64,128]{1,0:T(8,128)(2,1)S(1)} %get-tuple-element.62), channel_id=1, source_target_pairs={{0,64},{64,0},{128,192},{192,128},{1,65},{65,1},{129,193},{193,129... | collective-permute-start | bytes 49160 | tf_op jit(solution)/shard_map/ppermute | solution.py:365
  128.6 1.7 %unpack_low.1 = (bf16[128,2048]{1,0:T(8,128)(2,1)}, bf16[128,2048]{1,0:T(8,128)(2,1)}, bf16[128,2048]{1,0:T(8,128)(2,1)}, bf16[128,2048]{1,0:T(8,128)(2,1)}, bf16[4,128,128]{2,1,0:T(8,128)(2,1)S(1)}) custom-call(s32[2]{0:T(128)S(1)} %pad_add_fusion.ids, bf16[512,256]{1,0:T(8,128)(2,1)S(1)} %get-tuple-element.37.z0_ref, ...), custom_call_target="tpu_custom_call" | custom-call | tf_op jit(solution)/shard_map/unpack_low/pallas_call | solution.py:415
  130.3 5.6 %collective-permute-done.10.g3_ref = bf16[256,128]{1,0:T(8,128)(2,1)S(1)} collective-permute-done((bf16[256,128]{1,0:T(8,128)(2,1)S(1)}, bf16[256,128]{1,0:T(8,128)(2,1)S(1)}, u32[]{:S(2)}, u32[]{:S(2)}) %collective-permute-start.10) | collective-permute-done | bytes 65568 | tf_op jit(solution)/shard_map/ppermute | solution.py:365
  135.9 0.0 collective-permute-done.11.g5_ref
  135.9 0.0 all-to-all-done.3.xy_ref
  135.9 2.0 %unpack_high.1 = (bf16[128,2048]{1,0:T(8,128)(2,1)}, bf16[128,2048]{1,0:T(8,128)(2,1)}, bf16[128,2048]{1,0:T(8,128)(2,1)}, bf16[128,2048]{1,0:T(8,128)(2,1)}, f32[1,16]{1,0:T(1,128)}) custom-call(s32[2]{0:T(128)S(1)} %pad_add_fusion.ids, ...), custom_call_target="tpu_custom_call", output_to_operand_aliasing={{0}: (1, {}), {1}: (2, {}), {2}: (3, {}), {3}: (4, {})} | custom-call | tf_op jit(solution)/shard_map/unpack_high/pallas_call | solution.py:426
Async XLA Ops:
  0.7 16.2 %copy-start = (bf16[1,128,2048]{2,1,0:T(8,128)(2,1)S(1)}, bf16[1,128,2048]{2,1,0:T(8,128)(2,1)}, u32[]{:S(2)}) copy-start(bf16[1,128,2048]{2,1,0:T(8,128)(2,1)} %param.6) | copy-start | bytes 1572868
  0.7 16.2 %copy-start.1 = (bf16[1,128,2048]{2,1,0:T(8,128)(2,1)S(1)}, bf16[1,128,2048]{2,1,0:T(8,128)(2,1)}, u32[]{:S(2)}) copy-start(bf16[1,128,2048]{2,1,0:T(8,128)(2,1)} %param.7) | copy-start | bytes 1572868
  0.7 16.2 %copy-start.2 = (bf16[1,128,2048]{2,1,0:T(8,128)(2,1)S(1)}, bf16[1,128,2048]{2,1,0:T(8,128)(2,1)}, u32[]{:S(2)}) copy-start(bf16[1,128,2048]{2,1,0:T(8,128)(2,1)} %param.8) | copy-start | bytes 1572868
  0.7 16.2 %copy-start.3 = (bf16[1,128,2048]{2,1,0:T(8,128)(2,1)S(1)}, bf16[1,128,2048]{2,1,0:T(8,128)(2,1)}, u32[]{:S(2)}) copy-start(bf16[1,128,2048]{2,1,0:T(8,128)(2,1)} %param.9) | copy-start | bytes 1572868
  18.4 29.2 %all-to-all-start.1 = ((bf16[4,128,128]{2,1,0:T(8,128)(2,1)}), bf16[4,128,128]{2,1,0:T(8,128)(2,1)S(1)}, u32[]{:S(2)}, u32[]{:S(2)}) async-start(bf16[4,128,128]{2,1,0:T(8,128)(2,1)} %shard_map.104), calls=%async_computation.1 | async-start | bytes 262144 | tf_op jit(solution)/shard_map/all_to_all | solution.py:394
  34.6 25.4 %collective-permute-start = (bf16[1024,128]{1,0:T(8,128)(2,1)S(1)}, bf16[1024,128]{1,0:T(8,128)(2,1)S(1)}, u32[]{:S(2)}, u32[]{:S(2)}) collective-permute-start(bf16[1024,128]{1,0:T(8,128)(2,1)S(1)} %get-tuple-element.38), channel_id=1, source_target_pairs={{0,4},{4,0},{8,12},{12,8},{1,5},{5,1},{9,13},{13,9},{2,6},{6,2},{1... | collective-permute-start | bytes 786440 | tf_op jit(solution)/shard_map/ppermute | solution.py:365
  37.2 10.4 %collective-permute-start.3 = (bf16[256,128]{1,0:T(8,128)(2,1)S(1)}, bf16[256,128]{1,0:T(8,128)(2,1)S(1)}, u32[]{:S(2)}, u32[]{:S(2)}) collective-permute-start(bf16[256,128]{1,0:T(8,128)(2,1)S(1)} %get-tuple-element.44), channel_id=1, source_target_pairs={{0,16},{16,0},{32,48},{48,32},{1,17},{17,1},{33,49},{49,33},{2,18}... | collective-permute-start | bytes 196616 | tf_op jit(solution)/shard_map/ppermute | solution.py:365
  44.5 20.6 %collective-permute-start.1 = (bf16[512,128]{1,0:T(8,128)(2,1)}, bf16[512,128]{1,0:T(8,128)(2,1)S(1)}, u32[]{:S(2)}, u32[]{:S(2)}) collective-permute-start(bf16[512,128]{1,0:T(8,128)(2,1)} %get-tuple-element.42), channel_id=1, source_target_pairs={{8,0},{12,4},{9,1},{13,5},{10,2},{14,6},{11,3},{15,7},{24,16},{28,... | collective-permute-start | bytes 393224 | tf_op jit(solution)/shard_map/ppermute | solution.py:369
  45.8 19.4 %collective-permute-start.2 = (bf16[512,128]{1,0:T(8,128)(2,1)S(1)}, bf16[512,128]{1,0:T(8,128)(2,1)S(1)}, u32[]{:S(2)}, u32[]{:S(2)}) collective-permute-start(bf16[512,128]{1,0:T(8,128)(2,1)S(1)} %get-tuple-element.43), channel_id=1, source_target_pairs={{8,4},{12,0},{9,5},{13,1},{10,6},{14,2},{11,7},{15,3},{24,20},{28,... | collective-permute-start | bytes 393224 | tf_op jit(solution)/shard_map/ppermute | solution.py:369
  48.4 16.8 %collective-permute-start.4 = (bf16[512,128]{1,0:T(8,128)(2,1)S(1)}, bf16[512,128]{1,0:T(8,128)(2,1)S(1)}, u32[]{:S(2)}, u32[]{:S(2)}) collective-permute-start(bf16[512,128]{1,0:T(8,128)(2,1)S(1)} %get-tuple-element.46), channel_id=1, source_target_pairs={{8,12},{12,8},{9,13},{13,9},{10,14},{14,10},{11,15},{15,11},{24,28... | collective-permute-start | bytes 393224 | tf_op jit(solution)/shard_map/ppermute | solution.py:369
  49.1 16.1 %collective-permute-start.5 = (bf16[512,128]{1,0:T(8,128)(2,1)S(1)}, bf16[512,128]{1,0:T(8,128)(2,1)S(1)}, u32[]{:S(2)}, u32[]{:S(2)}) collective-permute-start(bf16[512,128]{1,0:T(8,128)(2,1)S(1)} %get-tuple-element.47), channel_id=1, source_target_pairs={{0,8},{4,12},{1,9},{5,13},{2,10},{6,14},{3,11},{7,15},{16,24},{20,... | collective-permute-start | bytes 393224 | tf_op jit(solution)/shard_map/ppermute | solution.py:369
  60.1 1.3 copy-start.4
  60.1 1.3 copy-start.5
  60.1 5.1 %collective-permute-start.6 = (bf16[512,128]{1,0:T(8,128)(2,1)S(1)}, bf16[512,128]{1,0:T(8,128)(2,1)S(1)}, u32[]{:S(2)}, u32[]{:S(2)}) collective-permute-start(bf16[512,128]{1,0:T(8,128)(2,1)S(1)} %get-tuple-element.48), channel_id=1, source_target_pairs={{0,12},{4,8},{1,13},{5,9},{2,14},{6,10},{3,15},{7,11},{16,28},{20,... | collective-permute-start | bytes 393224 | tf_op jit(solution)/shard_map/ppermute | solution.py:369
  68.8 22.8 %collective-permute-start.7 = (bf16[1040,128]{1,0:T(8,128)(2,1)S(1)}, bf16[1040,128]{1,0:T(8,128)(2,1)S(1)}, u32[]{:S(2)}, u32[]{:S(2)}) collective-permute-start(bf16[1040,128]{1,0:T(8,128)(2,1)S(1)} %get-tuple-element.52), channel_id=1, source_target_pairs={{0,4},{4,0},{8,12},{12,8},{1,5},{5,1},{9,13},{13,9},{2,6},{6,2},{1... | collective-permute-start | bytes 798728 | tf_op jit(solution)/shard_map/ppermute | solution.py:365
  77.7 7.5 %collective-permute-start.8 = (bf16[528,128]{1,0:T(8,128)(2,1)S(1)}, bf16[528,128]{1,0:T(8,128)(2,1)S(1)}, u32[]{:S(2)}, u32[]{:S(2)}) collective-permute-start(bf16[528,128]{1,0:T(8,128)(2,1)S(1)} %get-tuple-element.53), channel_id=1, source_target_pairs={{0,8},{4,12},{8,0},{12,4},{1,9},{5,13},{9,1},{13,5},{2,10},{6,14},... | collective-permute-start | bytes 405512 | tf_op jit(solution)/shard_map/ppermute | solution.py:365
  81.5 10.1 %collective-permute-start.9 = (bf16[528,128]{1,0:T(8,128)(2,1)S(1)}, bf16[528,128]{1,0:T(8,128)(2,1)S(1)}, u32[]{:S(2)}, u32[]{:S(2)}) collective-permute-start(bf16[528,128]{1,0:T(8,128)(2,1)S(1)} %get-tuple-element.54), channel_id=1, source_target_pairs={{0,12},{4,8},{8,4},{12,0},{1,13},{5,9},{9,5},{13,1},{2,14},{6,10},... | collective-permute-start | bytes 405512 | tf_op jit(solution)/shard_map/ppermute | solution.py:365
  112.1 23.8 %all-to-all-start.3 = ((bf16[32,48,128]{2,1,0:T(8,128)(2,1)}), bf16[32,48,128]{2,1,0:T(8,128)(2,1)S(1)}, u32[]{:S(2)}, u32[]{:S(2)}) async-start(bf16[32,48,128]{2,1,0:T(8,128)(2,1)} %get-tuple-element.63), calls=%async_computation.3 | async-start | bytes 786432 | tf_op jit(solution)/shard_map/all_to_all | solution.py:411
  122.2 13.7 %collective-permute-start.10 = (bf16[256,128]{1,0:T(8,128)(2,1)S(1)}, bf16[256,128]{1,0:T(8,128)(2,1)S(1)}, u32[]{:S(2)}, u32[]{:S(2)}) collective-permute-start(bf16[256,128]{1,0:T(8,128)(2,1)S(1)} %get-tuple-element.60), channel_id=1, source_target_pairs={{0,16},{16,0},{32,48},{48,32},{1,17},{17,1},{33,49},{49,33},{2,18}... | collective-permute-start | bytes 196616 | tf_op jit(solution)/shard_map/ppermute | solution.py:365
  125.3 10.6 %collective-permute-start.11 = (bf16[64,128]{1,0:T(8,128)(2,1)S(1)}, bf16[64,128]{1,0:T(8,128)(2,1)S(1)}, u32[]{:S(2)}, u32[]{:S(2)}) collective-permute-start(bf16[64,128]{1,0:T(8,128)(2,1)S(1)} %get-tuple-element.62), channel_id=1, source_target_pairs={{0,64},{64,0},{128,192},{192,128},{1,65},{65,1},{129,193},{193,129... | collective-permute-start | bytes 49160 | tf_op jit(solution)/shard_map/ppermute | solution.py:365

commit v6 on v5

--- a/solution.py
+++ b/solution.py
@@ -95,17 +95,14 @@
     out_ref[3] = mm(perm, xy_ref[:, 0:32].reshape(256, D)).astype(BF)
 
 
-def early_kernel(ids, q_ref, k_ref, v_ref, u_ref, g3_ref, own_ref, e1_ref, e2_ref, e3_ref):
+def early_kernel(ids, q_ref, k_ref, v_ref, u_ref, g1_ref, g3_ref):
     _, _, q, r = xyqr(ids[0])
     j3 = 1 - (q & 1)
     h1 = 3 - (r & 1)
     s3 = pick(3, j3)
     for t, ref in enumerate((q_ref, k_ref, v_ref, u_ref)):
-        lo = t * 128
+        g1_ref[t * 128 : (t + 1) * 128] = cols(ref, h1)
         g3_ref[t * 64 : (t + 1) * 64] = mm(s3, cols(ref, 6 + j3)).astype(BF)
-        for v, out in enumerate((own_ref, e1_ref, e2_ref, e3_ref)):
-            out[lo : lo + 128] = cols(ref, 4 + ((r ^ v) & 1))
-        e1_ref[512 + lo : 640 + lo] = cols(ref, h1)
 
 
 def to_r_kernel(ids, q_ref, k_ref, v_ref, u_ref, g3_ref, qr_ref, own_ref, t1_ref, t2_ref, t3_ref, tmp):
@@ -114,12 +111,14 @@
     s3 = pick(3, j3)
     for t, ref in enumerate((q_ref, k_ref, v_ref, u_ref)):
         lo = t * 128
-        tmp[0, lo : lo + 64] = mm(s3, cols(ref, 6 + j3)).astype(BF)
-        tmp[0, lo + 64 : lo + 128] = g3_ref[t * 64 : (t + 1) * 64]
+        tmp[0, lo : lo + 128] = ref[:, 4 * D : 5 * D]
+        tmp[1, lo : lo + 128] = ref[:, 5 * D : 6 * D]
+        tmp[2, lo : lo + 64] = mm(s3, cols(ref, 6 + j3)).astype(BF)
+        tmp[2, lo + 64 : lo + 128] = g3_ref[t * 64 : (t + 1) * 64]
         for u in range(4):
-            tmp[1, lo + u * 32 : lo + u * 32 + 32] = qr_ref[u, t * 32 : (t + 1) * 32]
+            tmp[3, lo + u * 32 : lo + u * 32 + 32] = qr_ref[u, t * 32 : (t + 1) * 32]
     for v, ref in enumerate((own_ref, t1_ref, t2_ref, t3_ref)):
-        ref[...] = tmp[(r ^ v) & 1]
+        ref[...] = tmp[r ^ v]
 
 
 def attention(qs, ks, vs, us, docs, mult):
@@ -189,7 +188,7 @@
     there = doc_onehot((dev ^ 1) * 128 + row, bounds)
     refs = (q_ref, k_ref, v_ref, u_ref)
     h = 2 + (r & 1)
-    blocks = [[cols(ref, h), g1_ref[512 + t * 128 : 640 + t * 128]] for t, ref in enumerate(refs)]
+    blocks = [[cols(ref, h), g1_ref[t * 128 : (t + 1) * 128]] for t, ref in enumerate(refs)]
     *res, term = attention(*blocks, [here, there], sharp[h] * (1.0 / math.sqrt(D)))
     for t in range(4):
         own_ref[t * 128 : (t + 1) * 128] = res[t][0]
@@ -205,8 +204,8 @@
     return jnp.where(row == 0, hi, jnp.where(row == 1, mid, jnp.where(row == 2, lo, 0.0))).astype(BF)
 
 
-def task_kernel(ids, sharp, sizes, e0, e1, e2, e3, i0, i1, i2, i3, terms_ref, back_ref, o0, o1, o2, o3):
-    ins, outs = ((e0, i0), (e1, i1), (e2, i2), (e3, i3)), (o0, o1, o2, o3)
+def task_kernel(ids, sharp, sizes, i0, i1, i2, i3, terms_ref, o0, o1, o2, o3):
+    ins, outs = (i0, i1, i2, i3), (o0, o1, o2, o3)
     x, y, q, r = xyqr(ids[0])
     m = iota((128, 128), 0)
     near, r3 = r < 2, r == 2
@@ -225,15 +224,13 @@
     bounds = doc_bounds(sizes)
     docs = [doc_onehot(low + (r ^ v) * 128, bounds) for v in range(4)]
     head = level * 2 + j
-    at = lambda ref, t: ref[t * 128 : (t + 1) * 128]
-    blocks = [[jnp.where(r < 2, at(a, t), at(b, t)) for a, b in ins] for t in range(4)]
+    blocks = [[ref[t * 128 : (t + 1) * 128] for ref in ins] for t in range(4)]
     *res, term = attention(*blocks, docs, sharp[head] * (1.0 / math.sqrt(D)))
     extra = pieces(terms_ref[0:1] + at_lane(term, head))
     for v, ref in enumerate(outs):
         for t in range(4):
             ref[t * 128 : (t + 1) * 128] = res[t][v]
         ref[512:528] = extra
-    o1[528:1040] = back_ref[...]
 
 
 def total4(blocks):
@@ -287,7 +284,7 @@
     ref[:, pl.ds(pl.multiple_of(head * D, D), D)] = value.astype(BF)
 
 
-def unpack_low_kernel(ids, z0_ref, own_ref, r0, r1, r2, r3, o_ref, dq_ref, dk_ref, dv_ref, mine_ref):
+def unpack_low_kernel(ids, z0_ref, own_ref, g1_ref, r0, r1, r2, r3, o_ref, dq_ref, dk_ref, dv_ref, mine_ref):
     _, _, q, r = xyqr(ids[0])
     res = (o_ref, dq_ref, dk_ref, dv_ref)
     j1, j3 = r & 1, q & 1
@@ -295,7 +292,7 @@
         lo = t * 128
         ref[:, : 2 * D] = z0_ref[lo : lo + 128]
         put(ref, 2 + j1, own_ref[lo : lo + 128])
-        put(ref, 3 - j1, r1[528 + lo : 656 + lo])
+        put(ref, 3 - j1, g1_ref[lo : lo + 128])
     for v, src in enumerate((r0, r1, r2, r3)):
         role = r ^ v
 
@@ -365,10 +362,6 @@
     return lax.ppermute(array, axis, [(i, i ^ v) for i in range(4)])
 
 
-def send(array, v, senders):
-    return lax.ppermute(array, "r", [(i, i ^ v) for i in senders])
-
-
 def body(asking_vectors, lookup_vectors, payload_vectors, incoming_sensitivity, learned_sharpness, reply_list_sizes):
     raw = [a[0] for a in (asking_vectors, lookup_vectors, payload_vectors, incoming_sensitivity)]
     ids = jnp.stack([lax.axis_index(SEQ), lax.axis_index("dp")]).astype(jnp.int32)
@@ -387,21 +380,20 @@
     four = [stay(a) for a in raw]
     sizes = reply_list_sizes[0]
     z0, terms = call(local_kernel, [((512, 2 * D), BF), ((8, 128), F32)], [ids, learned_sharpness, sizes], four, [])
-    g3, e0, e1, e2, e3 = call(
-        early_kernel, [block(256), block(512), block(1024), block(512), block(512)], [ids], four, []
-    )
+    g1, g3 = call(early_kernel, [block(512), block(256)], [ids], four, [])
     qs = call(to_q_kernel, [((4, 128, D), BF)], [ids], four, [xy])
     qs = lax.all_to_all(qs, "q", 0, 0)
     g3 = swap(g3, "q", 1)
-    e1, e2, e3 = swap(e1, "r", 1), send(e2, 2, (2, 3)), send(e3, 3, (2, 3))
-    r0, r1, r2, r3 = call(to_r_kernel, [block(512)] * 4, [ids], four, [g3, qs], [pltpu.VMEM((2, 512, D), BF)])
-    r2, r3, r1 = send(r2, 2, (0, 1)), send(r3, 3, (0, 1)), send(r1, 1, (2, 3))
+    g1 = swap(g1, "r", 1)
+    r0, r1, r2, r3 = call(to_r_kernel, [block(512)] * 4, [ids], four, [g3, qs], [pltpu.VMEM((4, 512, D), BF)])
+    r1, r3, r2 = swap(r1, "r", 1), swap(r3, "r", 3), swap(r2, "r", 2)
     own1, back1, terms = call(
-        near_kernel, [block(512), block(512), ((8, 128), F32)], [ids, learned_sharpness, sizes], four, [e1, terms]
+        near_kernel, [block(512), block(512), ((8, 128), F32)], [ids, learned_sharpness, sizes], four, [g1, terms]
     )
+    back1 = swap(back1, "r", 1)
     r0, r1, r2, r3 = call(
-        task_kernel, [block(528), block(1040), block(528), block(528)], [ids, learned_sharpness, sizes], [],
-        [e0, e1, e2, e3, r0, r1, r2, r3, terms, back1],
+        task_kernel, [block(528)] * 4, [ids, learned_sharpness, sizes], [],
+        [r0, r1, r2, r3, terms],
     )
     r3, r2, r1 = swap(r3, "r", 3), swap(r2, "r", 2), swap(r1, "r", 1)
     back3, qs = call(from_r_kernel, [block(256), ((4, 144, D), BF)], [ids], [], [r0, r1, r2, r3])
@@ -411,7 +403,7 @@
     xy = lax.all_to_all(xy, ("x", "y", "dp"), 0, 0)
     back5 = swap(back5, "y", 1)
     result = jax.ShapeDtypeStruct((128, 16 * D), BF)
-    args = [stay(a) for a in (z0, own1, r0, r1, r2, r3)]
+    args = [stay(a) for a in (z0, own1, back1, r0, r1, r2, r3)]
     *outs, mine = pl.pallas_call(
         unpack_low_kernel,
         grid=(1,),

time: 139 us -> 138 us (level)
  starting transfers between devices: 72.4 us -> 62.1 us
  blocking collectives: 33 us -> 42 us
    ppermute x5 -> x0, starting transfers between devices: 15.5 us -> none  [send(): return lax.ppermute(array, 'r', [(i, i ^ v) for i in senders])]
    all_to_all x1, blocking collectives: 18.4 us -> 27.4 us  [body(): qs = lax.all_to_all(qs, 'q', 0, 0)]
    ppermute x7 -> x11, starting transfers between devices: 32.1 us -> 37.5 us  [swap(): return lax.ppermute(array, axis, [(i, i ^ v) for i in range(4)])]
    ppermute x7 -> x11, waiting for transfers between devices: 13.2 us -> 14.3 us  [swap(): return lax.ppermute(array, axis, [(i, i ^ v) for i in range(4)])]
  transfers between devices with their start and end apart: 14 -> 13, of which waited for: 4 -> 4; matrix products, arithmetic and copies ran while one was open for 0% -> 0% of each run, Pallas kernels for 6% -> 5%
where the time goes in v6:
time: 138 us; the launch traced here: 137 us
  starting transfers between devices  62.1 us (45%)
  blocking collectives  42 us (30%)
  Pallas kernels  17.6 us (13%)
  waiting for transfers between devices  14.3 us (10%)
    ppermute x11, starting transfers between devices, swap(): return lax.ppermute(array, axis, [(i, i ^ v) for i in range(4)])  37.5 us
    all_to_all x1, blocking collectives, body(): qs = lax.all_to_all(qs, 'q', 0, 0)  27.4 us
    all_to_all x1, starting transfers between devices, body(): qs = lax.all_to_all(qs, 'q', 0, 0)  14.8 us
    all_to_all x1, blocking collectives, body(): xy = lax.all_to_all(xy, ('x', 'y'), 0, 0)  14.6 us
    ppermute x11, waiting for transfers between devices, swap(): return lax.ppermute(array, axis, [(i, i ^ v) for i in range(4)])  14.3 us
    pallas_call x8, Pallas kernels, call(): return run(*scalars, *args)  12.3 us
    all_to_all x1, starting transfers between devices, body(): xy = lax.all_to_all(xy, ('x', 'y', 'dp'), 0, 0)  9.9 us
  transfers between devices with their start and end apart: 13, of which 4 were waited for; matrix products, arithmetic and copies ran while one was open for 0% of the time, Pallas kernels for 5%

profile of v6, /device:TPU:1, one launch (start us, length us, event | category | flops | bytes accessed | tf_op | source)
XLA Modules:
  0.0 137.0 jit_solution(4069279811949223311)
XLA Ops:
  0.6 0.1 pad_add_fusion.ids
  0.7 0.0 copy-start
  0.7 0.0 copy-start.1
  0.7 0.0 copy-start.2
  0.7 0.0 copy-start.3
  0.7 1.6 %pack.1 = bf16[8,96,128]{2,1,0:T(8,128)(2,1)S(1)} custom-call(s32[2]{0:T(128)S(1)} %pad_add_fusion.ids, bf16[128,2048]{1,0:T(8,128)(2,1)} %bitcast.12, bf16[128,2048]{1,0:T(8,128)(2,1)} %bitcast.18, bf16[128,2048]{1,0:T(8,128)(2,1)} %bitcast.24, bf16[128,2048]{1,0:T(8,128)(2,1)} %bitcast.30), custom_call_target="tpu_custom_call" | custom-call | tf_op jit(solution)/shard_map/pack/pallas_call | solution.py:370
  2.4 14.6 %all_to_all.20.xy_ref = bf16[8,96,128]{2,1,0:T(8,128)(2,1)S(1)} all-to-all(bf16[8,96,128]{2,1,0:T(8,128)(2,1)S(1)} %pack.1), channel_id=1, replica_groups=mesh['x'=2,'y'=4,'q'=4,'r'=4,'dp'=4] {'x','y'}, dimensions={0} | all-to-all | bytes 393216 | tf_op jit(solution)/shard_map/all_to_all | solution.py:379
  17.0 0.0 copy-done
  17.0 0.0 copy-done.1
  17.0 0.0 copy-done.2
  17.0 0.0 copy-done.3
  17.0 1.5 %shard_map.104 = bf16[4,128,128]{2,1,0:T(8,128)(2,1)} custom-call(s32[2]{0:T(128)S(1)} %pad_add_fusion.ids, bf16[128,2048]{1,0:T(8,128)(2,1)S(1)} %bitcast.13, bf16[128,2048]{1,0:T(8,128)(2,1)S(1)} %bitcast.19, bf16[128,2048]{1,0:T(8,128)(2,1)S(1)} %bitcast.25, bf16[128,2048]{1,0:T(8,128)(2,1)S(1)} %bitcast.31, bf16[8,96,128]{2,1,0:T(8,128)(2,1)S(1)} %all_to_all.20.xy_ref), custom_call_target="tpu_custom_call" | custom-call | tf_op jit(solution)/shard_map/pallas_call | solution.py:358
  18.4 14.8 %all-to-all-start.1 = ((bf16[4,128,128]{2,1,0:T(8,128)(2,1)}), bf16[4,128,128]{2,1,0:T(8,128)(2,1)S(1)}, u32[]{:S(2)}, u32[]{:S(2)}) async-start(bf16[4,128,128]{2,1,0:T(8,128)(2,1)} %shard_map.104), calls=%async_computation.1 | async-start | bytes 262144 | tf_op jit(solution)/shard_map/all_to_all | solution.py:385
  33.2 0.7 shard_map.102
  33.9 7.3 %collective-permute-start.2 = (bf16[256,128]{1,0:T(8,128)(2,1)S(1)}, bf16[256,128]{1,0:T(8,128)(2,1)S(1)}, u32[]{:S(2)}, u32[]{:S(2)}) collective-permute-start(bf16[256,128]{1,0:T(8,128)(2,1)S(1)} %get-tuple-element.39), channel_id=1, source_target_pairs={{0,16},{16,0},{32,48},{48,32},{1,17},{17,1},{33,49},{49,33},{2,18}... | collective-permute-start | bytes 196616 | tf_op jit(solution)/shard_map/ppermute | solution.py:362
  41.2 2.6 %collective-permute-start = (bf16[512,128]{1,0:T(8,128)(2,1)S(1)}, bf16[512,128]{1,0:T(8,128)(2,1)S(1)}, u32[]{:S(2)}, u32[]{:S(2)}) collective-permute-start(bf16[512,128]{1,0:T(8,128)(2,1)S(1)} %get-tuple-element.35), channel_id=1, source_target_pairs={{0,4},{4,0},{8,12},{12,8},{1,5},{5,1},{9,13},{13,9},{2,6},{6,2},{1... | collective-permute-start | bytes 393224 | tf_op jit(solution)/shard_map/ppermute | solution.py:362
  43.9 4.2 %collective-permute-done.2.g3_ref = bf16[256,128]{1,0:T(8,128)(2,1)S(1)} collective-permute-done((bf16[256,128]{1,0:T(8,128)(2,1)S(1)}, bf16[256,128]{1,0:T(8,128)(2,1)S(1)}, u32[]{:S(2)}, u32[]{:S(2)}) %collective-permute-start.2) | collective-permute-done | bytes 65568 | tf_op jit(solution)/shard_map/ppermute | solution.py:362
  48.1 0.0 all-to-all-done.1.qr_ref
  48.1 0.7 shard_map.105
  48.8 1.9 %collective-permute-start.3 = (bf16[512,128]{1,0:T(8,128)(2,1)S(1)}, bf16[512,128]{1,0:T(8,128)(2,1)S(1)}, u32[]{:S(2)}, u32[]{:S(2)}) collective-permute-start(bf16[512,128]{1,0:T(8,128)(2,1)S(1)} %get-tuple-element.41), channel_id=1, source_target_pairs={{0,4},{4,0},{8,12},{12,8},{1,5},{5,1},{9,13},{13,9},{2,6},{6,2},{1... | collective-permute-start | bytes 393224 | tf_op jit(solution)/shard_map/ppermute | solution.py:362
  50.8 1.9 %collective-permute-start.4 = (bf16[512,128]{1,0:T(8,128)(2,1)S(1)}, bf16[512,128]{1,0:T(8,128)(2,1)S(1)}, u32[]{:S(2)}, u32[]{:S(2)}) collective-permute-start(bf16[512,128]{1,0:T(8,128)(2,1)S(1)} %get-tuple-element.42), channel_id=1, source_target_pairs={{0,8},{4,12},{8,0},{12,4},{1,9},{5,13},{9,1},{13,5},{2,10},{6,14},... | collective-permute-start | bytes 393224 | tf_op jit(solution)/shard_map/ppermute | solution.py:362
  52.7 0.0 copy-start.4
  52.7 0.0 copy-start.5
  52.7 5.4 %collective-permute-start.5 = (bf16[512,128]{1,0:T(8,128)(2,1)S(1)}, bf16[512,128]{1,0:T(8,128)(2,1)S(1)}, u32[]{:S(2)}, u32[]{:S(2)}) collective-permute-start(bf16[512,128]{1,0:T(8,128)(2,1)S(1)} %get-tuple-element.43), channel_id=1, source_target_pairs={{0,12},{4,8},{8,4},{12,0},{1,13},{5,9},{9,5},{13,1},{2,14},{6,10},... | collective-permute-start | bytes 393224 | tf_op jit(solution)/shard_map/ppermute | solution.py:362
  58.1 0.0 copy-done.4
  58.1 0.0 copy-done.5
  58.2 1.9 %shard_map.101 = (bf16[512,256]{1,0:T(8,128)(2,1)S(1)}, f32[8,128]{1,0:T(8,128)S(1)}) custom-call(s32[2]{0:T(128)S(1)} %pad_add_fusion.ids, f32[16]{0:T(128)S(1)} %copy-done.4, s32[8]{0:T(128)S(1)} %bitcast.36, bf16[128,2048]{1,0:T(8,128)(2,1)S(1)} %bitcast.16, bf16[128,2048]{1,0:T(8,128)(2,1)S(1)} %bitcast.22, bf16[128,2048]{1,0:T(8,128)(2,1)S(1)} %bitcast.28, ...), custom_call_target="tpu_custom_call" | custom-call | tf_op jit(solution)/shard_map/pallas_call | solution.py:358
  60.1 0.0 collective-permute-done.g1_ref
  60.1 1.9 %shard_map.103 = (bf16[512,128]{1,0:T(8,128)(2,1)S(1)}, bf16[512,128]{1,0:T(8,128)(2,1)S(1)}, f32[8,128]{1,0:T(8,128)S(1)}) custom-call(s32[2]{0:T(128)S(1)} %pad_add_fusion.ids, f32[16]{0:T(128)S(1)} %copy-done.4, s32[8]{0:T(128)S(1)} %bitcast.37, bf16[128,2048]{1,0:T(8,128)(2,1)S(1)} %bitcast.17, bf16[128,2048]{1,0:T(8,128)(2,1)S(1)} %bitcast.23, ...), custom_call_target="tpu_custom_call" | custom-call | tf_op jit(solution)/shard_map/pallas_call | solution.py:358
  61.9 0.0 collective-permute-done.3.i1
  62.0 0.0 collective-permute-done.4.i2
  62.0 0.0 collective-permute-done.5.i3
  62.0 3.6 %shard_map.106 = (bf16[528,128]{1,0:T(8,128)(2,1)S(1)}, bf16[528,128]{1,0:T(8,128)(2,1)S(1)}, bf16[528,128]{1,0:T(8,128)(2,1)S(1)}, bf16[528,128]{1,0:T(8,128)(2,1)S(1)}) custom-call(s32[2]{0:T(128)S(1)} %pad_add_fusion.ids, f32[16]{0:T(128)S(1)} %copy-done.4, s32[8]{0:T(128)S(1)} %bitcast.38, bf16[512,128]{1,0:T(8,128)(2,1)S(1)} %get-tuple-element.40.i0, ...), custom_call_target="tpu_custom_call" | custom-call | tf_op jit(solution)/shard_map/pallas_call | solution.py:358
  65.5 1.9 %collective-permute-start.6 = (bf16[528,128]{1,0:T(8,128)(2,1)S(1)}, bf16[528,128]{1,0:T(8,128)(2,1)S(1)}, u32[]{:S(2)}, u32[]{:S(2)}) collective-permute-start(bf16[528,128]{1,0:T(8,128)(2,1)S(1)} %get-tuple-element.46), channel_id=1, source_target_pairs={{0,4},{4,0},{8,12},{12,8},{1,5},{5,1},{9,13},{13,9},{2,6},{6,2},{1... | collective-permute-start | bytes 405512 | tf_op jit(solution)/shard_map/ppermute | solution.py:362
  67.5 3.9 %collective-permute-start.7 = (bf16[528,128]{1,0:T(8,128)(2,1)S(1)}, bf16[528,128]{1,0:T(8,128)(2,1)S(1)}, u32[]{:S(2)}, u32[]{:S(2)}) collective-permute-start(bf16[528,128]{1,0:T(8,128)(2,1)S(1)} %get-tuple-element.47), channel_id=1, source_target_pairs={{0,8},{4,12},{8,0},{12,4},{1,9},{5,13},{9,1},{13,5},{2,10},{6,14},... | collective-permute-start | bytes 405512 | tf_op jit(solution)/shard_map/ppermute | solution.py:362
  71.4 3.4 %collective-permute-start.8 = (bf16[528,128]{1,0:T(8,128)(2,1)S(1)}, bf16[528,128]{1,0:T(8,128)(2,1)S(1)}, u32[]{:S(2)}, u32[]{:S(2)}) collective-permute-start(bf16[528,128]{1,0:T(8,128)(2,1)S(1)} %get-tuple-element.48), channel_id=1, source_target_pairs={{0,12},{4,8},{8,4},{12,0},{1,13},{5,9},{9,5},{13,1},{2,14},{6,10},... | collective-permute-start | bytes 405512 | tf_op jit(solution)/shard_map/ppermute | solution.py:362
  74.8 0.0 collective-permute-done.6.r1.i1
  74.9 0.7 collective-permute-done.7.r2.i2
  75.6 3.9 %collective-permute-done.8.r3.i3 = bf16[528,128]{1,0:T(8,128)(2,1)S(1)} collective-permute-done((bf16[528,128]{1,0:T(8,128)(2,1)S(1)}, bf16[528,128]{1,0:T(8,128)(2,1)S(1)}, u32[]{:S(2)}, u32[]{:S(2)}) %collective-permute-start.8) | collective-permute-done | bytes 135200 | tf_op jit(solution)/shard_map/ppermute | solution.py:362
  79.5 0.6 shard_map.107
  80.1 27.4 %all_to_all.21.in_ref.qr_ref = bf16[4,144,128]{2,1,0:T(8,128)(2,1)S(1)} all-to-all(bf16[4,144,128]{2,1,0:T(8,128)(2,1)S(1)} %get-tuple-element.55), channel_id=1, replica_groups=mesh['x'=2,'y'=4,'q'=4,'r'=4,'dp'=4] {'q'}, dimensions={0} | all-to-all | bytes 294912 | tf_op jit(solution)/shard_map/all_to_all | solution.py:400
  107.4 1.5 %shard_map.108 = (bf16[64,128]{1,0:T(8,128)(2,1)S(1)}, bf16[32,48,128]{2,1,0:T(8,128)(2,1)}) custom-call(s32[2]{0:T(128)S(1)} %pad_add_fusion.ids, bf16[4,144,128]{2,1,0:T(8,128)(2,1)S(1)} %all_to_all.21.in_ref.qr_ref), custom_call_target="tpu_custom_call" | custom-call | tf_op jit(solution)/shard_map/pallas_call | solution.py:358
  108.9 9.9 %all-to-all-start.3 = ((bf16[32,48,128]{2,1,0:T(8,128)(2,1)}), bf16[32,48,128]{2,1,0:T(8,128)(2,1)S(1)}, u32[]{:S(2)}, u32[]{:S(2)}) async-start(bf16[32,48,128]{2,1,0:T(8,128)(2,1)} %get-tuple-element.57), calls=%async_computation.3 | async-start | bytes 786432 | tf_op jit(solution)/shard_map/all_to_all | solution.py:403
  118.8 3.0 %collective-permute-start.1 = (bf16[512,128]{1,0:T(8,128)(2,1)S(1)}, bf16[512,128]{1,0:T(8,128)(2,1)S(1)}, u32[]{:S(2)}, u32[]{:S(2)}) collective-permute-start(bf16[512,128]{1,0:T(8,128)(2,1)S(1)} %get-tuple-element.38), channel_id=1, source_target_pairs={{0,4},{4,0},{8,12},{12,8},{1,5},{5,1},{9,13},{13,9},{2,6},{6,2},{1... | collective-permute-start | bytes 393224 | tf_op jit(solution)/shard_map/ppermute | solution.py:362
  121.8 2.7 %collective-permute-start.9 = (bf16[256,128]{1,0:T(8,128)(2,1)S(1)}, bf16[256,128]{1,0:T(8,128)(2,1)S(1)}, u32[]{:S(2)}, u32[]{:S(2)}) collective-permute-start(bf16[256,128]{1,0:T(8,128)(2,1)S(1)} %get-tuple-element.54), channel_id=1, source_target_pairs={{0,16},{16,0},{32,48},{48,32},{1,17},{17,1},{33,49},{49,33},{2,18}... | collective-permute-start | bytes 196616 | tf_op jit(solution)/shard_map/ppermute | solution.py:362
  124.5 3.3 %collective-permute-start.10 = (bf16[64,128]{1,0:T(8,128)(2,1)S(1)}, bf16[64,128]{1,0:T(8,128)(2,1)S(1)}, u32[]{:S(2)}, u32[]{:S(2)}) collective-permute-start(bf16[64,128]{1,0:T(8,128)(2,1)S(1)} %get-tuple-element.56), channel_id=1, source_target_pairs={{0,64},{64,0},{128,192},{192,128},{1,65},{65,1},{129,193},{193,129... | collective-permute-start | bytes 49160 | tf_op jit(solution)/shard_map/ppermute | solution.py:362
  127.8 0.0 collective-permute-done.1.g1_ref
  127.8 1.7 %unpack_low.1 = (bf16[128,2048]{1,0:T(8,128)(2,1)}, bf16[128,2048]{1,0:T(8,128)(2,1)}, bf16[128,2048]{1,0:T(8,128)(2,1)}, bf16[128,2048]{1,0:T(8,128)(2,1)}, bf16[4,128,128]{2,1,0:T(8,128)(2,1)S(1)}) custom-call(s32[2]{0:T(128)S(1)} %pad_add_fusion.ids, bf16[512,256]{1,0:T(8,128)(2,1)S(1)} %get-tuple-element.34.z0_ref, ...), custom_call_target="tpu_custom_call" | custom-call | tf_op jit(solution)/shard_map/unpack_low/pallas_call | solution.py:407
  129.6 5.5 %collective-permute-done.9.g3_ref = bf16[256,128]{1,0:T(8,128)(2,1)S(1)} collective-permute-done((bf16[256,128]{1,0:T(8,128)(2,1)S(1)}, bf16[256,128]{1,0:T(8,128)(2,1)S(1)}, u32[]{:S(2)}, u32[]{:S(2)}) %collective-permute-start.9) | collective-permute-done | bytes 65568 | tf_op jit(solution)/shard_map/ppermute | solution.py:362
  135.0 0.0 collective-permute-done.10.g5_ref
  135.0 0.0 all-to-all-done.3.xy_ref
  135.0 2.0 %unpack_high.1 = (bf16[128,2048]{1,0:T(8,128)(2,1)}, bf16[128,2048]{1,0:T(8,128)(2,1)}, bf16[128,2048]{1,0:T(8,128)(2,1)}, bf16[128,2048]{1,0:T(8,128)(2,1)}, f32[1,16]{1,0:T(1,128)}) custom-call(s32[2]{0:T(128)S(1)} %pad_add_fusion.ids, ...), custom_call_target="tpu_custom_call", output_to_operand_aliasing={{0}: (1, {}), {1}: (2, {}), {2}: (3, {}), {3}: (4, {})} | custom-call | tf_op jit(solution)/shard_map/unpack_high/pallas_call | solution.py:418
Async XLA Ops:
  0.7 16.2 %copy-start = (bf16[1,128,2048]{2,1,0:T(8,128)(2,1)S(1)}, bf16[1,128,2048]{2,1,0:T(8,128)(2,1)}, u32[]{:S(2)}) copy-start(bf16[1,128,2048]{2,1,0:T(8,128)(2,1)} %param.6) | copy-start | bytes 1572868
  0.7 16.2 %copy-start.1 = (bf16[1,128,2048]{2,1,0:T(8,128)(2,1)S(1)}, bf16[1,128,2048]{2,1,0:T(8,128)(2,1)}, u32[]{:S(2)}) copy-start(bf16[1,128,2048]{2,1,0:T(8,128)(2,1)} %param.7) | copy-start | bytes 1572868
  0.7 16.2 %copy-start.2 = (bf16[1,128,2048]{2,1,0:T(8,128)(2,1)S(1)}, bf16[1,128,2048]{2,1,0:T(8,128)(2,1)}, u32[]{:S(2)}) copy-start(bf16[1,128,2048]{2,1,0:T(8,128)(2,1)} %param.8) | copy-start | bytes 1572868
  0.7 16.2 %copy-start.3 = (bf16[1,128,2048]{2,1,0:T(8,128)(2,1)S(1)}, bf16[1,128,2048]{2,1,0:T(8,128)(2,1)}, u32[]{:S(2)}) copy-start(bf16[1,128,2048]{2,1,0:T(8,128)(2,1)} %param.9) | copy-start | bytes 1572868
  18.4 29.6 %all-to-all-start.1 = ((bf16[4,128,128]{2,1,0:T(8,128)(2,1)}), bf16[4,128,128]{2,1,0:T(8,128)(2,1)S(1)}, u32[]{:S(2)}, u32[]{:S(2)}) async-start(bf16[4,128,128]{2,1,0:T(8,128)(2,1)} %shard_map.104), calls=%async_computation.1 | async-start | bytes 262144 | tf_op jit(solution)/shard_map/all_to_all | solution.py:385
  33.9 14.1 %collective-permute-start.2 = (bf16[256,128]{1,0:T(8,128)(2,1)S(1)}, bf16[256,128]{1,0:T(8,128)(2,1)S(1)}, u32[]{:S(2)}, u32[]{:S(2)}) collective-permute-start(bf16[256,128]{1,0:T(8,128)(2,1)S(1)} %get-tuple-element.39), channel_id=1, source_target_pairs={{0,16},{16,0},{32,48},{48,32},{1,17},{17,1},{33,49},{49,33},{2,18}... | collective-permute-start | bytes 196616 | tf_op jit(solution)/shard_map/ppermute | solution.py:362
  41.2 18.8 %collective-permute-start = (bf16[512,128]{1,0:T(8,128)(2,1)S(1)}, bf16[512,128]{1,0:T(8,128)(2,1)S(1)}, u32[]{:S(2)}, u32[]{:S(2)}) collective-permute-start(bf16[512,128]{1,0:T(8,128)(2,1)S(1)} %get-tuple-element.35), channel_id=1, source_target_pairs={{0,4},{4,0},{8,12},{12,8},{1,5},{5,1},{9,13},{13,9},{2,6},{6,2},{1... | collective-permute-start | bytes 393224 | tf_op jit(solution)/shard_map/ppermute | solution.py:362
  48.8 13.1 %collective-permute-start.3 = (bf16[512,128]{1,0:T(8,128)(2,1)S(1)}, bf16[512,128]{1,0:T(8,128)(2,1)S(1)}, u32[]{:S(2)}, u32[]{:S(2)}) collective-permute-start(bf16[512,128]{1,0:T(8,128)(2,1)S(1)} %get-tuple-element.41), channel_id=1, source_target_pairs={{0,4},{4,0},{8,12},{12,8},{1,5},{5,1},{9,13},{13,9},{2,6},{6,2},{1... | collective-permute-start | bytes 393224 | tf_op jit(solution)/shard_map/ppermute | solution.py:362
  50.8 11.2 %collective-permute-start.4 = (bf16[512,128]{1,0:T(8,128)(2,1)S(1)}, bf16[512,128]{1,0:T(8,128)(2,1)S(1)}, u32[]{:S(2)}, u32[]{:S(2)}) collective-permute-start(bf16[512,128]{1,0:T(8,128)(2,1)S(1)} %get-tuple-element.42), channel_id=1, source_target_pairs={{0,8},{4,12},{8,0},{12,4},{1,9},{5,13},{9,1},{13,5},{2,10},{6,14},... | collective-permute-start | bytes 393224 | tf_op jit(solution)/shard_map/ppermute | solution.py:362
  52.7 5.4 %copy-start.4 = (f32[16]{0:T(128)S(1)}, f32[16]{0:T(128)}, u32[]{:S(2)}) copy-start(f32[16]{0:T(128)} %sharp.5) | copy-start | bytes 196
  52.7 5.4 %copy-start.5 = (s32[1,8]{1,0:T(1,128)S(1)}, s32[1,8]{1,0:T(1,128)}, u32[]{:S(2)}) copy-start(s32[1,8]{1,0:T(1,128)} %param.11) | copy-start | bytes 100
  52.7 9.2 %collective-permute-start.5 = (bf16[512,128]{1,0:T(8,128)(2,1)S(1)}, bf16[512,128]{1,0:T(8,128)(2,1)S(1)}, u32[]{:S(2)}, u32[]{:S(2)}) collective-permute-start(bf16[512,128]{1,0:T(8,128)(2,1)S(1)} %get-tuple-element.43), channel_id=1, source_target_pairs={{0,12},{4,8},{8,4},{12,0},{1,13},{5,9},{9,5},{13,1},{2,14},{6,10},... | collective-permute-start | bytes 393224 | tf_op jit(solution)/shard_map/ppermute | solution.py:362
  65.5 9.3 %collective-permute-start.6 = (bf16[528,128]{1,0:T(8,128)(2,1)S(1)}, bf16[528,128]{1,0:T(8,128)(2,1)S(1)}, u32[]{:S(2)}, u32[]{:S(2)}) collective-permute-start(bf16[528,128]{1,0:T(8,128)(2,1)S(1)} %get-tuple-element.46), channel_id=1, source_target_pairs={{0,4},{4,0},{8,12},{12,8},{1,5},{5,1},{9,13},{13,9},{2,6},{6,2},{1... | collective-permute-start | bytes 405512 | tf_op jit(solution)/shard_map/ppermute | solution.py:362
  67.5 8.1 %collective-permute-start.7 = (bf16[528,128]{1,0:T(8,128)(2,1)S(1)}, bf16[528,128]{1,0:T(8,128)(2,1)S(1)}, u32[]{:S(2)}, u32[]{:S(2)}) collective-permute-start(bf16[528,128]{1,0:T(8,128)(2,1)S(1)} %get-tuple-element.47), channel_id=1, source_target_pairs={{0,8},{4,12},{8,0},{12,4},{1,9},{5,13},{9,1},{13,5},{2,10},{6,14},... | collective-permute-start | bytes 405512 | tf_op jit(solution)/shard_map/ppermute | solution.py:362
  71.4 8.0 %collective-permute-start.8 = (bf16[528,128]{1,0:T(8,128)(2,1)S(1)}, bf16[528,128]{1,0:T(8,128)(2,1)S(1)}, u32[]{:S(2)}, u32[]{:S(2)}) collective-permute-start(bf16[528,128]{1,0:T(8,128)(2,1)S(1)} %get-tuple-element.48), channel_id=1, source_target_pairs={{0,12},{4,8},{8,4},{12,0},{1,13},{5,9},{9,5},{13,1},{2,14},{6,10},... | collective-permute-start | bytes 405512 | tf_op jit(solution)/shard_map/ppermute | solution.py:362
  108.9 26.1 %all-to-all-start.3 = ((bf16[32,48,128]{2,1,0:T(8,128)(2,1)}), bf16[32,48,128]{2,1,0:T(8,128)(2,1)S(1)}, u32[]{:S(2)}, u32[]{:S(2)}) async-start(bf16[32,48,128]{2,1,0:T(8,128)(2,1)} %get-tuple-element.57), calls=%async_computation.3 | async-start | bytes 786432 | tf_op jit(solution)/shard_map/all_to_all | solution.py:403
  118.8 9.0 %collective-permute-start.1 = (bf16[512,128]{1,0:T(8,128)(2,1)S(1)}, bf16[512,128]{1,0:T(8,128)(2,1)S(1)}, u32[]{:S(2)}, u32[]{:S(2)}) collective-permute-start(bf16[512,128]{1,0:T(8,128)(2,1)S(1)} %get-tuple-element.38), channel_id=1, source_target_pairs={{0,4},{4,0},{8,12},{12,8},{1,5},{5,1},{9,13},{13,9},{2,6},{6,2},{1... | collective-permute-start | bytes 393224 | tf_op jit(solution)/shard_map/ppermute | solution.py:362
  121.8 13.2 %collective-permute-start.9 = (bf16[256,128]{1,0:T(8,128)(2,1)S(1)}, bf16[256,128]{1,0:T(8,128)(2,1)S(1)}, u32[]{:S(2)}, u32[]{:S(2)}) collective-permute-start(bf16[256,128]{1,0:T(8,128)(2,1)S(1)} %get-tuple-element.54), channel_id=1, source_target_pairs={{0,16},{16,0},{32,48},{48,32},{1,17},{17,1},{33,49},{49,33},{2,18}... | collective-permute-start | bytes 196616 | tf_op jit(solution)/shard_map/ppermute | solution.py:362
  124.5 10.5 %collective-permute-start.10 = (bf16[64,128]{1,0:T(8,128)(2,1)S(1)}, bf16[64,128]{1,0:T(8,128)(2,1)S(1)}, u32[]{:S(2)}, u32[]{:S(2)}) collective-permute-start(bf16[64,128]{1,0:T(8,128)(2,1)S(1)} %get-tuple-element.56), channel_id=1, source_target_pairs={{0,64},{64,0},{128,192},{192,128},{1,65},{65,1},{129,193},{193,129... | collective-permute-start | bytes 49160 | tf_op jit(solution)/shard_map/ppermute | solution.py:362

commit v7 on v6

--- a/solution.py
+++ b/solution.py
@@ -60,11 +60,15 @@
     return jnp.where(y < 2, six, jnp.where(y == 2, seven, -1))
 
 
-def pack_kernel(ids, q_ref, k_ref, v_ref, u_ref, xy_ref):
-    x, y, _, _ = xyqr(ids[0])
+def pack_kernel(ids, q6_ref, k6_ref, v6_ref, u6_ref, q_ref, k_ref, v_ref, u_ref, g3_ref, xy_ref):
+    x, y, q, _ = xyqr(ids[0])
     srcs = (q_ref, k_ref, v_ref, u_ref)
     j5 = 1 - (y & 1)
     s5 = pick(5, j5)
+    j3 = 1 - (q & 1)
+    s3 = pick(3, j3)
+    for t, ref in enumerate((q6_ref, k6_ref, v6_ref, u6_ref)):
+        g3_ref[t * 64 : (t + 1) * 64] = mm(s3, cols(ref, j3)).astype(BF)
     xy_ref[...] = jnp.zeros(xy_ref.shape, BF)
     for t, ref in enumerate(srcs):
         xy_ref[x * 4 + (y ^ 1), 32 + t * 16 : 48 + t * 16] = mm(s5, cols(ref, 2 + j5)).astype(BF)
@@ -95,14 +99,10 @@
     out_ref[3] = mm(perm, xy_ref[:, 0:32].reshape(256, D)).astype(BF)
 
 
-def early_kernel(ids, q_ref, k_ref, v_ref, u_ref, g1_ref, g3_ref):
-    _, _, q, r = xyqr(ids[0])
-    j3 = 1 - (q & 1)
-    h1 = 3 - (r & 1)
-    s3 = pick(3, j3)
+def early_kernel(ids, q_ref, k_ref, v_ref, u_ref, g1_ref):
+    h1 = 3 - (ids[0] & 1)
     for t, ref in enumerate((q_ref, k_ref, v_ref, u_ref)):
         g1_ref[t * 128 : (t + 1) * 128] = cols(ref, h1)
-        g3_ref[t * 64 : (t + 1) * 64] = mm(s3, cols(ref, 6 + j3)).astype(BF)
 
 
 def to_r_kernel(ids, q_ref, k_ref, v_ref, u_ref, g3_ref, qr_ref, own_ref, t1_ref, t2_ref, t3_ref, tmp):
@@ -367,23 +367,25 @@
     ids = jnp.stack([lax.axis_index(SEQ), lax.axis_index("dp")]).astype(jnp.int32)
     block = lambda n: ((n, D), BF)
     held = [pltpu.with_memory_space_constraint(a, pltpu.HBM) for a in raw]
-    xy = pl.pallas_call(
+    g3, xy = pl.pallas_call(
         pack_kernel,
         grid=(1,),
-        in_specs=[SMEM] + [pl.BlockSpec((128, 8 * D), lambda i: (0, 1))] * 4,
-        out_specs=pl.BlockSpec((8, 96, D), lambda i: (0, 0, 0)),
-        out_shape=jax.ShapeDtypeStruct((8, 96, D), BF),
+        in_specs=[SMEM]
+        + [pl.BlockSpec((128, 2 * D), lambda i: (0, 3))] * 4
+        + [pl.BlockSpec((128, 8 * D), lambda i: (0, 1))] * 4,
+        out_specs=[pl.BlockSpec((256, D), lambda i: (0, 0)), pl.BlockSpec((8, 96, D), lambda i: (0, 0, 0))],
+        out_shape=[jax.ShapeDtypeStruct((256, D), BF), jax.ShapeDtypeStruct((8, 96, D), BF)],
         compiler_params=LIMIT,
         name="pack",
-    )(ids, *held)
+    )(ids, *held, *held)
+    g3 = swap(g3, "q", 1)
     xy = lax.all_to_all(xy, ("x", "y"), 0, 0)
     four = [stay(a) for a in raw]
     sizes = reply_list_sizes[0]
     z0, terms = call(local_kernel, [((512, 2 * D), BF), ((8, 128), F32)], [ids, learned_sharpness, sizes], four, [])
-    g1, g3 = call(early_kernel, [block(512), block(256)], [ids], four, [])
+    g1 = call(early_kernel, [block(512)], [ids], four, [])
     qs = call(to_q_kernel, [((4, 128, D), BF)], [ids], four, [xy])
     qs = lax.all_to_all(qs, "q", 0, 0)
-    g3 = swap(g3, "q", 1)
     g1 = swap(g1, "r", 1)
     r0, r1, r2, r3 = call(to_r_kernel, [block(512)] * 4, [ids], four, [g3, qs], [pltpu.VMEM((4, 512, D), BF)])
     r1, r3, r2 = swap(r1, "r", 1), swap(r3, "r", 3), swap(r2, "r", 2)

time: 138 us -> 138 us (level)
  blocking collectives: 42 us -> 38.1 us
  waiting for transfers between devices: 14.3 us -> 17.3 us
    all_to_all x1, blocking collectives: 27.4 us -> 23.5 us  [body(): qs = lax.all_to_all(qs, 'q', 0, 0)]
    ppermute x11, waiting for transfers between devices: 14.3 us -> 17.3 us  [swap(): return lax.ppermute(array, axis, [(i, i ^ v) for i in range(4)])]
where the time goes in v7:
time: 138 us; the launch traced here: 137 us
  starting transfers between devices  63.2 us (46%)
  blocking collectives  38.1 us (28%)
  Pallas kernels  17.7 us (13%)
  waiting for transfers between devices  17.3 us (13%)
    ppermute x11, starting transfers between devices, swap(): return lax.ppermute(array, axis, [(i, i ^ v) for i in range(4)])  38.4 us
    all_to_all x1, blocking collectives, body(): qs = lax.all_to_all(qs, 'q', 0, 0)  23.5 us
    ppermute x11, waiting for transfers between devices, swap(): return lax.ppermute(array, axis, [(i, i ^ v) for i in range(4)])  17.3 us
    all_to_all x1, starting transfers between devices, body(): qs = lax.all_to_all(qs, 'q', 0, 0)  14.8 us
    all_to_all x1, blocking collectives, body(): xy = lax.all_to_all(xy, ('x', 'y'), 0, 0)  14.6 us
    pallas_call x8, Pallas kernels, call(): return run(*scalars, *args)  12.2 us
    all_to_all x1, starting transfers between devices, body(): xy = lax.all_to_all(xy, ('x', 'y', 'dp'), 0, 0)  9.99 us
  transfers between devices with their start and end apart: 13, of which 4 were waited for; matrix products, arithmetic and copies ran while one was open for 0% of the time, Pallas kernels for 5%

profile of v7, /device:TPU:1, one launch (start us, length us, event | category | flops | bytes accessed | tf_op | source)
XLA Modules:
  0.0 137.2 jit_solution(10962103570293730146)
XLA Ops:
  0.6 0.1 pad_add_fusion.ids
  0.7 0.0 copy-start
  0.7 0.0 copy-start.1
  0.7 0.0 copy-start.2
  0.7 0.0 copy-start.3
  0.7 1.8 %pack.1 = (bf16[256,128]{1,0:T(8,128)(2,1)S(1)}, bf16[8,96,128]{2,1,0:T(8,128)(2,1)S(1)}) custom-call(s32[2]{0:T(128)S(1)} %pad_add_fusion.ids, bf16[128,2048]{1,0:T(8,128)(2,1)} %bitcast.12, bf16[128,2048]{1,0:T(8,128)(2,1)} %bitcast.19, bf16[128,2048]{1,0:T(8,128)(2,1)} %bitcast.26, bf16[128,2048]{1,0:T(8,128)(2,1)} %bitcast.33, ...), custom_call_target="tpu_custom_call" | custom-call | tf_op jit(solution)/shard_map/pack/pallas_call | solution.py:370
  2.5 14.6 %all_to_all.20.xy_ref = bf16[8,96,128]{2,1,0:T(8,128)(2,1)S(1)} all-to-all(bf16[8,96,128]{2,1,0:T(8,128)(2,1)S(1)} %get-tuple-element.39), channel_id=1, replica_groups=mesh['x'=2,'y'=4,'q'=4,'r'=4,'dp'=4] {'x','y'}, dimensions={0} | all-to-all | bytes 393216 | tf_op jit(solution)/shard_map/all_to_all | solution.py:382
  17.1 0.0 copy-done
  17.1 0.0 copy-done.1
  17.1 0.0 copy-done.2
  17.1 0.0 copy-done.3
  17.2 1.5 %shard_map.104 = bf16[4,128,128]{2,1,0:T(8,128)(2,1)} custom-call(s32[2]{0:T(128)S(1)} %pad_add_fusion.ids, bf16[128,2048]{1,0:T(8,128)(2,1)S(1)} %bitcast.14, bf16[128,2048]{1,0:T(8,128)(2,1)S(1)} %bitcast.21, bf16[128,2048]{1,0:T(8,128)(2,1)S(1)} %bitcast.28, bf16[128,2048]{1,0:T(8,128)(2,1)S(1)} %bitcast.35, bf16[8,96,128]{2,1,0:T(8,128)(2,1)S(1)} %all_to_all.20.xy_ref), custom_call_target="tpu_custom_call" | custom-call | tf_op jit(solution)/shard_map/pallas_call | solution.py:358
  18.6 14.8 %all-to-all-start.1 = ((bf16[4,128,128]{2,1,0:T(8,128)(2,1)}), bf16[4,128,128]{2,1,0:T(8,128)(2,1)S(1)}, u32[]{:S(2)}, u32[]{:S(2)}) async-start(bf16[4,128,128]{2,1,0:T(8,128)(2,1)} %shard_map.104), calls=%async_computation.1 | async-start | bytes 262144 | tf_op jit(solution)/shard_map/all_to_all | solution.py:388
  33.4 7.3 %collective-permute-start.2 = (bf16[256,128]{1,0:T(8,128)(2,1)S(1)}, bf16[256,128]{1,0:T(8,128)(2,1)S(1)}, u32[]{:S(2)}, u32[]{:S(2)}) collective-permute-start(bf16[256,128]{1,0:T(8,128)(2,1)S(1)} %get-tuple-element.38), channel_id=1, source_target_pairs={{0,16},{16,0},{32,48},{48,32},{1,17},{17,1},{33,49},{49,33},{2,18}... | collective-permute-start | bytes 196616 | tf_op jit(solution)/shard_map/ppermute | solution.py:362
  40.6 0.6 shard_map.102
  41.2 2.6 %collective-permute-start = (bf16[512,128]{1,0:T(8,128)(2,1)S(1)}, bf16[512,128]{1,0:T(8,128)(2,1)S(1)}, u32[]{:S(2)}, u32[]{:S(2)}) collective-permute-start(bf16[512,128]{1,0:T(8,128)(2,1)S(1)} %shard_map.102), channel_id=1, source_target_pairs={{0,4},{4,0},{8,12},{12,8},{1,5},{5,1},{9,13},{13,9},{2,6},{6,2},{1... | collective-permute-start | bytes 393224 | tf_op jit(solution)/shard_map/ppermute | solution.py:362
  43.9 6.4 %collective-permute-done.2.g3_ref = bf16[256,128]{1,0:T(8,128)(2,1)S(1)} collective-permute-done((bf16[256,128]{1,0:T(8,128)(2,1)S(1)}, bf16[256,128]{1,0:T(8,128)(2,1)S(1)}, u32[]{:S(2)}, u32[]{:S(2)}) %collective-permute-start.2) | collective-permute-done | bytes 65568 | tf_op jit(solution)/shard_map/ppermute | solution.py:362
  50.3 0.0 all-to-all-done.1.qr_ref
  50.3 0.7 shard_map.105
  51.0 1.9 %collective-permute-start.3 = (bf16[512,128]{1,0:T(8,128)(2,1)S(1)}, bf16[512,128]{1,0:T(8,128)(2,1)S(1)}, u32[]{:S(2)}, u32[]{:S(2)}) collective-permute-start(bf16[512,128]{1,0:T(8,128)(2,1)S(1)} %get-tuple-element.41), channel_id=1, source_target_pairs={{0,4},{4,0},{8,12},{12,8},{1,5},{5,1},{9,13},{13,9},{2,6},{6,2},{1... | collective-permute-start | bytes 393224 | tf_op jit(solution)/shard_map/ppermute | solution.py:362
  52.9 1.9 %collective-permute-start.4 = (bf16[512,128]{1,0:T(8,128)(2,1)S(1)}, bf16[512,128]{1,0:T(8,128)(2,1)S(1)}, u32[]{:S(2)}, u32[]{:S(2)}) collective-permute-start(bf16[512,128]{1,0:T(8,128)(2,1)S(1)} %get-tuple-element.42), channel_id=1, source_target_pairs={{0,8},{4,12},{8,0},{12,4},{1,9},{5,13},{9,1},{13,5},{2,10},{6,14},... | collective-permute-start | bytes 393224 | tf_op jit(solution)/shard_map/ppermute | solution.py:362
  54.9 0.0 copy-start.4
  54.9 0.0 copy-start.5
  54.9 5.4 %collective-permute-start.5 = (bf16[512,128]{1,0:T(8,128)(2,1)S(1)}, bf16[512,128]{1,0:T(8,128)(2,1)S(1)}, u32[]{:S(2)}, u32[]{:S(2)}) collective-permute-start(bf16[512,128]{1,0:T(8,128)(2,1)S(1)} %get-tuple-element.43), channel_id=1, source_target_pairs={{0,12},{4,8},{8,4},{12,0},{1,13},{5,9},{9,5},{13,1},{2,14},{6,10},... | collective-permute-start | bytes 393224 | tf_op jit(solution)/shard_map/ppermute | solution.py:362
  60.3 0.0 copy-done.4
  60.3 0.0 copy-done.5
  60.4 1.9 %shard_map.101 = (bf16[512,256]{1,0:T(8,128)(2,1)S(1)}, f32[8,128]{1,0:T(8,128)S(1)}) custom-call(s32[2]{0:T(128)S(1)} %pad_add_fusion.ids, f32[16]{0:T(128)S(1)} %copy-done.4, s32[8]{0:T(128)S(1)} %bitcast.40, bf16[128,2048]{1,0:T(8,128)(2,1)S(1)} %bitcast.17, bf16[128,2048]{1,0:T(8,128)(2,1)S(1)} %bitcast.24, bf16[128,2048]{1,0:T(8,128)(2,1)S(1)} %bitcast.31, ...), custom_call_target="tpu_custom_call" | custom-call | tf_op jit(solution)/shard_map/pallas_call | solution.py:358
  62.2 0.0 collective-permute-done.g1_ref
  62.3 1.9 %shard_map.103 = (bf16[512,128]{1,0:T(8,128)(2,1)S(1)}, bf16[512,128]{1,0:T(8,128)(2,1)S(1)}, f32[8,128]{1,0:T(8,128)S(1)}) custom-call(s32[2]{0:T(128)S(1)} %pad_add_fusion.ids, f32[16]{0:T(128)S(1)} %copy-done.4, s32[8]{0:T(128)S(1)} %bitcast.41, bf16[128,2048]{1,0:T(8,128)(2,1)S(1)} %bitcast.18, bf16[128,2048]{1,0:T(8,128)(2,1)S(1)} %bitcast.25, ...), custom_call_target="tpu_custom_call" | custom-call | tf_op jit(solution)/shard_map/pallas_call | solution.py:358
  64.1 0.0 collective-permute-done.3.i1
  64.1 0.0 collective-permute-done.4.i2
  64.2 0.0 collective-permute-done.5.i3
  64.2 3.6 %shard_map.106 = (bf16[528,128]{1,0:T(8,128)(2,1)S(1)}, bf16[528,128]{1,0:T(8,128)(2,1)S(1)}, bf16[528,128]{1,0:T(8,128)(2,1)S(1)}, bf16[528,128]{1,0:T(8,128)(2,1)S(1)}) custom-call(s32[2]{0:T(128)S(1)} %pad_add_fusion.ids, f32[16]{0:T(128)S(1)} %copy-done.4, s32[8]{0:T(128)S(1)} %bitcast.42, bf16[512,128]{1,0:T(8,128)(2,1)S(1)} %get-tuple-element.40.i0, ...), custom_call_target="tpu_custom_call" | custom-call | tf_op jit(solution)/shard_map/pallas_call | solution.py:358
  67.8 4.2 %collective-permute-start.6 = (bf16[528,128]{1,0:T(8,128)(2,1)S(1)}, bf16[528,128]{1,0:T(8,128)(2,1)S(1)}, u32[]{:S(2)}, u32[]{:S(2)}) collective-permute-start(bf16[528,128]{1,0:T(8,128)(2,1)S(1)} %get-tuple-element.46), channel_id=1, source_target_pairs={{0,4},{4,0},{8,12},{12,8},{1,5},{5,1},{9,13},{13,9},{2,6},{6,2},{1... | collective-permute-start | bytes 405512 | tf_op jit(solution)/shard_map/ppermute | solution.py:362
  72.0 2.5 %collective-permute-start.7 = (bf16[528,128]{1,0:T(8,128)(2,1)S(1)}, bf16[528,128]{1,0:T(8,128)(2,1)S(1)}, u32[]{:S(2)}, u32[]{:S(2)}) collective-permute-start(bf16[528,128]{1,0:T(8,128)(2,1)S(1)} %get-tuple-element.47), channel_id=1, source_target_pairs={{0,8},{4,12},{8,0},{12,4},{1,9},{5,13},{9,1},{13,5},{2,10},{6,14},... | collective-permute-start | bytes 405512 | tf_op jit(solution)/shard_map/ppermute | solution.py:362
  74.5 3.4 %collective-permute-start.8 = (bf16[528,128]{1,0:T(8,128)(2,1)S(1)}, bf16[528,128]{1,0:T(8,128)(2,1)S(1)}, u32[]{:S(2)}, u32[]{:S(2)}) collective-permute-start(bf16[528,128]{1,0:T(8,128)(2,1)S(1)} %get-tuple-element.48), channel_id=1, source_target_pairs={{0,12},{4,8},{8,4},{12,0},{1,13},{5,9},{9,5},{13,1},{2,14},{6,10},... | collective-permute-start | bytes 405512 | tf_op jit(solution)/shard_map/ppermute | solution.py:362
  77.9 0.0 collective-permute-done.6.r1.i1
  77.9 2.0 %collective-permute-done.7.r2.i2 = bf16[528,128]{1,0:T(8,128)(2,1)S(1)} collective-permute-done((bf16[528,128]{1,0:T(8,128)(2,1)S(1)}, bf16[528,128]{1,0:T(8,128)(2,1)S(1)}, u32[]{:S(2)}, u32[]{:S(2)}) %collective-permute-start.7) | collective-permute-done | bytes 135200 | tf_op jit(solution)/shard_map/ppermute | solution.py:362
  79.9 2.7 %collective-permute-done.8.r3.i3 = bf16[528,128]{1,0:T(8,128)(2,1)S(1)} collective-permute-done((bf16[528,128]{1,0:T(8,128)(2,1)S(1)}, bf16[528,128]{1,0:T(8,128)(2,1)S(1)}, u32[]{:S(2)}, u32[]{:S(2)}) %collective-permute-start.8) | collective-permute-done | bytes 135200 | tf_op jit(solution)/shard_map/ppermute | solution.py:362
  82.6 0.6 shard_map.107
  83.2 23.5 %all_to_all.21.in_ref.qr_ref = bf16[4,144,128]{2,1,0:T(8,128)(2,1)S(1)} all-to-all(bf16[4,144,128]{2,1,0:T(8,128)(2,1)S(1)} %get-tuple-element.55), channel_id=1, replica_groups=mesh['x'=2,'y'=4,'q'=4,'r'=4,'dp'=4] {'q'}, dimensions={0} | all-to-all | bytes 294912 | tf_op jit(solution)/shard_map/all_to_all | solution.py:402
  106.7 1.5 %shard_map.108 = (bf16[64,128]{1,0:T(8,128)(2,1)S(1)}, bf16[32,48,128]{2,1,0:T(8,128)(2,1)}) custom-call(s32[2]{0:T(128)S(1)} %pad_add_fusion.ids, bf16[4,144,128]{2,1,0:T(8,128)(2,1)S(1)} %all_to_all.21.in_ref.qr_ref), custom_call_target="tpu_custom_call" | custom-call | tf_op jit(solution)/shard_map/pallas_call | solution.py:358
  108.1 10.0 %all-to-all-start.3 = ((bf16[32,48,128]{2,1,0:T(8,128)(2,1)}), bf16[32,48,128]{2,1,0:T(8,128)(2,1)S(1)}, u32[]{:S(2)}, u32[]{:S(2)}) async-start(bf16[32,48,128]{2,1,0:T(8,128)(2,1)} %get-tuple-element.57), calls=%async_computation.3 | async-start | bytes 786432 | tf_op jit(solution)/shard_map/all_to_all | solution.py:405
  118.1 3.2 %collective-permute-start.1 = (bf16[512,128]{1,0:T(8,128)(2,1)S(1)}, bf16[512,128]{1,0:T(8,128)(2,1)S(1)}, u32[]{:S(2)}, u32[]{:S(2)}) collective-permute-start(bf16[512,128]{1,0:T(8,128)(2,1)S(1)} %get-tuple-element.37), channel_id=1, source_target_pairs={{0,4},{4,0},{8,12},{12,8},{1,5},{5,1},{9,13},{13,9},{2,6},{6,2},{1... | collective-permute-start | bytes 393224 | tf_op jit(solution)/shard_map/ppermute | solution.py:362
  121.3 2.7 %collective-permute-start.9 = (bf16[256,128]{1,0:T(8,128)(2,1)S(1)}, bf16[256,128]{1,0:T(8,128)(2,1)S(1)}, u32[]{:S(2)}, u32[]{:S(2)}) collective-permute-start(bf16[256,128]{1,0:T(8,128)(2,1)S(1)} %get-tuple-element.54), channel_id=1, source_target_pairs={{0,16},{16,0},{32,48},{48,32},{1,17},{17,1},{33,49},{49,33},{2,18}... | collective-permute-start | bytes 196616 | tf_op jit(solution)/shard_map/ppermute | solution.py:362
  124.0 3.3 %collective-permute-start.10 = (bf16[64,128]{1,0:T(8,128)(2,1)S(1)}, bf16[64,128]{1,0:T(8,128)(2,1)S(1)}, u32[]{:S(2)}, u32[]{:S(2)}) collective-permute-start(bf16[64,128]{1,0:T(8,128)(2,1)S(1)} %get-tuple-element.56), channel_id=1, source_target_pairs={{0,64},{64,0},{128,192},{192,128},{1,65},{65,1},{129,193},{193,129... | collective-permute-start | bytes 49160 | tf_op jit(solution)/shard_map/ppermute | solution.py:362
  127.3 0.0 collective-permute-done.1.g1_ref
  127.3 1.7 %unpack_low.1 = (bf16[128,2048]{1,0:T(8,128)(2,1)}, bf16[128,2048]{1,0:T(8,128)(2,1)}, bf16[128,2048]{1,0:T(8,128)(2,1)}, bf16[128,2048]{1,0:T(8,128)(2,1)}, bf16[4,128,128]{2,1,0:T(8,128)(2,1)S(1)}) custom-call(s32[2]{0:T(128)S(1)} %pad_add_fusion.ids, bf16[512,256]{1,0:T(8,128)(2,1)S(1)} %get-tuple-element.34.z0_ref, ...), custom_call_target="tpu_custom_call" | custom-call | tf_op jit(solution)/shard_map/unpack_low/pallas_call | solution.py:409
  129.0 6.2 %collective-permute-done.9.g3_ref = bf16[256,128]{1,0:T(8,128)(2,1)S(1)} collective-permute-done((bf16[256,128]{1,0:T(8,128)(2,1)S(1)}, bf16[256,128]{1,0:T(8,128)(2,1)S(1)}, u32[]{:S(2)}, u32[]{:S(2)}) %collective-permute-start.9) | collective-permute-done | bytes 65568 | tf_op jit(solution)/shard_map/ppermute | solution.py:362
  135.2 0.0 collective-permute-done.10.g5_ref
  135.2 0.0 all-to-all-done.3.xy_ref
  135.3 2.0 %unpack_high.1 = (bf16[128,2048]{1,0:T(8,128)(2,1)}, bf16[128,2048]{1,0:T(8,128)(2,1)}, bf16[128,2048]{1,0:T(8,128)(2,1)}, bf16[128,2048]{1,0:T(8,128)(2,1)}, f32[1,16]{1,0:T(1,128)}) custom-call(s32[2]{0:T(128)S(1)} %pad_add_fusion.ids, ...), custom_call_target="tpu_custom_call", output_to_operand_aliasing={{0}: (1, {}), {1}: (2, {}), {2}: (3, {}), {3}: (4, {})} | custom-call | tf_op jit(solution)/shard_map/unpack_high/pallas_call | solution.py:420
Async XLA Ops:
  0.7 16.4 %copy-start = (bf16[1,128,2048]{2,1,0:T(8,128)(2,1)S(1)}, bf16[1,128,2048]{2,1,0:T(8,128)(2,1)}, u32[]{:S(2)}) copy-start(bf16[1,128,2048]{2,1,0:T(8,128)(2,1)} %param.6) | copy-start | bytes 1572868
  0.7 16.4 %copy-start.1 = (bf16[1,128,2048]{2,1,0:T(8,128)(2,1)S(1)}, bf16[1,128,2048]{2,1,0:T(8,128)(2,1)}, u32[]{:S(2)}) copy-start(bf16[1,128,2048]{2,1,0:T(8,128)(2,1)} %param.7) | copy-start | bytes 1572868
  0.7 16.4 %copy-start.2 = (bf16[1,128,2048]{2,1,0:T(8,128)(2,1)S(1)}, bf16[1,128,2048]{2,1,0:T(8,128)(2,1)}, u32[]{:S(2)}) copy-start(bf16[1,128,2048]{2,1,0:T(8,128)(2,1)} %param.8) | copy-start | bytes 1572868
  0.7 16.4 %copy-start.3 = (bf16[1,128,2048]{2,1,0:T(8,128)(2,1)S(1)}, bf16[1,128,2048]{2,1,0:T(8,128)(2,1)}, u32[]{:S(2)}) copy-start(bf16[1,128,2048]{2,1,0:T(8,128)(2,1)} %param.9) | copy-start | bytes 1572868
  18.6 31.6 %all-to-all-start.1 = ((bf16[4,128,128]{2,1,0:T(8,128)(2,1)}), bf16[4,128,128]{2,1,0:T(8,128)(2,1)S(1)}, u32[]{:S(2)}, u32[]{:S(2)}) async-start(bf16[4,128,128]{2,1,0:T(8,128)(2,1)} %shard_map.104), calls=%async_computation.1 | async-start | bytes 262144 | tf_op jit(solution)/shard_map/all_to_all | solution.py:388
  33.4 16.9 %collective-permute-start.2 = (bf16[256,128]{1,0:T(8,128)(2,1)S(1)}, bf16[256,128]{1,0:T(8,128)(2,1)S(1)}, u32[]{:S(2)}, u32[]{:S(2)}) collective-permute-start(bf16[256,128]{1,0:T(8,128)(2,1)S(1)} %get-tuple-element.38), channel_id=1, source_target_pairs={{0,16},{16,0},{32,48},{48,32},{1,17},{17,1},{33,49},{49,33},{2,18}... | collective-permute-start | bytes 196616 | tf_op jit(solution)/shard_map/ppermute | solution.py:362
  41.2 21.0 %collective-permute-start = (bf16[512,128]{1,0:T(8,128)(2,1)S(1)}, bf16[512,128]{1,0:T(8,128)(2,1)S(1)}, u32[]{:S(2)}, u32[]{:S(2)}) collective-permute-start(bf16[512,128]{1,0:T(8,128)(2,1)S(1)} %shard_map.102), channel_id=1, source_target_pairs={{0,4},{4,0},{8,12},{12,8},{1,5},{5,1},{9,13},{13,9},{2,6},{6,2},{1... | collective-permute-start | bytes 393224 | tf_op jit(solution)/shard_map/ppermute | solution.py:362
  51.0 13.1 %collective-permute-start.3 = (bf16[512,128]{1,0:T(8,128)(2,1)S(1)}, bf16[512,128]{1,0:T(8,128)(2,1)S(1)}, u32[]{:S(2)}, u32[]{:S(2)}) collective-permute-start(bf16[512,128]{1,0:T(8,128)(2,1)S(1)} %get-tuple-element.41), channel_id=1, source_target_pairs={{0,4},{4,0},{8,12},{12,8},{1,5},{5,1},{9,13},{13,9},{2,6},{6,2},{1... | collective-permute-start | bytes 393224 | tf_op jit(solution)/shard_map/ppermute | solution.py:362
  52.9 11.2 %collective-permute-start.4 = (bf16[512,128]{1,0:T(8,128)(2,1)S(1)}, bf16[512,128]{1,0:T(8,128)(2,1)S(1)}, u32[]{:S(2)}, u32[]{:S(2)}) collective-permute-start(bf16[512,128]{1,0:T(8,128)(2,1)S(1)} %get-tuple-element.42), channel_id=1, source_target_pairs={{0,8},{4,12},{8,0},{12,4},{1,9},{5,13},{9,1},{13,5},{2,10},{6,14},... | collective-permute-start | bytes 393224 | tf_op jit(solution)/shard_map/ppermute | solution.py:362
  54.9 5.5 %copy-start.4 = (f32[16]{0:T(128)S(1)}, f32[16]{0:T(128)}, u32[]{:S(2)}) copy-start(f32[16]{0:T(128)} %sharp.5) | copy-start | bytes 196
  54.9 5.5 %copy-start.5 = (s32[1,8]{1,0:T(1,128)S(1)}, s32[1,8]{1,0:T(1,128)}, u32[]{:S(2)}) copy-start(s32[1,8]{1,0:T(1,128)} %param.11) | copy-start | bytes 100
  54.9 9.3 %collective-permute-start.5 = (bf16[512,128]{1,0:T(8,128)(2,1)S(1)}, bf16[512,128]{1,0:T(8,128)(2,1)S(1)}, u32[]{:S(2)}, u32[]{:S(2)}) collective-permute-start(bf16[512,128]{1,0:T(8,128)(2,1)S(1)} %get-tuple-element.43), channel_id=1, source_target_pairs={{0,12},{4,8},{8,4},{12,0},{1,13},{5,9},{9,5},{13,1},{2,14},{6,10},... | collective-permute-start | bytes 393224 | tf_op jit(solution)/shard_map/ppermute | solution.py:362
  67.8 10.1 %collective-permute-start.6 = (bf16[528,128]{1,0:T(8,128)(2,1)S(1)}, bf16[528,128]{1,0:T(8,128)(2,1)S(1)}, u32[]{:S(2)}, u32[]{:S(2)}) collective-permute-start(bf16[528,128]{1,0:T(8,128)(2,1)S(1)} %get-tuple-element.46), channel_id=1, source_target_pairs={{0,4},{4,0},{8,12},{12,8},{1,5},{5,1},{9,13},{13,9},{2,6},{6,2},{1... | collective-permute-start | bytes 405512 | tf_op jit(solution)/shard_map/ppermute | solution.py:362
  72.0 7.9 %collective-permute-start.7 = (bf16[528,128]{1,0:T(8,128)(2,1)S(1)}, bf16[528,128]{1,0:T(8,128)(2,1)S(1)}, u32[]{:S(2)}, u32[]{:S(2)}) collective-permute-start(bf16[528,128]{1,0:T(8,128)(2,1)S(1)} %get-tuple-element.47), channel_id=1, source_target_pairs={{0,8},{4,12},{8,0},{12,4},{1,9},{5,13},{9,1},{13,5},{2,10},{6,14},... | collective-permute-start | bytes 405512 | tf_op jit(solution)/shard_map/ppermute | solution.py:362
  74.5 8.1 %collective-permute-start.8 = (bf16[528,128]{1,0:T(8,128)(2,1)S(1)}, bf16[528,128]{1,0:T(8,128)(2,1)S(1)}, u32[]{:S(2)}, u32[]{:S(2)}) collective-permute-start(bf16[528,128]{1,0:T(8,128)(2,1)S(1)} %get-tuple-element.48), channel_id=1, source_target_pairs={{0,12},{4,8},{8,4},{12,0},{1,13},{5,9},{9,5},{13,1},{2,14},{6,10},... | collective-permute-start | bytes 405512 | tf_op jit(solution)/shard_map/ppermute | solution.py:362
  108.1 27.1 %all-to-all-start.3 = ((bf16[32,48,128]{2,1,0:T(8,128)(2,1)}), bf16[32,48,128]{2,1,0:T(8,128)(2,1)S(1)}, u32[]{:S(2)}, u32[]{:S(2)}) async-start(bf16[32,48,128]{2,1,0:T(8,128)(2,1)} %get-tuple-element.57), calls=%async_computation.3 | async-start | bytes 786432 | tf_op jit(solution)/shard_map/all_to_all | solution.py:405
  118.1 9.2 %collective-permute-start.1 = (bf16[512,128]{1,0:T(8,128)(2,1)S(1)}, bf16[512,128]{1,0:T(8,128)(2,1)S(1)}, u32[]{:S(2)}, u32[]{:S(2)}) collective-permute-start(bf16[512,128]{1,0:T(8,128)(2,1)S(1)} %get-tuple-element.37), channel_id=1, source_target_pairs={{0,4},{4,0},{8,12},{12,8},{1,5},{5,1},{9,13},{13,9},{2,6},{6,2},{1... | collective-permute-start | bytes 393224 | tf_op jit(solution)/shard_map/ppermute | solution.py:362
  121.3 14.0 %collective-permute-start.9 = (bf16[256,128]{1,0:T(8,128)(2,1)S(1)}, bf16[256,128]{1,0:T(8,128)(2,1)S(1)}, u32[]{:S(2)}, u32[]{:S(2)}) collective-permute-start(bf16[256,128]{1,0:T(8,128)(2,1)S(1)} %get-tuple-element.54), channel_id=1, source_target_pairs={{0,16},{16,0},{32,48},{48,32},{1,17},{17,1},{33,49},{49,33},{2,18}... | collective-permute-start | bytes 196616 | tf_op jit(solution)/shard_map/ppermute | solution.py:362
  124.0 11.3 %collective-permute-start.10 = (bf16[64,128]{1,0:T(8,128)(2,1)S(1)}, bf16[64,128]{1,0:T(8,128)(2,1)S(1)}, u32[]{:S(2)}, u32[]{:S(2)}) collective-permute-start(bf16[64,128]{1,0:T(8,128)(2,1)S(1)} %get-tuple-element.56), channel_id=1, source_target_pairs={{0,64},{64,0},{128,192},{192,128},{1,65},{65,1},{129,193},{193,129... | collective-permute-start | bytes 49160 | tf_op jit(solution)/shard_map/ppermute | solution.py:362
